TPU v7x, 512 devices: a whole 4x4x16 slice. The times are simulated.
512 devices in a mesh: ctx: 64 (over z_lo, y, core), head: 8 (over z_hi, x).
Axes of the slice: x: 4, y: 4, z: 16 (z_hi: 2, z_lo: 8; z = z_hi * 8 + z_lo), core: 2. Of those that a mesh axis runs over, the one named last changes fastest.
Arguments:
- queries: bfloat16 [8192, 4096], P('ctx', 'head'), may hold values from -8 to 8
- keys: bfloat16 [8192, 1024], P('ctx', 'head'), may hold values from -6 to 6
- values: bfloat16 [8192, 1024], P('ctx', 'head'), may hold values from -6 to 6
- out_weight: bfloat16 [4096, 8192], P('head', 'ctx'), may hold values from -2.390625 to 2.390625
- block_order: int32 [128], replicated, may hold values from 0 to 127, as said below
Outputs:
- projected: bfloat16 [8192, 8192], P('ctx', 'head')
Inputs may be any that keep to these rules, and one draw needn't show every extreme that they name: `block_order`: slot blocks 2 s and 2 s + 1 hold the position blocks p and 127 - p for some p, and each position block is held by exactly one slot block.
All inputs are finite; a program needn't handle non-finite values.
Results may differ from a plain program's by a relative error of at most 0.018.
Values may be sent and summed in bfloat16 or wider, within the bound.
No kernel may reach another device: no remote copies, remote signals or barrier semaphores. Data moves between devices by JAX's collectives and lax.ppermute only.
A program may use at most 128 MiB of HBM per device.

v0:
```python
import math

import jax
import jax.numpy as jnp
from jax import lax
from jax.sharding import PartitionSpec as P


def slot_positions(block_order, offset, number, block_len):
    row_index = offset + jnp.arange(number, dtype=jnp.int32)
    which_block = row_index // block_len
    matches = which_block[:, None] == jnp.arange(block_order.shape[0], dtype=jnp.int32)[None, :]
    block_start = jnp.sum(jnp.where(matches, block_order[None, :], 0), axis=1)
    return block_start * block_len + row_index % block_len


def local(queries, keys, values, out_weight, block_order):
    tok_rows = queries.shape[0]
    head_size = keys.shape[1]
    local_heads = queries.shape[1] // head_size
    block_len = tok_rows // 2
    query_heads = queries.reshape(tok_rows, local_heads, head_size)
    query_pos = slot_positions(block_order, lax.axis_index("ctx") * tok_rows, tok_rows, block_len)
    scaling = 1.0 / math.sqrt(head_size)
    running_max = jnp.full((local_heads, tok_rows), -1e30, jnp.float32)
    key_piece = lax.all_gather(keys, "ctx", axis=0, tiled=True)
    value_piece = lax.all_gather(values, "ctx", axis=0, tiled=True)
    key_pos = slot_positions(block_order, jnp.int32(0), key_piece.shape[0], block_len)
    scores = (
        jnp.einsum("thd,sd->hts", query_heads, key_piece, preferred_element_type=jnp.float32)
        * scaling
    )
    visible = key_pos[None, None, :] <= query_pos[None, :, None]
    scores = jnp.where(visible, scores, -1e30)
    new_max = jnp.maximum(running_max, jnp.max(scores, axis=-1))
    weights_now = jnp.where(visible, jnp.exp(scores - new_max[..., None]), 0.0)
    new_sum = jnp.sum(weights_now, axis=-1)
    weights_b = weights_now.astype(jnp.bfloat16)
    new_accum = jnp.einsum(
        "hts,sd->htd", weights_b, value_piece, preferred_element_type=jnp.float32
    )
    attended = (new_accum / new_sum[..., None]).astype(jnp.bfloat16)
    piece = lax.all_gather(out_weight, "ctx", axis=1, tiled=True)
    weight_heads = piece.reshape(local_heads, head_size, piece.shape[1])
    partial_value = jnp.einsum(
        "htd,hdc->htc", attended, weight_heads, preferred_element_type=jnp.float32
    ).astype(jnp.bfloat16)
    partial_value = lax.optimization_barrier(partial_value)
    term = jnp.sum(partial_value.astype(jnp.float32), axis=0)
    summed = lax.psum_scatter(term.astype(jnp.bfloat16), "head", scatter_dimension=1, tiled=True)
    return summed


def solution(mesh):
    in_specs = (P("ctx", "head"), P("ctx", "head"), P("ctx", "head"), P("head", "ctx"), P())
    out_specs = P("ctx", "head")
    return jax.shard_map(local, mesh=mesh, in_specs=in_specs, out_specs=out_specs, check_vma=False)
```

profile of v0, /device:TPU:1, one launch (start us, length us, event | category | flops | bytes accessed | tf_op | source)
XLA Modules:
  0.0 562.6 jit_solution(5981867400463570871)
XLA Ops:
  6.5 0.0 copy-start
  6.5 0.0 all-gather.4.cloned.1.call-start
  6.5 0.7 all-gather.4.cloned.1.call-update
  7.3 0.0 all-gather.6.cloned.1.call-start
  7.3 0.7 all-gather.6.cloned.1.call-update
  8.0 0.0 all-gather.8.cloned.1.call-start
  8.1 0.7 all-gather.8.cloned.1.call-update
  8.7 0.0 reduce-scatter.2.cloned.1.call-start
  8.8 0.8 select_reduce_fusion.1
  9.7 3.2 select_reduce_fusion
  12.9 3.7 broadcast_compare_fusion
  16.6 119.3 %all-gather.4.cloned.1.call-done = bf16[8192,128]{1,0:T(8,128)(2,1)} async-done(((bf16[128,128]{1,0:T(8,128)(2,1)}), bf16[8192,128]{1,0:T(8,128)(2,1)}) %all-gather.4.cloned.1.call-update) | async-done | bytes 2097168 | tf_op jit(solution)/shard_map/all_gather | solution.py:26
  136.0 0.0 copy-done
  136.0 3.8 fusion
  139.7 0.0 copy-start.1
  139.8 5.7 %copy-done.1 = f32[8192,128,4]{1,0,2:T(8,128)} copy-done((f32[8192,128,4]{1,0,2:T(8,128)}, f32[8192,128,4]{1,0,2:T(8,128)S(1)}, u32[]{:S(2)}) %copy-start.1) | copy-done | bytes 16777240
  145.5 4.2 fusion.1
  149.6 105.0 %all-gather.6.cloned.1.call-done = bf16[8192,128]{1,0:T(8,128)(2,1)} async-done(((bf16[128,128]{1,0:T(8,128)(2,1)}), bf16[8192,128]{1,0:T(8,128)(2,1)}) %all-gather.6.cloned.1.call-update) | async-done | bytes 2097168 | tf_op jit(solution)/shard_map/all_gather | solution.py:27
  254.7 137.2 %all-gather.8.cloned.1.call-done = bf16[512,8192]{1,0:T(8,128)(2,1)} async-done(((bf16[512,128]{1,0:T(8,128)(2,1)}), bf16[512,8192]{1,0:T(8,128)(2,1)}) %all-gather.8.cloned.1.call-update) | async-done | bytes 8388624 | tf_op jit(solution)/shard_map/all_gather | solution.py:43
  391.8 15.4 %convolution_convert_fusion = bf16[4,128,8192]{2,1,0:T(8,128)(2,1)} fusion(bf16[4,128,8192]{2,1,0:T(8,128)(2,1)} %bitcast.42, bf16[8192,128]{1,0:T(8,128)(2,1)} %all-gather.6.cloned.1.call-done, f32[8192,128,4]{1,0,2:T(8,128)} %copy-done.1, f32[4,128]{1,0:T(4,128)S(1)} %broadcast_maximum_fusion, pred[128,8192]{0,1:T(8,128)(4,1)S(1)} %broadcast_compare_fusion, ...), kind=kOutput, calls=%fused_computation.3 | convolution fusion | flops 2172780544 | bytes 36704256 | tf_op jit(solution)/shard_map/htd,hdc->htc/dot_general | solution.py:45
  407.3 6.9 %reduce_sum.42 = bf16[128,8192]{1,0:T(8,128)(2,1)} reduce(bf16[4,128,8192]{2,1,0:T(8,128)(2,1)} %convolution_convert_fusion, bf16[]{:T(256)} %constant.69.clone.1), dimensions={0}, to_apply=%region_4.5 | reduce | flops 3145728 | bytes 10485762 | tf_op jit(solution)/shard_map/reduce_sum | solution.py:49
  414.2 0.0 reduce-scatter.2.cloned.1.call-update
  414.2 141.9 %reduce-scatter.2.cloned.1.call-done = bf16[128,1024]{1,0:T(8,128)(2,1)} async-done(((bf16[128,8192]{1,0:T(8,128)(2,1)}), bf16[128,1024]{1,0:T(8,128)(2,1)}) %reduce-scatter.2.cloned.1.call-update) | async-done | bytes 262160 | tf_op jit(solution)/shard_map/reduce_scatter | solution.py:50
  (5 shorter events, 0.0 us)
Async XLA Ops:
  6.5 129.4 %copy-start = (bf16[128,512]{1,0:T(8,128)(2,1)S(1)}, bf16[128,512]{1,0:T(8,128)(2,1)}, u32[]{:S(2)}) copy-start(bf16[128,512]{1,0:T(8,128)(2,1)} %param.5) | copy-start | bytes 393220
  6.5 129.4 %all-gather.4.cloned.1.call-start = ((), (), s32[]{:S(2)}) async-start(), calls=%async_computation.1 | async-start | bytes 2129920 | tf_op jit(solution)/shard_map/all_gather | solution.py:26
  7.3 247.4 %all-gather.6.cloned.1.call-start = ((), (), s32[]{:S(2)}) async-start(), calls=%async_computation.2 | async-start | bytes 2129920 | tf_op jit(solution)/shard_map/all_gather | solution.py:27
  8.0 383.8 %all-gather.8.cloned.1.call-start = ((), (), s32[]{:S(2)}) async-start(), calls=%async_computation.3 | async-start | bytes 8519680 | tf_op jit(solution)/shard_map/all_gather | solution.py:43
  8.7 547.3 %reduce-scatter.2.cloned.1.call-start = ((), (), s32[]{:S(2)}) async-start(), calls=%async_computation.4 | async-start | bytes 2359296 | tf_op jit(solution)/shard_map/reduce_scatter | solution.py:50
  139.7 5.7 %copy-start.1 = (f32[8192,128,4]{1,0,2:T(8,128)}, f32[8192,128,4]{1,0,2:T(8,128)S(1)}, u32[]{:S(2)}) copy-start(f32[8192,128,4]{1,0,2:T(8,128)S(1)} %get-tuple-element.6) | copy-start | bytes 50331652
Sparse Core Ops, SparseCore 0:
  9.5 126.4 all-gather.3
  138.1 116.4 all-gather.5
  256.7 135.0 all-gather.7
  414.3 141.7 reduce-scatter.1
where the time goes:
time: 563 us
  waiting for transfers between devices  506 us (90%)
  matrix products  19.2 us (3%)
  other arithmetic  18.8 us (3%)
  between operations  13.2 us (2%)
  local copies, waits for them, and re-layouts  5.7 us (1%)
    reduce_scatter x1, waiting for transfers between devices, local(): lax.psum_scatter(term.astype(jnp.bfloat16), 'head', scatter_dimension=1,...  142 us
    all_gather x1, waiting for transfers between devices, local(): piece = lax.all_gather(out_weight, 'ctx', axis=1, tiled=True)  137 us
    all_gather x1, waiting for transfers between devices, local(): key_piece = lax.all_gather(keys, 'ctx', axis=0, tiled=True)  119 us
    all_gather x1, waiting for transfers between devices, local(): value_piece = lax.all_gather(values, 'ctx', axis=0, tiled=True)  105 us
    dot_general x1, matrix products, local(): jnp.einsum('htd,hdc->htc', attended, weight_heads, preferred_element_type...  15.4 us
  transfers between devices with their start and end apart: 4, of which 4 were waited for; matrix products, arithmetic and copies ran while one was open for 3% of the time, Pallas kernels for 0%

commit v1 on v0

v1 whole, which is shorter than its diff:
```python
import math

import jax
import jax.numpy as jnp
from jax import lax
from jax.experimental import pallas as pl
from jax.experimental.pallas import tpu as pltpu
from jax.sharding import Mesh
from jax.sharding import PartitionSpec as P

AXES = ("za", "zb", "y", "c", "h", "x")
SIZES = (2, 4, 4, 2, 2, 4)
CTX = ("za", "zb", "y", "c")
HEAD = ("h", "x")
DH = 128
TOK = 128
HEADS = 4
FEAT = HEADS * DH
STATS = 16
NEG = -1e30
F32 = jnp.float32
BF16 = jnp.bfloat16


def swap(value, axis, size, bit):
    return lax.ppermute(value, axis, [(i, i ^ bit) for i in range(size)])


def attend_kernel(where, order, q_ref, near_ref, far_ref, out_ref, score, prob, v_t, stat):
    za, zb, y, c = where[0], where[1], where[2], where[3]
    scale = math.log2(math.e) / math.sqrt(DH)
    lane = lax.broadcasted_iota(jnp.int32, (1, TOK), 1)
    half = lane // 64

    def slot(ctx, index, which):
        return jnp.where(which == 0, order[2 * ctx], order[2 * ctx + 1]) * 64 + index % 64

    base = (za * 4 + zb) * 4
    q_pos = jnp.concatenate([slot((base + j) * 2 + c, lane, half) for j in range(4)], axis=1)
    row = lax.broadcasted_iota(jnp.int32, (TOK, 1), 0)
    k_pos = []
    for side, ref in enumerate((near_ref, far_ref)):
        for p in range(8):
            a = za ^ (p & 1)
            b = zb ^ ((p >> 1) & 1) * 2 ^ ((p >> 2) & 1)
            ctx = ((a * 4 + b) * 4 + y) * 2 + (c ^ side)
            k_pos.append(slot(ctx, row, row // 64))
            v_t[:, (side * 8 + p) * TOK : (side * 8 + p + 1) * TOK] = ref[p, TOK:, :].T
    stat[...] = jnp.zeros_like(stat)
    for h in range(HEADS):
        q = jnp.concatenate([q_ref[j, :, h * DH : (h + 1) * DH] for j in range(4)], axis=0)
        top = jnp.full((1, 4 * TOK), NEG, F32)
        for p in range(16):
            k = (near_ref if p < 8 else far_ref)[p % 8, :TOK, :]
            s = lax.dot_general(k, q, (((1,), (1,)), ((), ())), preferred_element_type=F32)
            s = jnp.where(k_pos[p] <= q_pos, s * scale, NEG)
            score[p * TOK : (p + 1) * TOK, :] = s
            top = jnp.maximum(top, jnp.max(s, axis=0, keepdims=True))
        total = jnp.zeros((1, 4 * TOK), F32)
        for p in range(16):
            e = jnp.exp2(score[p * TOK : (p + 1) * TOK, :] - top)
            total = total + jnp.sum(e, axis=0, keepdims=True)
            prob[p * TOK : (p + 1) * TOK, :] = e.astype(BF16)
        o = jnp.dot(v_t[...], prob[...], preferred_element_type=F32) / total
        for j in range(4):
            out_ref[j, h * DH : (h + 1) * DH, :] = o[:, j * TOK : (j + 1) * TOK].astype(BF16)
        rest = top + jnp.log2(total)
        for i in range(3):
            part = rest.astype(BF16).astype(F32)
            stat[3 * h + i : 3 * h + i + 1, :] = part
            rest = rest - part
    for j in range(4):
        out_ref[j, FEAT:, :] = stat[:, j * TOK : (j + 1) * TOK].astype(BF16)


def merge_kernel(in_ref, out_ref):
    stats = [in_ref[j, FEAT:, :].astype(F32) for j in range(4)]
    for h in range(HEADS):
        logs = [s[3 * h : 3 * h + 1] + s[3 * h + 1 : 3 * h + 2] + s[3 * h + 2 : 3 * h + 3] for s in stats]
        top = jnp.maximum(jnp.maximum(logs[0], logs[1]), jnp.maximum(logs[2], logs[3]))
        parts = [jnp.exp2(s - top) for s in logs]
        total = parts[0] + parts[1] + parts[2] + parts[3]
        o = jnp.zeros((DH, TOK), F32)
        for j in range(4):
            o = o + in_ref[j, h * DH : (h + 1) * DH, :].astype(F32) * (parts[j] / total)
        out_ref[:, h * DH : (h + 1) * DH] = o.T.astype(BF16)


def project_kernel(where, a_ref, near_ref, far_ref, out_ref):
    za, zb, c, h = where[0], where[1], where[3], where[4]
    for r in range(4):
        dest = zb ^ (r & 1) * 2 ^ ((r >> 1) & 1)
        w = []
        for g in range(2):
            near, far = near_ref[2 * r + g], far_ref[2 * r + g]
            left = jnp.where(c == 0, near, far)
            right = jnp.where(c == 0, far, near)
            w.append(jnp.concatenate([left, right], axis=1))
        for j in range(4):
            acc = jnp.zeros((TOK, 2 * TOK), F32)
            for g in range(2):
                a = a_ref[j, za ^ g ^ h]
                acc = acc + jnp.dot(a, w[g], preferred_element_type=F32)
            out_ref[dest * 4 + j] = acc.astype(BF16)


def add_kernel(in_ref, out_ref):
    for j in range(4):
        total = in_ref[j].astype(F32)
        for i in range(1, 4):
            total = total + in_ref[i * 4 + j].astype(F32)
        out_ref[:, j * 256 : (j + 1) * 256] = total.astype(BF16)


SM = pl.BlockSpec(memory_space=pltpu.SMEM)
VM = pl.BlockSpec(memory_space=pltpu.VMEM)
PARAMS = pltpu.CompilerParams(vmem_limit_bytes=40 << 20)


def local(queries, keys, values, out_weight, block_order):
    where = jnp.stack([lax.axis_index(a).astype(jnp.int32) for a in AXES])
    kv = jnp.concatenate([keys, values], axis=0)[None]
    z4 = swap(kv, "za", 2, 1)
    q_all = lax.all_to_all(jnp.broadcast_to(queries[None], (4,) + queries.shape), "y", 0, 0, tiled=True)
    kv = jnp.concatenate([kv, z4], axis=0)
    kv = jnp.concatenate([kv, swap(kv, "zb", 4, 2)], axis=0)
    kv = jnp.concatenate([kv, swap(kv, "zb", 4, 1)], axis=0)
    kv, w = lax.optimization_barrier((kv, out_weight))
    kv_far = swap(kv, "c", 2, 1)

    w = lax.ppermute(w, ("za", "h"), [(0, 0), (1, 2), (2, 1), (3, 3)])[None]
    w = jnp.concatenate([w, swap(w, "za", 2, 1)], axis=0)
    w = jnp.concatenate([w, swap(w, "zb", 4, 2)], axis=0)
    w = jnp.concatenate([w, swap(w, "zb", 4, 1)], axis=0)
    w_far = swap(w, "c", 2, 1)

    part = pl.pallas_call(
        attend_kernel,
        out_shape=jax.ShapeDtypeStruct((4, FEAT + STATS, TOK), BF16),
        in_specs=[SM, SM, VM, VM, VM],
        out_specs=VM,
        scratch_shapes=[
            pltpu.VMEM((16 * TOK, 4 * TOK), F32),
            pltpu.VMEM((16 * TOK, 4 * TOK), BF16),
            pltpu.VMEM((DH, 16 * TOK), BF16),
            pltpu.VMEM((STATS, 4 * TOK), F32),
        ],
        compiler_params=PARAMS,
        name="attend",
    )(where, block_order, q_all, kv, kv_far)
    part = lax.all_to_all(part, "y", 0, 0, tiled=True)
    attended = pl.pallas_call(
        merge_kernel,
        out_shape=jax.ShapeDtypeStruct((TOK, FEAT), BF16),
        in_specs=[VM],
        out_specs=VM,
        compiler_params=PARAMS,
        name="merge",
    )(part)
    other = swap(attended, "h", 2, 1)
    pair = jnp.stack([attended, other])
    a_all = lax.all_to_all(jnp.broadcast_to(pair[None], (4,) + pair.shape), "y", 0, 0, tiled=True)
    tiles = pl.pallas_call(
        project_kernel,
        out_shape=jax.ShapeDtypeStruct((16, TOK, 256), BF16),
        in_specs=[SM, VM, VM, VM],
        out_specs=VM,
        compiler_params=PARAMS,
        name="project",
    )(where, a_all, w, w_far)
    tiles = lax.all_to_all(tiles, ("x", "y"), 0, 0, tiled=True)
    return pl.pallas_call(
        add_kernel,
        out_shape=jax.ShapeDtypeStruct((TOK, 1024), BF16),
        in_specs=[VM],
        out_specs=VM,
        compiler_params=PARAMS,
        name="add",
    )(tiles)


def solution(mesh):
    fine = Mesh(mesh.devices.reshape(SIZES), AXES)
    in_specs = (P(CTX, HEAD), P(CTX, HEAD), P(CTX, HEAD), P(HEAD, CTX), P())
    return jax.shard_map(local, mesh=fine, in_specs=in_specs, out_specs=P(CTX, HEAD), check_vma=False)
```

time: 563 us -> 178 us (0.32)
  the two profiles are of different devices: /device:TPU:1 before, /device:TPU:64 now
where the time goes in v1:
time: 178 us; the launch traced here: 177 us
  starting transfers between devices  74.6 us (42%)
  waiting for transfers between devices  49.2 us (28%)
  blocking collectives  39.2 us (22%)
  Pallas kernels  11.7 us (7%)
    ppermute x9, starting transfers between devices, swap(): return lax.ppermute(value, axis, [(i, i ^ bit) for i in range(size)])  66 us
    ppermute x9, waiting for transfers between devices, swap(): return lax.ppermute(value, axis, [(i, i ^ bit) for i in range(size)])  36.4 us
    all_to_all x1, blocking collectives, local(): tiles = lax.all_to_all(tiles, ('x', 'y'), 0, 0, tiled=True)  21.3 us
    all_to_all x1, blocking collectives, local(): lax.all_to_all(jnp.broadcast_to(pair[None], (4,) + pair.shape), 'y', 0, 0...  18 us
    pallas_call x1, Pallas kernels, local(): pl.pallas_call(attend_kernel, out_shape=jax.ShapeDtypeStruct((4, FEAT + S...  8.84 us
    all_to_all x1, waiting for transfers between devices, local(): part = lax.all_to_all(part, 'y', 0, 0, tiled=True)  7.39 us
    all_to_all x1, waiting for transfers between devices, local(): lax.all_to_all(jnp.broadcast_to(queries[None], (4,) + queries.shape), 'y'...  5.41 us
    all_to_all x1, starting transfers between devices, local(): lax.all_to_all(jnp.broadcast_to(queries[None], (4,) + queries.shape), 'y'...  4.46 us
  transfers between devices with their start and end apart: 12, of which 8 were waited for; matrix products, arithmetic and copies ran while one was open for 1% of the time, Pallas kernels for 5%

profile of v1, /device:TPU:64, one launch (start us, length us, event | category | flops | bytes accessed | tf_op | source)
XLA Modules:
  0.0 177.0 jit_solution(232993779400587683)
XLA Ops:
  0.0 0.8 maximum_bitcast_fusion
  0.8 9.1 %collective-permute-start = (bf16[1,256,128]{2,1,0:T(8,128)(2,1)S(1)}, bf16[1,256,128]{2,1,0:T(8,128)(2,1)S(1)}, u32[]{:S(2)}, u32[]{:S(2)}) collective-permute-start(bf16[1,256,128]{2,1,0:T(8,128)(2,1)S(1)} %maximum_bitcast_fusion), channel_id=1, source_target_pairs={{0,256},{256,0},{1,257},{257,1},{2,258},{258,2},{3,259},{259,3},{4... | collective-permute-start | bytes 196616 | tf_op jit(solution)/shard_map/ppermute | solution.py:26
  9.9 3.7 %collective-permute-done = bf16[1,256,128]{2,1,0:T(8,128)(2,1)S(1)} collective-permute-done((bf16[1,256,128]{2,1,0:T(8,128)(2,1)S(1)}, bf16[1,256,128]{2,1,0:T(8,128)(2,1)S(1)}, u32[]{:S(2)}, u32[]{:S(2)}) %collective-permute-start) | collective-permute-done | bytes 65568 | tf_op jit(solution)/shard_map/ppermute | solution.py:26
  13.6 4.9 %collective-permute-start.1 = (bf16[2,256,128]{2,1,0:T(8,128)(2,1)S(1)}, bf16[2,256,128]{2,1,0:T(8,128)(2,1)S(1)}, u32[]{:S(2)}, u32[]{:S(2)}) collective-permute-start(bf16[2,256,128]{2,1,0:T(8,128)(2,1)S(1)} %pad_maximum_fusion.6), channel_id=1, source_target_pairs={{0,128},{64,192},{128,0},{192,64},{1,129},{65,193},{129,1},{193,65... | collective-permute-start | bytes 393224 | tf_op jit(solution)/shard_map/ppermute | solution.py:26
  18.6 3.3 %collective-permute-done.1 = bf16[2,256,128]{2,1,0:T(8,128)(2,1)S(1)} collective-permute-done((bf16[2,256,128]{2,1,0:T(8,128)(2,1)S(1)}, bf16[2,256,128]{2,1,0:T(8,128)(2,1)S(1)}, u32[]{:S(2)}, u32[]{:S(2)}) %collective-permute-start.1) | collective-permute-done | bytes 131104 | tf_op jit(solution)/shard_map/ppermute | solution.py:26
  21.8 0.0 copy-start.2
  21.9 5.9 %collective-permute-start.2 = (bf16[4,256,128]{2,1,0:T(8,128)(2,1)S(1)}, bf16[4,256,128]{2,1,0:T(8,128)(2,1)S(1)}, u32[]{:S(2)}, u32[]{:S(2)}) collective-permute-start(bf16[4,256,128]{2,1,0:T(8,128)(2,1)S(1)} %pad_maximum_fusion.3), channel_id=1, source_target_pairs={{0,64},{64,0},{128,192},{192,128},{1,65},{65,1},{129,193},{193,129... | collective-permute-start | bytes 786440 | tf_op jit(solution)/shard_map/ppermute | solution.py:26
  27.7 6.5 %collective-permute-done.2 = bf16[4,256,128]{2,1,0:T(8,128)(2,1)S(1)} collective-permute-done((bf16[4,256,128]{2,1,0:T(8,128)(2,1)S(1)}, bf16[4,256,128]{2,1,0:T(8,128)(2,1)S(1)}, u32[]{:S(2)}, u32[]{:S(2)}) %collective-permute-start.2) | collective-permute-done | bytes 262176 | tf_op jit(solution)/shard_map/ppermute | solution.py:26
  34.2 0.1 pad_maximum_fusion.1.near_ref
  34.3 0.0 copy-done.2
  34.3 0.7 collective-permute-start.5
  34.9 0.0 collective-permute-done.5
  34.9 0.0 copy-start.1
  35.0 22.4 %collective-permute-start.6 = (bf16[1,512,128]{2,1,0:T(8,128)(2,1)S(1)}, bf16[1,512,128]{2,1,0:T(8,128)(2,1)S(1)}, u32[]{:S(2)}, u32[]{:S(2)}) collective-permute-start(bf16[1,512,128]{2,1,0:T(8,128)(2,1)S(1)} %bitcast.12), channel_id=1, source_target_pairs={{0,256},{256,0},{1,257},{257,1},{2,258},{258,2},{3,259},{259,3},{4... | collective-permute-start | bytes 393224 | tf_op jit(solution)/shard_map/ppermute | solution.py:26
  57.3 7.4 %collective-permute-done.6 = bf16[1,512,128]{2,1,0:T(8,128)(2,1)S(1)} collective-permute-done((bf16[1,512,128]{2,1,0:T(8,128)(2,1)S(1)}, bf16[1,512,128]{2,1,0:T(8,128)(2,1)S(1)}, u32[]{:S(2)}, u32[]{:S(2)}) %collective-permute-start.6) | collective-permute-done | bytes 131104 | tf_op jit(solution)/shard_map/ppermute | solution.py:26
  64.8 9.7 %collective-permute-start.7 = (bf16[2,512,128]{2,1,0:T(8,128)(2,1)S(1)}, bf16[2,512,128]{2,1,0:T(8,128)(2,1)S(1)}, u32[]{:S(2)}, u32[]{:S(2)}) collective-permute-start(bf16[2,512,128]{2,1,0:T(8,128)(2,1)S(1)} %pad_maximum_fusion.5), channel_id=1, source_target_pairs={{0,128},{64,192},{128,0},{192,64},{1,129},{65,193},{129,1},{193,65... | collective-permute-start | bytes 786440 | tf_op jit(solution)/shard_map/ppermute | solution.py:26
  74.5 1.9 %collective-permute-start.3 = (bf16[8,256,128]{2,1,0:T(8,128)(2,1)S(1)}, bf16[8,256,128]{2,1,0:T(8,128)(2,1)S(1)}, u32[]{:S(2)}, u32[]{:S(2)}) collective-permute-start(bf16[8,256,128]{2,1,0:T(8,128)(2,1)S(1)} %pad_maximum_fusion.1.near_ref), channel_id=1, source_target_pairs={{0,8},{8,0},{1,9},{9,1},{2,10},{10,2},{3,11},{11,3},{4,12},{12,4},... | collective-permute-start | bytes 1572872 | tf_op jit(solution)/shard_map/ppermute | solution.py:26
  76.4 0.0 copy-done.1
  76.4 0.8 broadcast_in_dim.8
  77.2 4.5 %all-to-all-start = ((bf16[4,128,512]{2,1,0:T(8,128)(2,1)}), bf16[4,128,512]{2,1,0:T(8,128)(2,1)S(1)}, u32[]{:S(2)}, u32[]{:S(2)}) async-start(bf16[4,128,512]{2,1,0:T(8,128)(2,1)} %broadcast_in_dim.8), calls=%async_computation | async-start | bytes 1048576 | tf_op jit(solution)/shard_map/all_to_all | solution.py:124
  81.7 1.3 collective-permute-done.7
  83.0 0.1 pad_maximum_fusion.2
  83.1 3.2 %collective-permute-start.8 = (bf16[4,512,128]{2,1,0:T(8,128)(2,1)S(1)}, bf16[4,512,128]{2,1,0:T(8,128)(2,1)S(1)}, u32[]{:S(2)}, u32[]{:S(2)}) collective-permute-start(bf16[4,512,128]{2,1,0:T(8,128)(2,1)S(1)} %pad_maximum_fusion.2), channel_id=1, source_target_pairs={{0,64},{64,0},{128,192},{192,128},{1,65},{65,1},{129,193},{193,129... | collective-permute-start | bytes 1572872 | tf_op jit(solution)/shard_map/ppermute | solution.py:26
  86.3 0.0 copy-start
  86.3 0.1 stack.36.where
  86.4 5.4 %all-to-all-done.q_ref = bf16[4,128,512]{2,1,0:T(8,128)(2,1)S(1)} async-done(((bf16[4,128,512]{2,1,0:T(8,128)(2,1)}), bf16[4,128,512]{2,1,0:T(8,128)(2,1)S(1)}, u32[]{:S(2)}, u32[]{:S(2)}) %all-to-all-start) | async-done | bytes 524320 | tf_op jit(solution)/shard_map/all_to_all | solution.py:124
  91.8 0.0 collective-permute-done.3.far_ref
  91.8 0.0 copy-done
  91.8 8.8 %attend.1 = bf16[4,528,128]{2,1,0:T(8,128)(2,1)} custom-call(s32[6]{0:T(128)S(1)} %stack.36.where, s32[128]{0:T(128)S(1)} %copy-done, bf16[4,128,512]{2,1,0:T(8,128)(2,1)S(1)} %all-to-all-done.q_ref, bf16[8,256,128]{2,1,0:T(8,128)(2,1)S(1)} %pad_maximum_fusion.1.near_ref, bf16[8,256,128]{2,1,0:T(8,128)(2,1)S(1)} %collective-permute-done.3.far_ref), custom_call_target="tpu_custom_call" | custom-call | tf_op jit(solution)/shard_map/attend/pallas_call | solution.py:137
  100.7 3.5 %all-to-all-start.1 = ((bf16[4,528,128]{2,1,0:T(8,128)(2,1)}), bf16[4,528,128]{2,1,0:T(8,128)(2,1)S(1)}, u32[]{:S(2)}, u32[]{:S(2)}) async-start(bf16[4,528,128]{2,1,0:T(8,128)(2,1)} %attend.1), calls=%async_computation.1 | async-start | bytes 1081344 | tf_op jit(solution)/shard_map/all_to_all | solution.py:151
  104.2 0.0 collective-permute-done.8
  104.2 0.1 pad_maximum_fusion.near_ref
  104.3 1.9 %collective-permute-start.9 = (bf16[8,512,128]{2,1,0:T(8,128)(2,1)S(1)}, bf16[8,512,128]{2,1,0:T(8,128)(2,1)S(1)}, u32[]{:S(2)}, u32[]{:S(2)}) collective-permute-start(bf16[8,512,128]{2,1,0:T(8,128)(2,1)S(1)} %pad_maximum_fusion.near_ref), channel_id=1, source_target_pairs={{0,8},{8,0},{1,9},{9,1},{2,10},{10,2},{3,11},{11,3},{4,12},{12,4},... | collective-permute-start | bytes 3145736 | tf_op jit(solution)/shard_map/ppermute | solution.py:26
  106.2 7.4 %all-to-all-done.1.in_ref = bf16[4,528,128]{2,1,0:T(8,128)(2,1)S(1)} async-done(((bf16[4,528,128]{2,1,0:T(8,128)(2,1)}), bf16[4,528,128]{2,1,0:T(8,128)(2,1)S(1)}, u32[]{:S(2)}, u32[]{:S(2)}) %all-to-all-start.1) | async-done | bytes 540704 | tf_op jit(solution)/shard_map/all_to_all | solution.py:151
  113.6 0.2 merge.1
  113.8 6.9 %collective-permute-start.4 = (bf16[128,512]{1,0:T(8,128)(2,1)S(1)}, bf16[128,512]{1,0:T(8,128)(2,1)S(1)}, u32[]{:S(2)}, u32[]{:S(2)}) collective-permute-start(bf16[128,512]{1,0:T(8,128)(2,1)S(1)} %merge.1), channel_id=1, source_target_pairs={{0,4},{4,0},{1,5},{5,1},{2,6},{6,2},{3,7},{7,3},{8,12},{12,8},{9,1... | collective-permute-start | bytes 393224 | tf_op jit(solution)/shard_map/ppermute | solution.py:26
  120.7 14.2 %collective-permute-done.4 = bf16[128,512]{1,0:T(8,128)(2,1)S(1)} collective-permute-done((bf16[128,512]{1,0:T(8,128)(2,1)S(1)}, bf16[128,512]{1,0:T(8,128)(2,1)S(1)}, u32[]{:S(2)}, u32[]{:S(2)}) %collective-permute-start.4) | collective-permute-done | bytes 131104 | tf_op jit(solution)/shard_map/ppermute | solution.py:26
  135.0 0.1 broadcast_in_dim.20
  135.1 18.0 %all_to_all.20.a_ref = bf16[4,2,128,512]{3,2,1,0:T(8,128)(2,1)S(1)} all-to-all(bf16[4,2,128,512]{3,2,1,0:T(8,128)(2,1)S(1)} %broadcast_in_dim.20), channel_id=1, replica_groups=mesh['za'=2,'zb'=4,'y'=4,'c'=2,'h'=2,'x'=4] {'y'}, dimensions={0} | all-to-all | bytes 2097152 | tf_op jit(solution)/shard_map/all_to_all | solution.py:162
  153.1 0.0 collective-permute-done.9.far_ref
  153.1 1.9 %project.1 = bf16[16,128,256]{2,1,0:T(8,128)(2,1)S(1)} custom-call(s32[6]{0:T(128)S(1)} %stack.36.where, bf16[4,2,128,512]{3,2,1,0:T(8,128)(2,1)S(1)} %all_to_all.20.a_ref, bf16[8,512,128]{2,1,0:T(8,128)(2,1)S(1)} %pad_maximum_fusion.near_ref, bf16[8,512,128]{2,1,0:T(8,128)(2,1)S(1)} %collective-permute-done.9.far_ref), custom_call_target="tpu_custom_call" | custom-call | tf_op jit(solution)/shard_map/project/pallas_call | solution.py:163
  154.9 21.3 %all_to_all.21.in_ref = bf16[16,128,256]{2,1,0:T(8,128)(2,1)S(1)} all-to-all(bf16[16,128,256]{2,1,0:T(8,128)(2,1)S(1)} %project.1), channel_id=1, replica_groups=mesh['za'=2,'zb'=4,'y'=4,'c'=2,'h'=2,'x'=4] {'x','y'}, dimensions={0} | all-to-all | bytes 2097152 | tf_op jit(solution)/shard_map/all_to_all | solution.py:171
  176.2 0.8 add.1
  (4 shorter events, 0.1 us)
Async XLA Ops:
  0.8 12.8 %collective-permute-start = (bf16[1,256,128]{2,1,0:T(8,128)(2,1)S(1)}, bf16[1,256,128]{2,1,0:T(8,128)(2,1)S(1)}, u32[]{:S(2)}, u32[]{:S(2)}) collective-permute-start(bf16[1,256,128]{2,1,0:T(8,128)(2,1)S(1)} %maximum_bitcast_fusion), channel_id=1, source_target_pairs={{0,256},{256,0},{1,257},{257,1},{2,258},{258,2},{3,259},{259,3},{4... | collective-permute-start | bytes 196616 | tf_op jit(solution)/shard_map/ppermute | solution.py:26
  13.6 8.2 %collective-permute-start.1 = (bf16[2,256,128]{2,1,0:T(8,128)(2,1)S(1)}, bf16[2,256,128]{2,1,0:T(8,128)(2,1)S(1)}, u32[]{:S(2)}, u32[]{:S(2)}) collective-permute-start(bf16[2,256,128]{2,1,0:T(8,128)(2,1)S(1)} %pad_maximum_fusion.6), channel_id=1, source_target_pairs={{0,128},{64,192},{128,0},{192,64},{1,129},{65,193},{129,1},{193,65... | collective-permute-start | bytes 393224 | tf_op jit(solution)/shard_map/ppermute | solution.py:26
  21.8 12.4 %copy-start.2 = (bf16[512,128]{1,0:T(8,128)(2,1)S(1)}, bf16[512,128]{1,0:T(8,128)(2,1)}, u32[]{:S(2)}) copy-start(bf16[512,128]{1,0:T(8,128)(2,1)} %param.8) | copy-start | bytes 393220
  21.9 12.3 %collective-permute-start.2 = (bf16[4,256,128]{2,1,0:T(8,128)(2,1)S(1)}, bf16[4,256,128]{2,1,0:T(8,128)(2,1)S(1)}, u32[]{:S(2)}, u32[]{:S(2)}) collective-permute-start(bf16[4,256,128]{2,1,0:T(8,128)(2,1)S(1)} %pad_maximum_fusion.3), channel_id=1, source_target_pairs={{0,64},{64,0},{128,192},{192,128},{1,65},{65,1},{129,193},{193,129... | collective-permute-start | bytes 786440 | tf_op jit(solution)/shard_map/ppermute | solution.py:26
  34.3 0.7 collective-permute-start.5
  34.9 41.4 %copy-start.1 = (bf16[128,512]{1,0:T(8,128)(2,1)S(1)}, bf16[128,512]{1,0:T(8,128)(2,1)}, u32[]{:S(2)}) copy-start(bf16[128,512]{1,0:T(8,128)(2,1)} %param.5) | copy-start | bytes 393220
  35.0 29.8 %collective-permute-start.6 = (bf16[1,512,128]{2,1,0:T(8,128)(2,1)S(1)}, bf16[1,512,128]{2,1,0:T(8,128)(2,1)S(1)}, u32[]{:S(2)}, u32[]{:S(2)}) collective-permute-start(bf16[1,512,128]{2,1,0:T(8,128)(2,1)S(1)} %bitcast.12), channel_id=1, source_target_pairs={{0,256},{256,0},{1,257},{257,1},{2,258},{258,2},{3,259},{259,3},{4... | collective-permute-start | bytes 393224 | tf_op jit(solution)/shard_map/ppermute | solution.py:26
  64.8 18.3 %collective-permute-start.7 = (bf16[2,512,128]{2,1,0:T(8,128)(2,1)S(1)}, bf16[2,512,128]{2,1,0:T(8,128)(2,1)S(1)}, u32[]{:S(2)}, u32[]{:S(2)}) collective-permute-start(bf16[2,512,128]{2,1,0:T(8,128)(2,1)S(1)} %pad_maximum_fusion.5), channel_id=1, source_target_pairs={{0,128},{64,192},{128,0},{192,64},{1,129},{65,193},{129,1},{193,65... | collective-permute-start | bytes 786440 | tf_op jit(solution)/shard_map/ppermute | solution.py:26
  74.5 17.4 %collective-permute-start.3 = (bf16[8,256,128]{2,1,0:T(8,128)(2,1)S(1)}, bf16[8,256,128]{2,1,0:T(8,128)(2,1)S(1)}, u32[]{:S(2)}, u32[]{:S(2)}) collective-permute-start(bf16[8,256,128]{2,1,0:T(8,128)(2,1)S(1)} %pad_maximum_fusion.1.near_ref), channel_id=1, source_target_pairs={{0,8},{8,0},{1,9},{9,1},{2,10},{10,2},{3,11},{11,3},{4,12},{12,4},... | collective-permute-start | bytes 1572872 | tf_op jit(solution)/shard_map/ppermute | solution.py:26
  77.2 14.6 %all-to-all-start = ((bf16[4,128,512]{2,1,0:T(8,128)(2,1)}), bf16[4,128,512]{2,1,0:T(8,128)(2,1)S(1)}, u32[]{:S(2)}, u32[]{:S(2)}) async-start(bf16[4,128,512]{2,1,0:T(8,128)(2,1)} %broadcast_in_dim.8), calls=%async_computation | async-start | bytes 1048576 | tf_op jit(solution)/shard_map/all_to_all | solution.py:124
  83.1 21.1 %collective-permute-start.8 = (bf16[4,512,128]{2,1,0:T(8,128)(2,1)S(1)}, bf16[4,512,128]{2,1,0:T(8,128)(2,1)S(1)}, u32[]{:S(2)}, u32[]{:S(2)}) collective-permute-start(bf16[4,512,128]{2,1,0:T(8,128)(2,1)S(1)} %pad_maximum_fusion.2), channel_id=1, source_target_pairs={{0,64},{64,0},{128,192},{192,128},{1,65},{65,1},{129,193},{193,129... | collective-permute-start | bytes 1572872 | tf_op jit(solution)/shard_map/ppermute | solution.py:26
  86.3 5.5 %copy-start = (s32[128]{0:T(128)S(1)}, s32[128]{0:T(128)}, u32[]{:S(2)}) copy-start(s32[128]{0:T(128)} %order.1) | copy-start | bytes 1540
  100.7 12.9 %all-to-all-start.1 = ((bf16[4,528,128]{2,1,0:T(8,128)(2,1)}), bf16[4,528,128]{2,1,0:T(8,128)(2,1)S(1)}, u32[]{:S(2)}, u32[]{:S(2)}) async-start(bf16[4,528,128]{2,1,0:T(8,128)(2,1)} %attend.1), calls=%async_computation.1 | async-start | bytes 1081344 | tf_op jit(solution)/shard_map/all_to_all | solution.py:151
  104.3 48.8 %collective-permute-start.9 = (bf16[8,512,128]{2,1,0:T(8,128)(2,1)S(1)}, bf16[8,512,128]{2,1,0:T(8,128)(2,1)S(1)}, u32[]{:S(2)}, u32[]{:S(2)}) collective-permute-start(bf16[8,512,128]{2,1,0:T(8,128)(2,1)S(1)} %pad_maximum_fusion.near_ref), channel_id=1, source_target_pairs={{0,8},{8,0},{1,9},{9,1},{2,10},{10,2},{3,11},{11,3},{4,12},{12,4},... | collective-permute-start | bytes 3145736 | tf_op jit(solution)/shard_map/ppermute | solution.py:26
  113.8 21.2 %collective-permute-start.4 = (bf16[128,512]{1,0:T(8,128)(2,1)S(1)}, bf16[128,512]{1,0:T(8,128)(2,1)S(1)}, u32[]{:S(2)}, u32[]{:S(2)}) collective-permute-start(bf16[128,512]{1,0:T(8,128)(2,1)S(1)} %merge.1), channel_id=1, source_target_pairs={{0,4},{4,0},{1,5},{5,1},{2,6},{6,2},{3,7},{7,3},{8,12},{12,8},{9,1... | collective-permute-start | bytes 393224 | tf_op jit(solution)/shard_map/ppermute | solution.py:26

commit v2 on v1

v2 whole, which is shorter than its diff:
```python
import functools
import math

import jax
import jax.numpy as jnp
from jax import lax
from jax.experimental import pallas as pl
from jax.experimental.pallas import tpu as pltpu
from jax.sharding import Mesh
from jax.sharding import PartitionSpec as P

AXES = ("za", "zb", "y", "c", "h", "x")
SIZES = (2, 4, 4, 2, 2, 4)
CTX = ("za", "zb", "y", "c")
HEAD = ("h", "x")
DH = 128
TOK = 128
HEADS = 4
FEAT = HEADS * DH
STATS = 16
NEG = -1e30
F32 = jnp.float32
BF16 = jnp.bfloat16


def swap(value, axis, size, bit):
    return lax.ppermute(value, axis, [(i, i ^ bit) for i in range(size)])


def attend_kernel(sides, first, last, where, order, *refs):
    q_refs, refs = refs[:4], refs[4:]
    pieces, refs = refs[: len(sides)], refs[len(sides) :]
    if not first:
        acc_in, stat_in, *refs = refs
    if last:
        out_ref, *refs = refs
    else:
        acc_out, stat_out, *refs = refs
    score, prob, v_t, parts = refs
    za, zb, y, c = where[0], where[1], where[2], where[3]
    scale = math.log2(math.e) / math.sqrt(DH)
    lane = lax.broadcasted_iota(jnp.int32, (1, TOK), 1)
    row = lax.broadcasted_iota(jnp.int32, (TOK, 1), 0)

    def slot(ctx, index):
        return jnp.where(index < 64, order[2 * ctx], order[2 * ctx + 1]) * 64 + index % 64

    q_pos = jnp.concatenate([slot(((za * 4 + zb) * 4 + (y ^ j)) * 2 + c, lane) for j in range(4)], axis=1)
    blocks = []
    for ref, (a, side) in zip(pieces, sides):
        for p in range(4):
            n = len(blocks)
            v_t[:, n * TOK : (n + 1) * TOK] = ref[p, TOK:, :].T
            blocks.append((ref, p, slot((((za ^ a) * 4 + p) * 4 + y) * 2 + (c ^ side), row)))
    if last:
        parts[...] = jnp.zeros_like(parts)
    for h in range(HEADS):
        q = jnp.concatenate([ref[:, h * DH : (h + 1) * DH] for ref in q_refs], axis=0)
        top = jnp.full((1, 4 * TOK), NEG, F32) if first else stat_in[h : h + 1, :]
        before = top
        for n, (ref, p, k_pos) in enumerate(blocks):
            s = lax.dot_general(ref[p, :TOK, :], q, (((1,), (1,)), ((), ())), preferred_element_type=F32)
            s = jnp.where(k_pos <= q_pos, s * scale, NEG)
            score[n * TOK : (n + 1) * TOK, :] = s
            top = jnp.maximum(top, jnp.max(s, axis=0, keepdims=True))
        total = jnp.zeros((1, 4 * TOK), F32)
        for n in range(len(blocks)):
            e = jnp.exp2(score[n * TOK : (n + 1) * TOK, :] - top)
            total = total + jnp.sum(e, axis=0, keepdims=True)
            prob[n * TOK : (n + 1) * TOK, :] = e.astype(BF16)
        o = jnp.dot(v_t[...], prob[...], preferred_element_type=F32)
        if not first:
            keep = jnp.exp2(before - top)
            total = total + stat_in[HEADS + h : HEADS + h + 1, :] * keep
            o = o + acc_in[h] * keep
        if not last:
            acc_out[h] = o
            stat_out[h : h + 1, :] = top
            stat_out[HEADS + h : HEADS + h + 1, :] = total
            continue
        o = o / total
        for j in range(4):
            out_ref[y ^ j, h * DH : (h + 1) * DH, :] = o[:, j * TOK : (j + 1) * TOK].astype(BF16)
        rest = top + jnp.log2(total)
        for i in range(3):
            part = rest.astype(BF16).astype(F32)
            parts[3 * h + i : 3 * h + i + 1, :] = part
            rest = rest - part
    if last:
        for j in range(4):
            out_ref[y ^ j, FEAT:, :] = parts[:, j * TOK : (j + 1) * TOK].astype(BF16)


def merge_kernel(in_ref, out_ref):
    stats = [in_ref[j, FEAT:, :].astype(F32) for j in range(4)]
    for h in range(HEADS):
        logs = [s[3 * h : 3 * h + 1] + s[3 * h + 1 : 3 * h + 2] + s[3 * h + 2 : 3 * h + 3] for s in stats]
        top = jnp.maximum(jnp.maximum(logs[0], logs[1]), jnp.maximum(logs[2], logs[3]))
        parts = [jnp.exp2(s - top) for s in logs]
        total = parts[0] + parts[1] + parts[2] + parts[3]
        o = jnp.zeros((DH, TOK), F32)
        for j in range(4):
            o = o + in_ref[j, h * DH : (h + 1) * DH, :].astype(F32) * (parts[j] / total)
        out_ref[:, h * DH : (h + 1) * DH] = o.T.astype(BF16)


def project_kernel(where, own_ref, other_ref, near_ref, far_ref, out_ref):
    za, zb, c, h = where[0], where[1], where[3], where[4]
    for r in range(4):
        dest = zb ^ (r & 1) * 2 ^ ((r >> 1) & 1)
        w = []
        for g in range(2):
            near, far = near_ref[2 * r + g], far_ref[2 * r + g]
            left = jnp.where(c == 0, near, far)
            right = jnp.where(c == 0, far, near)
            w.append(jnp.concatenate([left, right], axis=1))
        w_own = jnp.where(za == h, w[0], w[1])
        w_other = jnp.where(za == h, w[1], w[0])
        for j in range(4):
            acc = jnp.dot(own_ref[j], w_own, preferred_element_type=F32)
            acc = acc + jnp.dot(other_ref[j], w_other, preferred_element_type=F32)
            out_ref[dest * 4 + j] = acc.astype(BF16)


def add_kernel(in_ref, out_ref):
    for j in range(4):
        total = in_ref[j].astype(F32)
        for i in range(1, 4):
            total = total + in_ref[i * 4 + j].astype(F32)
        out_ref[:, j * 256 : (j + 1) * 256] = total.astype(BF16)


SM = pl.BlockSpec(memory_space=pltpu.SMEM)
VM = pl.BlockSpec(memory_space=pltpu.VMEM)
PARAMS = pltpu.CompilerParams(vmem_limit_bytes=40 << 20)


def attend(sides, first, last, where, order, q, *arrays):
    keys = len(sides) * 4 * TOK
    if last:
        out_shape = jax.ShapeDtypeStruct((4, FEAT + STATS, TOK), BF16)
        out_specs = VM
    else:
        out_shape = (
            jax.ShapeDtypeStruct((HEADS, DH, 4 * TOK), F32),
            jax.ShapeDtypeStruct((2 * HEADS, 4 * TOK), F32),
        )
        out_specs = (VM, VM)
    return pl.pallas_call(
        functools.partial(attend_kernel, sides, first, last),
        out_shape=out_shape,
        in_specs=[SM, SM] + [VM] * (4 + len(arrays)),
        out_specs=out_specs,
        scratch_shapes=[
            pltpu.VMEM((keys, 4 * TOK), F32),
            pltpu.VMEM((keys, 4 * TOK), BF16),
            pltpu.VMEM((DH, keys), BF16),
            pltpu.VMEM((STATS, 4 * TOK), F32),
        ],
        compiler_params=PARAMS,
        cost_estimate=pl.CostEstimate(
            flops=4 * HEADS * keys * 4 * TOK * DH,
            transcendentals=HEADS * keys * 4 * TOK,
            bytes_accessed=12 << 20,
        ),
        name="attend",
    )(where, order, *q, *arrays)


def call(kernel, shape, specs, *arrays):
    return pl.pallas_call(
        kernel,
        out_shape=jax.ShapeDtypeStruct(shape, BF16),
        in_specs=specs,
        out_specs=VM,
        compiler_params=PARAMS,
    )(*arrays)


def share(value, axis):
    wide = jnp.broadcast_to(value[None], (4,) + value.shape)
    return lax.all_to_all(wide, axis, 0, 0, tiled=True)


def local(queries, keys, values, out_weight, block_order):
    together = lax.optimization_barrier
    where = jnp.stack([lax.axis_index(a).astype(jnp.int32) for a in AXES])
    kv = jnp.concatenate([keys, values], axis=0)
    away = swap(kv, "za", 2, 1)
    near0 = share(kv, "zb")
    w = lax.ppermute(out_weight, ("za", "h"), [(0, 0), (1, 2), (2, 1), (3, 3)])[None]
    away, near0, w, queries = together((away, near0, w, queries))

    near1 = share(away, "zb")
    far0 = swap(near0, "c", 2, 1)
    q = [queries] + [swap(queries, "y", 4, j) for j in (1, 2, 3)]
    w = jnp.concatenate([w, swap(w, "za", 2, 1)], axis=0)
    acc, stat = attend(((0, 0), (0, 1)), True, False, where, block_order, q, near0, far0)
    near1, acc, stat, w = together((near1, acc, stat, w))

    far1 = swap(near1, "c", 2, 1)
    w = jnp.concatenate([w, swap(w, "zb", 4, 2)], axis=0)
    acc, stat = attend(((1, 0),), False, False, where, block_order, q, near1, acc, stat)
    part = attend(((1, 1),), False, True, where, block_order, q, far1, acc, stat)
    part, w = together((part, w))

    part = lax.all_to_all(part, "y", 0, 0, tiled=True)
    w = jnp.concatenate([w, swap(w, "zb", 4, 1)], axis=0)
    part, w = together((part, w))

    attended = call(merge_kernel, (TOK, FEAT), [VM], part)
    other = swap(attended, "h", 2, 1)
    own = share(attended, "y")
    w_far = swap(w, "c", 2, 1)
    other, own, w, w_far = together((other, own, w, w_far))

    other = share(other, "y")
    tiles = call(project_kernel, (16, TOK, 256), [SM, VM, VM, VM, VM], where, own, other, w, w_far)
    tiles = lax.all_to_all(tiles, ("x", "y"), 0, 0, tiled=True)
    return call(add_kernel, (TOK, 1024), [VM], tiles)


def solution(mesh):
    fine = Mesh(mesh.devices.reshape(SIZES), AXES)
    in_specs = (P(CTX, HEAD), P(CTX, HEAD), P(CTX, HEAD), P(HEAD, CTX), P())
    return jax.shard_map(local, mesh=fine, in_specs=in_specs, out_specs=P(CTX, HEAD), check_vma=False)
```

time: 178 us -> 164 us (0.921)
  the two profiles are of different devices: /device:TPU:64 before, /device:TPU:32 now
where the time goes in v2:
time: 164 us
  starting transfers between devices  78 us (48%)
  waiting for transfers between devices  35.5 us (22%)
  blocking collectives  32.6 us (20%)
  Pallas kernels  13.9 us (8%)
  local copies, waits for them, and re-layouts  3.23 us (2%)
    ppermute x11, starting transfers between devices, swap(): return lax.ppermute(value, axis, [(i, i ^ bit) for i in range(size)])  52.5 us
    ppermute x11, waiting for transfers between devices, swap(): return lax.ppermute(value, axis, [(i, i ^ bit) for i in range(size)])  35.3 us
    all_to_all x3, starting transfers between devices, share(): return lax.all_to_all(wide, axis, 0, 0, tiled=True)  20.6 us
    all_to_all x1, blocking collectives, local(): tiles = lax.all_to_all(tiles, ('x', 'y'), 0, 0, tiled=True)  19.8 us
    all_to_all x1, blocking collectives, share(): return lax.all_to_all(wide, axis, 0, 0, tiled=True)  12.8 us
    pallas_call x3, Pallas kernels, attend(): pl.pallas_call(functools.partial(attend_kernel, sides, first, last), out_...  11 us
    all_to_all x1, starting transfers between devices, local(): part = lax.all_to_all(part, 'y', 0, 0, tiled=True)  4.32 us
  transfers between devices with their start and end apart: 16, of which 9 were waited for; matrix products, arithmetic and copies ran while one was open for 1% of the time, Pallas kernels for 5%

profile of v2, /device:TPU:32, one launch (start us, length us, event | category | flops | bytes accessed | tf_op | source)
XLA Modules:
  0.0 163.6 jit_solution(7200729077670016221)
XLA Ops:
  0.0 0.0 copy-start.2
  0.0 0.8 constant_dynamic-update-slice_fusion.1
  0.8 0.0 copy-done.2
  0.8 0.7 broadcast_in_dim.10
  1.5 0.0 copy-start.3
  1.5 9.0 %all-to-all-start = ((bf16[4,256,128]{2,1,0:T(8,128)(2,1)}), bf16[4,256,128]{2,1,0:T(8,128)(2,1)S(1)}, u32[]{:S(2)}, u32[]{:S(2)}) async-start(bf16[4,256,128]{2,1,0:T(8,128)(2,1)} %broadcast_in_dim.10), calls=%async_computation | async-start | bytes 524288 | tf_op jit(solution)/shard_map/all_to_all | solution.py:182
  10.5 0.0 copy-done.3
  10.5 0.7 collective-permute-start.1
  11.2 12.2 %collective-permute-start = (bf16[256,128]{1,0:T(8,128)(2,1)S(1)}, bf16[256,128]{1,0:T(8,128)(2,1)S(1)}, u32[]{:S(2)}, u32[]{:S(2)}) collective-permute-start(bf16[256,128]{1,0:T(8,128)(2,1)S(1)} %constant_dynamic-update-slice_fusion), channel_id=1, source_target_pairs={{0,256},{256,0},{1,257},{257,1},{2,258},{258,2},{3,259},{259,3},{4... | collective-permute-start | bytes 196616 | tf_op jit(solution)/shard_map/ppermute | solution.py:27
  23.3 2.6 %collective-permute-done = bf16[256,128]{1,0:T(8,128)(2,1)S(1)} collective-permute-done((bf16[256,128]{1,0:T(8,128)(2,1)S(1)}, bf16[256,128]{1,0:T(8,128)(2,1)S(1)}, u32[]{:S(2)}, u32[]{:S(2)}) %collective-permute-start) | collective-permute-done | bytes 65568 | tf_op jit(solution)/shard_map/ppermute | solution.py:27
  25.9 0.0 collective-permute-done.1
  25.9 0.0 all-to-all-done.refs_4_
  25.9 0.7 broadcast_in_dim.12
  26.7 0.0 copy-start
  26.7 7.5 %all-to-all-start.1 = ((bf16[4,256,128]{2,1,0:T(8,128)(2,1)}), bf16[4,256,128]{2,1,0:T(8,128)(2,1)S(1)}, u32[]{:S(2)}, u32[]{:S(2)}) async-start(bf16[4,256,128]{2,1,0:T(8,128)(2,1)} %broadcast_in_dim.12), calls=%async_computation.1 | async-start | bytes 524288 | tf_op jit(solution)/shard_map/all_to_all | solution.py:182
  34.2 1.9 %collective-permute-start.5 = (bf16[4,256,128]{2,1,0:T(8,128)(2,1)S(1)}, bf16[4,256,128]{2,1,0:T(8,128)(2,1)S(1)}, u32[]{:S(2)}, u32[]{:S(2)}) collective-permute-start(bf16[4,256,128]{2,1,0:T(8,128)(2,1)S(1)} %all-to-all-done.refs_4_), channel_id=1, source_target_pairs={{0,8},{8,0},{1,9},{9,1},{2,10},{10,2},{3,11},{11,3},{4,12},{12,4},... | collective-permute-start | bytes 786440 | tf_op jit(solution)/shard_map/ppermute | solution.py:27
  36.1 8.2 %collective-permute-start.6 = (bf16[1,512,128]{2,1,0:T(8,128)(2,1)S(1)}, bf16[1,512,128]{2,1,0:T(8,128)(2,1)S(1)}, u32[]{:S(2)}, u32[]{:S(2)}) collective-permute-start(bf16[1,512,128]{2,1,0:T(8,128)(2,1)S(1)} %bitcast.7), channel_id=1, source_target_pairs={{0,256},{256,0},{1,257},{257,1},{2,258},{258,2},{3,259},{259,3},{4... | collective-permute-start | bytes 393224 | tf_op jit(solution)/shard_map/ppermute | solution.py:27
  44.3 0.0 copy-done
  44.3 4.9 %collective-permute-start.4 = (bf16[128,512]{1,0:T(8,128)(2,1)S(1)}, bf16[128,512]{1,0:T(8,128)(2,1)S(1)}, u32[]{:S(2)}, u32[]{:S(2)}) collective-permute-start(bf16[128,512]{1,0:T(8,128)(2,1)S(1)} %copy-done), channel_id=1, source_target_pairs={{0,48},{16,32},{32,16},{48,0},{1,49},{17,33},{33,17},{49,1},{2,50}... | collective-permute-start | bytes 393224 | tf_op jit(solution)/shard_map/ppermute | solution.py:27
  49.2 2.5 %collective-permute-start.3 = (bf16[128,512]{1,0:T(8,128)(2,1)S(1)}, bf16[128,512]{1,0:T(8,128)(2,1)S(1)}, u32[]{:S(2)}, u32[]{:S(2)}) collective-permute-start(bf16[128,512]{1,0:T(8,128)(2,1)S(1)} %copy-done), channel_id=1, source_target_pairs={{0,32},{16,48},{32,0},{48,16},{1,33},{17,49},{33,1},{49,17},{2,34}... | collective-permute-start | bytes 393224 | tf_op jit(solution)/shard_map/ppermute | solution.py:27
  51.8 2.4 %collective-permute-start.2 = (bf16[128,512]{1,0:T(8,128)(2,1)S(1)}, bf16[128,512]{1,0:T(8,128)(2,1)S(1)}, u32[]{:S(2)}, u32[]{:S(2)}) collective-permute-start(bf16[128,512]{1,0:T(8,128)(2,1)S(1)} %copy-done), channel_id=1, source_target_pairs={{0,16},{16,0},{32,48},{48,32},{1,17},{17,1},{33,49},{49,33},{2,18}... | collective-permute-start | bytes 393224 | tf_op jit(solution)/shard_map/ppermute | solution.py:27
  54.2 0.1 stack.27.where
  54.2 0.0 copy-start.1
  54.2 0.6 collective-permute-done.6
  54.9 0.3 collective-permute-done.4.refs_3_
  55.2 3.2 %collective-permute-done.3.refs_2_ = bf16[128,512]{1,0:T(8,128)(2,1)S(1)} collective-permute-done((bf16[128,512]{1,0:T(8,128)(2,1)S(1)}, bf16[128,512]{1,0:T(8,128)(2,1)S(1)}, u32[]{:S(2)}, u32[]{:S(2)}) %collective-permute-start.3) | collective-permute-done | bytes 131104 | tf_op jit(solution)/shard_map/ppermute | solution.py:27
  58.4 0.4 collective-permute-done.2.refs_1_
  58.7 0.0 collective-permute-done.5.refs_5_
  58.7 0.0 copy-done.1
  58.7 4.6 %attend.3 = (f32[4,128,512]{2,1,0:T(8,128)S(1)}, f32[8,512]{1,0:T(8,128)S(1)}) custom-call(s32[6]{0:T(128)S(1)} %stack.27.where, s32[128]{0:T(128)S(1)} %copy-done.1, bf16[128,512]{1,0:T(8,128)(2,1)S(1)} %copy-done, bf16[128,512]{1,0:T(8,128)(2,1)S(1)} %collective-permute-done.2.refs_1_, bf16[128,512]{1,0:T(8,128)(2,1)S(1)} %collective-permute-done.3.refs_2_, ...), custom_call_target="tpu_custom_call" | custom-call | flops 1073741824 | bytes 12582912 | tf_op jit(solution)/shard_map/attend/pallas_call | solution.py:149
  63.4 0.0 all-to-all-done.1.refs_4_
  63.4 4.3 %collective-permute-start.8 = (bf16[2,512,128]{2,1,0:T(8,128)(2,1)S(1)}, bf16[2,512,128]{2,1,0:T(8,128)(2,1)S(1)}, u32[]{:S(2)}, u32[]{:S(2)}) collective-permute-start(bf16[2,512,128]{2,1,0:T(8,128)(2,1)S(1)} %pad_maximum_fusion.2), channel_id=1, source_target_pairs={{0,128},{64,192},{128,0},{192,64},{1,129},{65,193},{129,1},{193,65... | collective-permute-start | bytes 786440 | tf_op jit(solution)/shard_map/ppermute | solution.py:27
  67.7 1.9 %collective-permute-start.7 = (bf16[4,256,128]{2,1,0:T(8,128)(2,1)S(1)}, bf16[4,256,128]{2,1,0:T(8,128)(2,1)S(1)}, u32[]{:S(2)}, u32[]{:S(2)}) collective-permute-start(bf16[4,256,128]{2,1,0:T(8,128)(2,1)S(1)} %all-to-all-done.1.refs_4_), channel_id=1, source_target_pairs={{0,8},{8,0},{1,9},{9,1},{2,10},{10,2},{3,11},{11,3},{4,12},{12,4},... | collective-permute-start | bytes 786440 | tf_op jit(solution)/shard_map/ppermute | solution.py:27
  69.6 2.8 %attend.4 = (f32[4,128,512]{2,1,0:T(8,128)S(1)}, f32[8,512]{1,0:T(8,128)S(1)}) custom-call(s32[6]{0:T(128)S(1)} %stack.27.where, s32[128]{0:T(128)S(1)} %copy-done.1, bf16[128,512]{1,0:T(8,128)(2,1)S(1)} %copy-done, bf16[128,512]{1,0:T(8,128)(2,1)S(1)} %collective-permute-done.2.refs_1_, bf16[128,512]{1,0:T(8,128)(2,1)S(1)} %collective-permute-done.3.refs_2_, ...), custom_call_target="tpu_custom_call" | custom-call | flops 536870912 | bytes 12582912 | tf_op jit(solution)/shard_map/attend/pallas_call | solution.py:149
  72.4 5.4 %collective-permute-done.8 = bf16[2,512,128]{2,1,0:T(8,128)(2,1)S(1)} collective-permute-done((bf16[2,512,128]{2,1,0:T(8,128)(2,1)S(1)}, bf16[2,512,128]{2,1,0:T(8,128)(2,1)S(1)}, u32[]{:S(2)}, u32[]{:S(2)}) %collective-permute-start.8) | collective-permute-done | bytes 262176 | tf_op jit(solution)/shard_map/ppermute | solution.py:27
  77.8 0.0 collective-permute-done.7.refs_4_
  77.8 3.6 %attend.5 = bf16[4,528,128]{2,1,0:T(8,128)(2,1)} custom-call(s32[6]{0:T(128)S(1)} %stack.27.where, s32[128]{0:T(128)S(1)} %copy-done.1, bf16[128,512]{1,0:T(8,128)(2,1)S(1)} %copy-done, bf16[128,512]{1,0:T(8,128)(2,1)S(1)} %collective-permute-done.2.refs_1_, bf16[128,512]{1,0:T(8,128)(2,1)S(1)} %collective-permute-done.3.refs_2_, ...), custom_call_target="tpu_custom_call" | custom-call | flops 536870912 | bytes 12582912 | tf_op jit(solution)/shard_map/attend/pallas_call | solution.py:149
  81.4 3.2 %collective-permute-start.9 = (bf16[4,512,128]{2,1,0:T(8,128)(2,1)S(1)}, bf16[4,512,128]{2,1,0:T(8,128)(2,1)S(1)}, u32[]{:S(2)}, u32[]{:S(2)}) collective-permute-start(bf16[4,512,128]{2,1,0:T(8,128)(2,1)S(1)} %pad_maximum_fusion.1), channel_id=1, source_target_pairs={{0,64},{64,0},{128,192},{192,128},{1,65},{65,1},{129,193},{193,129... | collective-permute-start | bytes 1572872 | tf_op jit(solution)/shard_map/ppermute | solution.py:27
  84.6 4.3 %all-to-all-start.2 = ((bf16[4,528,128]{2,1,0:T(8,128)(2,1)}), bf16[4,528,128]{2,1,0:T(8,128)(2,1)S(1)}, u32[]{:S(2)}, u32[]{:S(2)}) async-start(bf16[4,528,128]{2,1,0:T(8,128)(2,1)} %attend.5), calls=%async_computation.2 | async-start | bytes 1081344 | tf_op jit(solution)/shard_map/all_to_all | solution.py:207
  88.9 8.2 %collective-permute-done.9 = bf16[4,512,128]{2,1,0:T(8,128)(2,1)S(1)} collective-permute-done((bf16[4,512,128]{2,1,0:T(8,128)(2,1)S(1)}, bf16[4,512,128]{2,1,0:T(8,128)(2,1)S(1)}, u32[]{:S(2)}, u32[]{:S(2)}) %collective-permute-start.9) | collective-permute-done | bytes 524320 | tf_op jit(solution)/shard_map/ppermute | solution.py:27
  97.1 0.1 pad_maximum_fusion.near_ref
  97.2 0.3 all-to-all-done.2.in_ref
  97.5 1.9 %collective-permute-start.11 = (bf16[8,512,128]{2,1,0:T(8,128)(2,1)S(1)}, bf16[8,512,128]{2,1,0:T(8,128)(2,1)S(1)}, u32[]{:S(2)}, u32[]{:S(2)}) collective-permute-start(bf16[8,512,128]{2,1,0:T(8,128)(2,1)S(1)} %pad_maximum_fusion.near_ref), channel_id=1, source_target_pairs={{0,8},{8,0},{1,9},{9,1},{2,10},{10,2},{3,11},{11,3},{4,12},{12,4},... | collective-permute-start | bytes 3145736 | tf_op jit(solution)/shard_map/ppermute | solution.py:27
  99.4 0.2 shard_map.55
  99.6 0.8 broadcast_in_dim.13
  100.4 4.1 %all-to-all-start.3 = ((bf16[4,128,512]{2,1,0:T(8,128)(2,1)}), bf16[4,128,512]{2,1,0:T(8,128)(2,1)S(1)}, u32[]{:S(2)}, u32[]{:S(2)}) async-start(bf16[4,128,512]{2,1,0:T(8,128)(2,1)} %broadcast_in_dim.13), calls=%async_computation.3 | async-start | bytes 1048576 | tf_op jit(solution)/shard_map/all_to_all | solution.py:182
  104.5 9.1 %collective-permute-start.10 = (bf16[128,512]{1,0:T(8,128)(2,1)S(1)}, bf16[128,512]{1,0:T(8,128)(2,1)S(1)}, u32[]{:S(2)}, u32[]{:S(2)}) collective-permute-start(bf16[128,512]{1,0:T(8,128)(2,1)S(1)} %shard_map.55), channel_id=1, source_target_pairs={{0,4},{4,0},{1,5},{5,1},{2,6},{6,2},{3,7},{7,3},{8,12},{12,8},{9,1... | collective-permute-start | bytes 393224 | tf_op jit(solution)/shard_map/ppermute | solution.py:27
  113.6 14.7 %collective-permute-done.10 = bf16[128,512]{1,0:T(8,128)(2,1)S(1)} collective-permute-done((bf16[128,512]{1,0:T(8,128)(2,1)S(1)}, bf16[128,512]{1,0:T(8,128)(2,1)S(1)}, u32[]{:S(2)}, u32[]{:S(2)}) %collective-permute-start.10) | collective-permute-done | bytes 131104 | tf_op jit(solution)/shard_map/ppermute | solution.py:27
  128.3 0.0 all-to-all-done.3.own_ref
  128.3 0.0 collective-permute-done.11.far_ref
  128.3 12.8 %all_to_all.30.other_ref = bf16[4,128,512]{2,1,0:T(8,128)(2,1)S(1)} all-to-all(bf16[4,128,512]{2,1,0:T(8,128)(2,1)S(1)} %broadcast_in_dim.14), channel_id=1, replica_groups=mesh['za'=2,'zb'=4,'y'=4,'c'=2,'h'=2,'x'=4] {'y'}, dimensions={0} | all-to-all | bytes 1048576 | tf_op jit(solution)/shard_map/all_to_all | solution.py:182
  141.2 1.9 %shard_map.56 = bf16[16,128,256]{2,1,0:T(8,128)(2,1)S(1)} custom-call(s32[6]{0:T(128)S(1)} %stack.27.where, bf16[4,128,512]{2,1,0:T(8,128)(2,1)S(1)} %all-to-all-done.3.own_ref, bf16[4,128,512]{2,1,0:T(8,128)(2,1)S(1)} %all_to_all.30.other_ref, bf16[8,512,128]{2,1,0:T(8,128)(2,1)S(1)} %pad_maximum_fusion.near_ref, ...), custom_call_target="tpu_custom_call" | custom-call | tf_op jit(solution)/shard_map/pallas_call | solution.py:171
  143.0 19.8 %all_to_all.31.in_ref = bf16[16,128,256]{2,1,0:T(8,128)(2,1)S(1)} all-to-all(bf16[16,128,256]{2,1,0:T(8,128)(2,1)S(1)} %shard_map.56), channel_id=1, replica_groups=mesh['za'=2,'zb'=4,'y'=4,'c'=2,'h'=2,'x'=4] {'x','y'}, dimensions={0} | all-to-all | bytes 2097152 | tf_op jit(solution)/shard_map/all_to_all | solution.py:219
  162.8 0.8 shard_map.57
  (4 shorter events, 0.1 us)
Async XLA Ops:
  0.0 0.8 copy-start.2
  1.5 9.0 %copy-start.3 = (bf16[512,128]{1,0:T(8,128)(2,1)S(1)}, bf16[512,128]{1,0:T(8,128)(2,1)}, u32[]{:S(2)}) copy-start(bf16[512,128]{1,0:T(8,128)(2,1)} %param.8) | copy-start | bytes 393220
  1.5 24.4 %all-to-all-start = ((bf16[4,256,128]{2,1,0:T(8,128)(2,1)}), bf16[4,256,128]{2,1,0:T(8,128)(2,1)S(1)}, u32[]{:S(2)}, u32[]{:S(2)}) async-start(bf16[4,256,128]{2,1,0:T(8,128)(2,1)} %broadcast_in_dim.10), calls=%async_computation | async-start | bytes 524288 | tf_op jit(solution)/shard_map/all_to_all | solution.py:182
  10.5 15.4 %collective-permute-start.1 = (bf16[512,128]{1,0:T(8,128)(2,1)S(1)}, bf16[512,128]{1,0:T(8,128)(2,1)S(1)}, u32[]{:S(2)}, u32[]{:S(2)}) collective-permute-start(bf16[512,128]{1,0:T(8,128)(2,1)S(1)} %copy-done.3), channel_id=1, source_target_pairs={{0,0},{4,256},{256,4},{260,260},{1,1},{5,257},{257,5},{261,261},{2... | collective-permute-start | bytes 393224 | tf_op jit(solution)/shard_map/ppermute | solution.py:191
  11.2 14.8 %collective-permute-start = (bf16[256,128]{1,0:T(8,128)(2,1)S(1)}, bf16[256,128]{1,0:T(8,128)(2,1)S(1)}, u32[]{:S(2)}, u32[]{:S(2)}) collective-permute-start(bf16[256,128]{1,0:T(8,128)(2,1)S(1)} %constant_dynamic-update-slice_fusion), channel_id=1, source_target_pairs={{0,256},{256,0},{1,257},{257,1},{2,258},{258,2},{3,259},{259,3},{4... | collective-permute-start | bytes 196616 | tf_op jit(solution)/shard_map/ppermute | solution.py:27
  26.7 17.6 %copy-start = (bf16[128,512]{1,0:T(8,128)(2,1)S(1)}, bf16[128,512]{1,0:T(8,128)(2,1)}, u32[]{:S(2)}) copy-start(bf16[128,512]{1,0:T(8,128)(2,1)} %refs_0_.2) | copy-start | bytes 393220
  26.7 36.7 %all-to-all-start.1 = ((bf16[4,256,128]{2,1,0:T(8,128)(2,1)}), bf16[4,256,128]{2,1,0:T(8,128)(2,1)S(1)}, u32[]{:S(2)}, u32[]{:S(2)}) async-start(bf16[4,256,128]{2,1,0:T(8,128)(2,1)} %broadcast_in_dim.12), calls=%async_computation.1 | async-start | bytes 524288 | tf_op jit(solution)/shard_map/all_to_all | solution.py:182
  34.2 24.6 %collective-permute-start.5 = (bf16[4,256,128]{2,1,0:T(8,128)(2,1)S(1)}, bf16[4,256,128]{2,1,0:T(8,128)(2,1)S(1)}, u32[]{:S(2)}, u32[]{:S(2)}) collective-permute-start(bf16[4,256,128]{2,1,0:T(8,128)(2,1)S(1)} %all-to-all-done.refs_4_), channel_id=1, source_target_pairs={{0,8},{8,0},{1,9},{9,1},{2,10},{10,2},{3,11},{11,3},{4,12},{12,4},... | collective-permute-start | bytes 786440 | tf_op jit(solution)/shard_map/ppermute | solution.py:27
  36.1 18.7 %collective-permute-start.6 = (bf16[1,512,128]{2,1,0:T(8,128)(2,1)S(1)}, bf16[1,512,128]{2,1,0:T(8,128)(2,1)S(1)}, u32[]{:S(2)}, u32[]{:S(2)}) collective-permute-start(bf16[1,512,128]{2,1,0:T(8,128)(2,1)S(1)} %bitcast.7), channel_id=1, source_target_pairs={{0,256},{256,0},{1,257},{257,1},{2,258},{258,2},{3,259},{259,3},{4... | collective-permute-start | bytes 393224 | tf_op jit(solution)/shard_map/ppermute | solution.py:27
  44.3 10.9 %collective-permute-start.4 = (bf16[128,512]{1,0:T(8,128)(2,1)S(1)}, bf16[128,512]{1,0:T(8,128)(2,1)S(1)}, u32[]{:S(2)}, u32[]{:S(2)}) collective-permute-start(bf16[128,512]{1,0:T(8,128)(2,1)S(1)} %copy-done), channel_id=1, source_target_pairs={{0,48},{16,32},{32,16},{48,0},{1,49},{17,33},{33,17},{49,1},{2,50}... | collective-permute-start | bytes 393224 | tf_op jit(solution)/shard_map/ppermute | solution.py:27
  49.2 9.1 %collective-permute-start.3 = (bf16[128,512]{1,0:T(8,128)(2,1)S(1)}, bf16[128,512]{1,0:T(8,128)(2,1)S(1)}, u32[]{:S(2)}, u32[]{:S(2)}) collective-permute-start(bf16[128,512]{1,0:T(8,128)(2,1)S(1)} %copy-done), channel_id=1, source_target_pairs={{0,32},{16,48},{32,0},{48,16},{1,33},{17,49},{33,1},{49,17},{2,34}... | collective-permute-start | bytes 393224 | tf_op jit(solution)/shard_map/ppermute | solution.py:27
  51.8 7.0 %collective-permute-start.2 = (bf16[128,512]{1,0:T(8,128)(2,1)S(1)}, bf16[128,512]{1,0:T(8,128)(2,1)S(1)}, u32[]{:S(2)}, u32[]{:S(2)}) collective-permute-start(bf16[128,512]{1,0:T(8,128)(2,1)S(1)} %copy-done), channel_id=1, source_target_pairs={{0,16},{16,0},{32,48},{48,32},{1,17},{17,1},{33,49},{49,33},{2,18}... | collective-permute-start | bytes 393224 | tf_op jit(solution)/shard_map/ppermute | solution.py:27
  54.2 4.5 %copy-start.1 = (s32[128]{0:T(128)S(1)}, s32[128]{0:T(128)}, u32[]{:S(2)}) copy-start(s32[128]{0:T(128)} %order.5) | copy-start | bytes 1540
  63.4 14.4 %collective-permute-start.8 = (bf16[2,512,128]{2,1,0:T(8,128)(2,1)S(1)}, bf16[2,512,128]{2,1,0:T(8,128)(2,1)S(1)}, u32[]{:S(2)}, u32[]{:S(2)}) collective-permute-start(bf16[2,512,128]{2,1,0:T(8,128)(2,1)S(1)} %pad_maximum_fusion.2), channel_id=1, source_target_pairs={{0,128},{64,192},{128,0},{192,64},{1,129},{65,193},{129,1},{193,65... | collective-permute-start | bytes 786440 | tf_op jit(solution)/shard_map/ppermute | solution.py:27
  67.7 10.1 %collective-permute-start.7 = (bf16[4,256,128]{2,1,0:T(8,128)(2,1)S(1)}, bf16[4,256,128]{2,1,0:T(8,128)(2,1)S(1)}, u32[]{:S(2)}, u32[]{:S(2)}) collective-permute-start(bf16[4,256,128]{2,1,0:T(8,128)(2,1)S(1)} %all-to-all-done.1.refs_4_), channel_id=1, source_target_pairs={{0,8},{8,0},{1,9},{9,1},{2,10},{10,2},{3,11},{11,3},{4,12},{12,4},... | collective-permute-start | bytes 786440 | tf_op jit(solution)/shard_map/ppermute | solution.py:27
  81.4 15.7 %collective-permute-start.9 = (bf16[4,512,128]{2,1,0:T(8,128)(2,1)S(1)}, bf16[4,512,128]{2,1,0:T(8,128)(2,1)S(1)}, u32[]{:S(2)}, u32[]{:S(2)}) collective-permute-start(bf16[4,512,128]{2,1,0:T(8,128)(2,1)S(1)} %pad_maximum_fusion.1), channel_id=1, source_target_pairs={{0,64},{64,0},{128,192},{192,128},{1,65},{65,1},{129,193},{193,129... | collective-permute-start | bytes 1572872 | tf_op jit(solution)/shard_map/ppermute | solution.py:27
  84.6 12.9 %all-to-all-start.2 = ((bf16[4,528,128]{2,1,0:T(8,128)(2,1)}), bf16[4,528,128]{2,1,0:T(8,128)(2,1)S(1)}, u32[]{:S(2)}, u32[]{:S(2)}) async-start(bf16[4,528,128]{2,1,0:T(8,128)(2,1)} %attend.5), calls=%async_computation.2 | async-start | bytes 1081344 | tf_op jit(solution)/shard_map/all_to_all | solution.py:207
  97.5 30.8 %collective-permute-start.11 = (bf16[8,512,128]{2,1,0:T(8,128)(2,1)S(1)}, bf16[8,512,128]{2,1,0:T(8,128)(2,1)S(1)}, u32[]{:S(2)}, u32[]{:S(2)}) collective-permute-start(bf16[8,512,128]{2,1,0:T(8,128)(2,1)S(1)} %pad_maximum_fusion.near_ref), channel_id=1, source_target_pairs={{0,8},{8,0},{1,9},{9,1},{2,10},{10,2},{3,11},{11,3},{4,12},{12,4},... | collective-permute-start | bytes 3145736 | tf_op jit(solution)/shard_map/ppermute | solution.py:27
  100.4 27.9 %all-to-all-start.3 = ((bf16[4,128,512]{2,1,0:T(8,128)(2,1)}), bf16[4,128,512]{2,1,0:T(8,128)(2,1)S(1)}, u32[]{:S(2)}, u32[]{:S(2)}) async-start(bf16[4,128,512]{2,1,0:T(8,128)(2,1)} %broadcast_in_dim.13), calls=%async_computation.3 | async-start | bytes 1048576 | tf_op jit(solution)/shard_map/all_to_all | solution.py:182
  104.5 23.8 %collective-permute-start.10 = (bf16[128,512]{1,0:T(8,128)(2,1)S(1)}, bf16[128,512]{1,0:T(8,128)(2,1)S(1)}, u32[]{:S(2)}, u32[]{:S(2)}) collective-permute-start(bf16[128,512]{1,0:T(8,128)(2,1)S(1)} %shard_map.55), channel_id=1, source_target_pairs={{0,4},{4,0},{1,5},{5,1},{2,6},{6,2},{3,7},{7,3},{8,12},{12,8},{9,1... | collective-permute-start | bytes 393224 | tf_op jit(solution)/shard_map/ppermute | solution.py:27

commit v3 on v2

v3 whole, which is shorter than its diff:
```python
import functools
import itertools
import math

import jax
import jax.numpy as jnp
from jax import lax
from jax.experimental import pallas as pl
from jax.experimental.pallas import tpu as pltpu
from jax.sharding import Mesh
from jax.sharding import PartitionSpec as P

AXES = ("za", "zc", "zd", "ya", "yb", "c", "h", "x")
SIZES = (2, 2, 2, 2, 2, 2, 2, 4)
CTX = AXES[:6]
HEAD = AXES[6:]
Y = ("ya", "yb")
TEAM = ("zd", "yb")
DH = 128
TOK = 128
HEADS = 4
FEAT = HEADS * DH
STATS = 16
NEG = -1e30
F32 = jnp.float32
BF16 = jnp.bfloat16


def swap(value, axis):
    return lax.ppermute(value, axis, [(0, 1), (1, 0)])


def attend_kernel(count, near, side, first, last, where, order, *refs):
    q_refs, kv_ref, refs = [ref.at[i] for ref in refs[:2] for i in range(2)], refs[2], refs[3:]
    if not first:
        acc_in, stat_in, *refs = refs
    if last:
        out_ref, *refs = refs
    else:
        acc_out, stat_out, *refs = refs
    score, prob, v_t, parts = refs
    za, zb, y, c = where[0], where[1], where[2], where[3]
    scale = math.log2(math.e) / math.sqrt(DH)
    lane = lax.broadcasted_iota(jnp.int32, (1, TOK), 1)
    row = lax.broadcasted_iota(jnp.int32, (TOK, 1), 0)

    def slot(ctx, index):
        return jnp.where(index < 64, order[2 * ctx], order[2 * ctx + 1]) * 64 + index % 64

    q_pos = jnp.concatenate([slot(((za * 4 + zb) * 4 + (y ^ j)) * 2 + c, lane) for j in range(4)], axis=1)
    blocks = []
    for n in range(count):
        p = n + near
        a, b = za ^ (p & 1), zb ^ (p & 2) ^ (p >> 2)
        v_t[:, n * TOK : (n + 1) * TOK] = kv_ref[n, TOK:, :].T
        blocks.append(slot(((a * 4 + b) * 4 + y) * 2 + (c ^ side), row))
    if last:
        parts[...] = jnp.zeros_like(parts)
    for h in range(HEADS):
        q = jnp.concatenate([ref[:, h * DH : (h + 1) * DH] for ref in q_refs], axis=0)
        top = jnp.full((1, 4 * TOK), NEG, F32) if first else stat_in[h : h + 1, :]
        before = top
        for n, k_pos in enumerate(blocks):
            s = lax.dot_general(kv_ref[n, :TOK, :], q, (((1,), (1,)), ((), ())), preferred_element_type=F32)
            s = jnp.where(k_pos <= q_pos, s * scale, NEG)
            score[n * TOK : (n + 1) * TOK, :] = s
            top = jnp.maximum(top, jnp.max(s, axis=0, keepdims=True))
        total = jnp.zeros((1, 4 * TOK), F32)
        for n in range(len(blocks)):
            e = jnp.exp2(score[n * TOK : (n + 1) * TOK, :] - top)
            total = total + jnp.sum(e, axis=0, keepdims=True)
            prob[n * TOK : (n + 1) * TOK, :] = e.astype(BF16)
        o = jnp.dot(v_t[...], prob[...], preferred_element_type=F32)
        if not first:
            keep = jnp.exp2(before - top)
            total = total + stat_in[HEADS + h : HEADS + h + 1, :] * keep
            o = o + acc_in[h] * keep
        if not last:
            acc_out[h] = o
            stat_out[h : h + 1, :] = top
            stat_out[HEADS + h : HEADS + h + 1, :] = total
            continue
        o = o / total
        for j in range(4):
            out_ref[y ^ j, h * DH : (h + 1) * DH, :] = o[:, j * TOK : (j + 1) * TOK].astype(BF16)
        rest = top + jnp.log2(total)
        for i in range(3):
            part = rest.astype(BF16).astype(F32)
            parts[3 * h + i : 3 * h + i + 1, :] = part
            rest = rest - part
    if last:
        for j in range(4):
            out_ref[y ^ j, FEAT:, :] = parts[:, j * TOK : (j + 1) * TOK].astype(BF16)


def merge_kernel(in_ref, out_ref):
    stats = [in_ref[j, FEAT:, :].astype(F32) for j in range(4)]
    for h in range(HEADS):
        logs = [s[3 * h : 3 * h + 1] + s[3 * h + 1 : 3 * h + 2] + s[3 * h + 2 : 3 * h + 3] for s in stats]
        top = jnp.maximum(jnp.maximum(logs[0], logs[1]), jnp.maximum(logs[2], logs[3]))
        parts = [jnp.exp2(s - top) for s in logs]
        total = parts[0] + parts[1] + parts[2] + parts[3]
        o = jnp.zeros((DH, TOK), F32)
        for j in range(4):
            o = o + in_ref[j, h * DH : (h + 1) * DH, :].astype(F32) * (parts[j] / total)
        out_ref[:, h * DH : (h + 1) * DH] = o.T.astype(BF16)


def copies_kernel(own_ref, other_ref, out_ref):
    for j in range(4):
        out_ref[j, 0] = own_ref[...]
        out_ref[j, 1] = other_ref[...]


def project_kernel(where, pair_ref, near_ref, far_ref, out_ref):
    za, zc, ya, c, h = where[0], where[1] // 2, where[2] // 2, where[3], where[4]
    for r in range(4):
        dest = (zc ^ (r & 1)) * 2 + (ya ^ (r >> 1))
        w = []
        for g in range(2):
            near, far = near_ref[2 * r + g], far_ref[2 * r + g]
            left = jnp.where(c == 0, near, far)
            right = jnp.where(c == 0, far, near)
            w.append(jnp.concatenate([left, right], axis=1))
        w_own = jnp.where(za == h, w[0], w[1])
        w_other = jnp.where(za == h, w[1], w[0])
        for j in range(4):
            acc = jnp.dot(pair_ref[j, 0], w_own, preferred_element_type=F32)
            acc = acc + jnp.dot(pair_ref[j, 1], w_other, preferred_element_type=F32)
            out_ref[j * 4 + dest] = acc.astype(BF16)


def add_kernel(in_ref, out_ref):
    for j in range(4):
        total = in_ref[4 * j].astype(F32)
        for i in range(1, 4):
            total = total + in_ref[4 * j + i].astype(F32)
        out_ref[:, j * 256 : (j + 1) * 256] = total.astype(BF16)


SM = pl.BlockSpec(memory_space=pltpu.SMEM)
VM = pl.BlockSpec(memory_space=pltpu.VMEM)
PARAMS = pltpu.CompilerParams(vmem_limit_bytes=40 << 20)


def attend(near, side, first, last, where, order, q, kv, *arrays):
    count = kv.shape[0]
    keys = count * TOK
    if last:
        out_shape = jax.ShapeDtypeStruct((4, FEAT + STATS, TOK), BF16)
        out_specs = VM
    else:
        out_shape = (
            jax.ShapeDtypeStruct((HEADS, DH, 4 * TOK), F32),
            jax.ShapeDtypeStruct((2 * HEADS, 4 * TOK), F32),
        )
        out_specs = (VM, VM)
    return pl.pallas_call(
        functools.partial(attend_kernel, count, near, side, first, last),
        out_shape=out_shape,
        in_specs=[SM, SM] + [VM] * (3 + len(arrays)),
        out_specs=out_specs,
        scratch_shapes=[
            pltpu.VMEM((keys, 4 * TOK), F32),
            pltpu.VMEM((keys, 4 * TOK), BF16),
            pltpu.VMEM((DH, keys), BF16),
            pltpu.VMEM((STATS, 4 * TOK), F32),
        ],
        compiler_params=PARAMS,
        cost_estimate=pl.CostEstimate(
            flops=4 * HEADS * keys * 4 * TOK * DH,
            transcendentals=HEADS * keys * 4 * TOK,
            bytes_accessed=12 << 20,
        ),
        name="attend",
    )(where, order, *q, kv, *arrays)


def call(kernel, shape, specs, *arrays):
    return pl.pallas_call(
        kernel,
        out_shape=jax.ShapeDtypeStruct(shape, BF16),
        in_specs=specs,
        out_specs=VM,
        compiler_params=PARAMS,
    )(*arrays)


def weight_moves():
    moves = []
    for za, zd, ya, h in itertools.product(range(2), repeat=4):
        source = ((za * 2 + zd) * 2 + ya) * 2 + h
        target = ((h * 2 + ya) * 2 + zd) * 2 + za
        moves.append((source, target))
    return moves


def local(queries, keys, values, out_weight, block_order):
    together = lax.optimization_barrier
    za, zc, zd, ya, yb, c, h, _ = [lax.axis_index(a).astype(jnp.int32) for a in AXES]
    where = jnp.stack([za, zc * 2 + zd, ya * 2 + yb, c, h])
    kv = jnp.concatenate([keys, values], axis=0)[None]
    kv, queries, out_weight = together((kv, queries, out_weight))
    kv_in = swap(kv, "za")
    q = swap(queries, "yb")
    w = lax.ppermute(out_weight, ("za", "zd", "ya", "h"), weight_moves())[None]
    kv_in, q, kv, queries, w = together((kv_in, q, kv, queries, w))

    kv = jnp.concatenate([kv, kv_in], axis=0)
    kv_in = swap(kv, "zc")
    q = jnp.stack([queries, q])
    q_in = swap(q, "ya")
    kv_in, q_in, kv, q, w = together((kv_in, q_in, kv, q, w))

    kv = jnp.concatenate([kv, kv_in], axis=0)
    kv_in = swap(kv, "zd")
    w_in = swap(w, "za")
    q = (q, q_in)
    acc, stat = attend(0, 0, True, False, where, block_order, q, kv)
    kv_in, acc, stat, kv = together((kv_in, acc, stat, kv))

    far = swap(jnp.concatenate([kv, kv_in], axis=0), "c")
    acc, stat = attend(4, 0, False, False, where, block_order, q, kv_in, acc, stat)
    part = attend(0, 1, False, True, where, block_order, q, far, acc, stat)
    part, w, w_in = together((part, w, w_in))

    part = lax.all_to_all(part, Y, 0, 0, tiled=True)
    w = jnp.concatenate([w, w_in], axis=0)
    w_in = swap(w, "zc")
    part, w, w_in = together((part, w, w_in))

    attended = call(merge_kernel, (TOK, FEAT), [VM], part)
    other = swap(attended, "h")
    w = jnp.concatenate([w, w_in], axis=0)
    w_in = swap(w, "ya")
    attended, other, w, w_in = together((attended, other, w, w_in))

    w = jnp.concatenate([w, w_in], axis=0)
    w_far = swap(w, "c")
    pair = call(copies_kernel, (4, 2, TOK, FEAT), [VM, VM], attended, other)
    pair = lax.all_to_all(pair, TEAM, 0, 0, tiled=True)
    tiles = call(project_kernel, (16, TOK, 256), [SM, VM, VM, VM], where, pair, w, w_far)
    tiles = lax.all_to_all(tiles, TEAM + ("x",), 0, 0, tiled=True)
    return call(add_kernel, (TOK, 1024), [VM], tiles)


def solution(mesh):
    fine = Mesh(mesh.devices.reshape(SIZES), AXES)
    in_specs = (P(CTX, HEAD), P(CTX, HEAD), P(CTX, HEAD), P(HEAD, CTX), P())
    return jax.shard_map(local, mesh=fine, in_specs=in_specs, out_specs=P(CTX, HEAD), check_vma=False)
```

time: 164 us -> 157 us (0.957)
  the two profiles are of different devices: /device:TPU:32 before, /device:TPU:1 now
where the time goes in v3:
time: 157 us; the launch traced here: 155 us
  starting transfers between devices  70.6 us (45%)
  waiting for transfers between devices  46.8 us (30%)
  blocking collectives  20.7 us (13%)
  Pallas kernels  14.7 us (9%)
    ppermute x11, starting transfers between devices, swap(): return lax.ppermute(value, axis, [(0, 1), (1, 0)])  62.1 us
    ppermute x11, waiting for transfers between devices, swap(): return lax.ppermute(value, axis, [(0, 1), (1, 0)])  45.5 us
    all_to_all x1, blocking collectives, local(): tiles = lax.all_to_all(tiles, TEAM + ('x',), 0, 0, tiled=True)  20.7 us
    pallas_call x3, Pallas kernels, attend(): pl.pallas_call(functools.partial(attend_kernel, count, near, side, first,...  10.8 us
    pallas_call x4, Pallas kernels, call(): pl.pallas_call(kernel, out_shape=jax.ShapeDtypeStruct(shape, BF16), in_sp...  3.91 us
    all_to_all x1, starting transfers between devices, local(): pair = lax.all_to_all(pair, TEAM, 0, 0, tiled=True)  3.51 us
    all_to_all x1, starting transfers between devices, local(): part = lax.all_to_all(part, Y, 0, 0, tiled=True)  3.47 us
  transfers between devices with their start and end apart: 14, of which 8 were waited for; matrix products, arithmetic and copies ran while one was open for 0% of the time, Pallas kernels for 7%

profile of v3, /device:TPU:1, one launch (start us, length us, event | category | flops | bytes accessed | tf_op | source)
XLA Modules:
  0.0 154.9 jit_solution(16900777331345015435)
XLA Ops:
  0.0 0.0 copy-start.1
  0.0 0.8 maximum_bitcast_fusion
  0.8 1.6 %collective-permute-start.2 = (bf16[512,128]{1,0:T(8,128)(2,1)}, bf16[512,128]{1,0:T(8,128)(2,1)S(1)}, u32[]{:S(2)}, u32[]{:S(2)}) collective-permute-start(bf16[512,128]{1,0:T(8,128)(2,1)} %param.8), channel_id=1, source_target_pairs={{0,0},{4,256},{32,64},{36,320},{64,32},{68,288},{96,96},{100,352},... | collective-permute-start | bytes 393224 | tf_op jit(solution)/shard_map/ppermute | solution.py:206
  2.4 0.0 copy-done.1
  2.4 4.0 %collective-permute-start.1 = (bf16[128,512]{1,0:T(8,128)(2,1)S(1)}, bf16[128,512]{1,0:T(8,128)(2,1)S(1)}, u32[]{:S(2)}, u32[]{:S(2)}) collective-permute-start(bf16[128,512]{1,0:T(8,128)(2,1)S(1)} %copy-done.1), channel_id=1, source_target_pairs={{0,16},{16,0},{1,17},{17,1},{2,18},{18,2},{3,19},{19,3},{4,20},{20... | collective-permute-start | bytes 393224 | tf_op jit(solution)/shard_map/ppermute | solution.py:30
  6.4 16.1 %collective-permute-start = (bf16[1,256,128]{2,1,0:T(8,128)(2,1)S(1)}, bf16[1,256,128]{2,1,0:T(8,128)(2,1)S(1)}, u32[]{:S(2)}, u32[]{:S(2)}) collective-permute-start(bf16[1,256,128]{2,1,0:T(8,128)(2,1)S(1)} %maximum_bitcast_fusion), channel_id=1, source_target_pairs={{0,256},{256,0},{1,257},{257,1},{2,258},{258,2},{3,259},{259,3},{4... | collective-permute-start | bytes 196616 | tf_op jit(solution)/shard_map/ppermute | solution.py:30
  22.5 1.6 %collective-permute-done = bf16[1,256,128]{2,1,0:T(8,128)(2,1)S(1)} collective-permute-done((bf16[1,256,128]{2,1,0:T(8,128)(2,1)S(1)}, bf16[1,256,128]{2,1,0:T(8,128)(2,1)S(1)}, u32[]{:S(2)}, u32[]{:S(2)}) %collective-permute-start) | collective-permute-done | bytes 65568 | tf_op jit(solution)/shard_map/ppermute | solution.py:30
  24.2 0.0 collective-permute-done.2
  24.2 0.0 collective-permute-done.1
  24.2 8.4 %collective-permute-start.4 = (bf16[2,128,512]{2,1,0:T(8,128)(2,1)S(1)}, bf16[2,128,512]{2,1,0:T(8,128)(2,1)S(1)}, u32[]{:S(2)}, u32[]{:S(2)}) collective-permute-start(bf16[2,128,512]{2,1,0:T(8,128)(2,1)S(1)} %pad_maximum_fusion.1.refs_0_), channel_id=1, source_target_pairs={{0,32},{32,0},{1,33},{33,1},{2,34},{34,2},{3,35},{35,3},{4,36},{36... | collective-permute-start | bytes 786440 | tf_op jit(solution)/shard_map/ppermute | solution.py:30
  32.6 5.5 %collective-permute-start.3 = (bf16[2,256,128]{2,1,0:T(8,128)(2,1)S(1)}, bf16[2,256,128]{2,1,0:T(8,128)(2,1)S(1)}, u32[]{:S(2)}, u32[]{:S(2)}) collective-permute-start(bf16[2,256,128]{2,1,0:T(8,128)(2,1)S(1)} %constant_dynamic-update-slice_fusion), channel_id=1, source_target_pairs={{0,128},{128,0},{1,129},{129,1},{2,130},{130,2},{3,131},{131,3},{4... | collective-permute-start | bytes 393224 | tf_op jit(solution)/shard_map/ppermute | solution.py:30
  38.1 6.2 %collective-permute-done.3 = bf16[2,256,128]{2,1,0:T(8,128)(2,1)S(1)} collective-permute-done((bf16[2,256,128]{2,1,0:T(8,128)(2,1)S(1)}, bf16[2,256,128]{2,1,0:T(8,128)(2,1)S(1)}, u32[]{:S(2)}, u32[]{:S(2)}) %collective-permute-start.3) | collective-permute-done | bytes 131104 | tf_op jit(solution)/shard_map/ppermute | solution.py:30
  44.3 0.0 collective-permute-done.4.refs_1_
  44.3 1.9 %collective-permute-start.5 = (bf16[4,256,128]{2,1,0:T(8,128)(2,1)S(1)}, bf16[4,256,128]{2,1,0:T(8,128)(2,1)S(1)}, u32[]{:S(2)}, u32[]{:S(2)}) collective-permute-start(bf16[4,256,128]{2,1,0:T(8,128)(2,1)S(1)} %constant_dynamic-update-slice_fusion.2.refs_2_), channel_id=1, source_target_pairs={{0,64},{64,0},{1,65},{65,1},{2,66},{66,2},{3,67},{67,3},{4,68},{68... | collective-permute-start | bytes 786440 | tf_op jit(solution)/shard_map/ppermute | solution.py:30
  46.3 0.0 copy-start
  46.3 0.1 stack.32.where
  46.4 0.6 copy-done
  46.9 2.7 %attend.3 = (f32[4,128,512]{2,1,0:T(8,128)S(1)}, f32[8,512]{1,0:T(8,128)S(1)}) custom-call(s32[5]{0:T(128)S(1)} %stack.32.where, s32[128]{0:T(128)S(1)} %copy-done, bf16[2,128,512]{2,1,0:T(8,128)(2,1)S(1)} %pad_maximum_fusion.1.refs_0_, bf16[2,128,512]{2,1,0:T(8,128)(2,1)S(1)} %collective-permute-done.4.refs_1_, ...), custom_call_target="tpu_custom_call" | custom-call | flops 536870912 | bytes 12582912 | tf_op jit(solution)/shard_map/attend/pallas_call | solution.py:158
  49.6 3.8 %collective-permute-done.5.refs_2_ = bf16[4,256,128]{2,1,0:T(8,128)(2,1)S(1)} collective-permute-done((bf16[4,256,128]{2,1,0:T(8,128)(2,1)S(1)}, bf16[4,256,128]{2,1,0:T(8,128)(2,1)S(1)}, u32[]{:S(2)}, u32[]{:S(2)}) %collective-permute-start.5) | collective-permute-done | bytes 262176 | tf_op jit(solution)/shard_map/ppermute | solution.py:30
  53.5 3.5 %collective-permute-start.6 = (bf16[8,256,128]{2,1,0:T(8,128)(2,1)S(1)}, bf16[8,256,128]{2,1,0:T(8,128)(2,1)S(1)}, u32[]{:S(2)}, u32[]{:S(2)}) collective-permute-start(bf16[8,256,128]{2,1,0:T(8,128)(2,1)S(1)} %pad_maximum_fusion), channel_id=1, source_target_pairs={{0,8},{8,0},{1,9},{9,1},{2,10},{10,2},{3,11},{11,3},{4,12},{12,4},... | collective-permute-start | bytes 1572872 | tf_op jit(solution)/shard_map/ppermute | solution.py:30
  56.9 2.3 %collective-permute-start.7 = (bf16[1,512,128]{2,1,0:T(8,128)(2,1)S(1)}, bf16[1,512,128]{2,1,0:T(8,128)(2,1)S(1)}, u32[]{:S(2)}, u32[]{:S(2)}) collective-permute-start(bf16[1,512,128]{2,1,0:T(8,128)(2,1)S(1)} %bitcast.10), channel_id=1, source_target_pairs={{0,256},{256,0},{1,257},{257,1},{2,258},{258,2},{3,259},{259,3},{4... | collective-permute-start | bytes 393224 | tf_op jit(solution)/shard_map/ppermute | solution.py:30
  59.3 2.8 %attend.4 = (f32[4,128,512]{2,1,0:T(8,128)S(1)}, f32[8,512]{1,0:T(8,128)S(1)}) custom-call(s32[5]{0:T(128)S(1)} %stack.32.where, s32[128]{0:T(128)S(1)} %copy-done, bf16[2,128,512]{2,1,0:T(8,128)(2,1)S(1)} %pad_maximum_fusion.1.refs_0_, bf16[2,128,512]{2,1,0:T(8,128)(2,1)S(1)} %collective-permute-done.4.refs_1_, ...), custom_call_target="tpu_custom_call" | custom-call | flops 536870912 | bytes 12582912 | tf_op jit(solution)/shard_map/attend/pallas_call | solution.py:158
  62.1 0.0 collective-permute-done.6.refs_2_
  62.1 5.3 %attend.5 = bf16[4,528,128]{2,1,0:T(8,128)(2,1)} custom-call(s32[5]{0:T(128)S(1)} %stack.32.where, s32[128]{0:T(128)S(1)} %copy-done, bf16[2,128,512]{2,1,0:T(8,128)(2,1)S(1)} %pad_maximum_fusion.1.refs_0_, bf16[2,128,512]{2,1,0:T(8,128)(2,1)S(1)} %collective-permute-done.4.refs_1_, bf16[8,256,128]{2,1,0:T(8,128)(2,1)S(1)} %collective-permute-done.6.refs_2_, ...), custom_call_target="tpu_custom_call" | custom-call | flops 1073741824 | bytes 12582912 | tf_op jit(solution)/shard_map/attend/pallas_call | solution.py:158
  67.4 8.2 %collective-permute-done.7 = bf16[1,512,128]{2,1,0:T(8,128)(2,1)S(1)} collective-permute-done((bf16[1,512,128]{2,1,0:T(8,128)(2,1)S(1)}, bf16[1,512,128]{2,1,0:T(8,128)(2,1)S(1)}, u32[]{:S(2)}, u32[]{:S(2)}) %collective-permute-start.7) | collective-permute-done | bytes 131104 | tf_op jit(solution)/shard_map/ppermute | solution.py:30
  75.6 3.5 %all-to-all-start = ((bf16[4,528,128]{2,1,0:T(8,128)(2,1)}), bf16[4,528,128]{2,1,0:T(8,128)(2,1)S(1)}, u32[]{:S(2)}, u32[]{:S(2)}) async-start(bf16[4,528,128]{2,1,0:T(8,128)(2,1)} %attend.5), calls=%async_computation | async-start | bytes 1081344 | tf_op jit(solution)/shard_map/all_to_all | solution.py:227
  79.1 1.9 %collective-permute-start.8 = (bf16[2,512,128]{2,1,0:T(8,128)(2,1)S(1)}, bf16[2,512,128]{2,1,0:T(8,128)(2,1)S(1)}, u32[]{:S(2)}, u32[]{:S(2)}) collective-permute-start(bf16[2,512,128]{2,1,0:T(8,128)(2,1)S(1)} %constant_dynamic-update-slice_fusion.4), channel_id=1, source_target_pairs={{0,128},{128,0},{1,129},{129,1},{2,130},{130,2},{3,131},{131,3},{4... | collective-permute-start | bytes 786440 | tf_op jit(solution)/shard_map/ppermute | solution.py:30
  81.1 12.0 %collective-permute-done.8 = bf16[2,512,128]{2,1,0:T(8,128)(2,1)S(1)} collective-permute-done((bf16[2,512,128]{2,1,0:T(8,128)(2,1)S(1)}, bf16[2,512,128]{2,1,0:T(8,128)(2,1)S(1)}, u32[]{:S(2)}, u32[]{:S(2)}) %collective-permute-start.8) | collective-permute-done | bytes 262176 | tf_op jit(solution)/shard_map/ppermute | solution.py:30
  93.0 0.0 all-to-all-done.in_ref
  93.1 4.8 %collective-permute-start.10 = (bf16[4,512,128]{2,1,0:T(8,128)(2,1)S(1)}, bf16[4,512,128]{2,1,0:T(8,128)(2,1)S(1)}, u32[]{:S(2)}, u32[]{:S(2)}) collective-permute-start(bf16[4,512,128]{2,1,0:T(8,128)(2,1)S(1)} %constant_dynamic-update-slice_fusion.6), channel_id=1, source_target_pairs={{0,32},{32,0},{1,33},{33,1},{2,34},{34,2},{3,35},{35,3},{4,36},{36... | collective-permute-start | bytes 1572872 | tf_op jit(solution)/shard_map/ppermute | solution.py:30
  97.9 0.2 shard_map.55.own_ref
  98.1 7.4 %collective-permute-start.9 = (bf16[128,512]{1,0:T(8,128)(2,1)S(1)}, bf16[128,512]{1,0:T(8,128)(2,1)S(1)}, u32[]{:S(2)}, u32[]{:S(2)}) collective-permute-start(bf16[128,512]{1,0:T(8,128)(2,1)S(1)} %shard_map.55.own_ref), channel_id=1, source_target_pairs={{0,4},{4,0},{1,5},{5,1},{2,6},{6,2},{3,7},{7,3},{8,12},{12,8},{9,1... | collective-permute-start | bytes 393224 | tf_op jit(solution)/shard_map/ppermute | solution.py:30
  105.5 11.6 %collective-permute-done.9.other_ref = bf16[128,512]{1,0:T(8,128)(2,1)S(1)} collective-permute-done((bf16[128,512]{1,0:T(8,128)(2,1)S(1)}, bf16[128,512]{1,0:T(8,128)(2,1)S(1)}, u32[]{:S(2)}, u32[]{:S(2)}) %collective-permute-start.9) | collective-permute-done | bytes 131104 | tf_op jit(solution)/shard_map/ppermute | solution.py:30
  117.1 0.0 collective-permute-done.10
  117.1 1.0 shard_map.56
  118.1 3.5 %all-to-all-start.1 = ((bf16[4,2,128,512]{3,2,1,0:T(8,128)(2,1)}), bf16[4,2,128,512]{3,2,1,0:T(8,128)(2,1)S(1)}, u32[]{:S(2)}, u32[]{:S(2)}) async-start(bf16[4,2,128,512]{3,2,1,0:T(8,128)(2,1)} %shard_map.56), calls=%async_computation.1 | async-start | bytes 2097152 | tf_op jit(solution)/shard_map/all_to_all | solution.py:241
  121.7 0.1 constant_dynamic-update-slice_fusion.8.near_ref
  121.8 6.2 %collective-permute-start.11 = (bf16[8,512,128]{2,1,0:T(8,128)(2,1)S(1)}, bf16[8,512,128]{2,1,0:T(8,128)(2,1)S(1)}, u32[]{:S(2)}, u32[]{:S(2)}) collective-permute-start(bf16[8,512,128]{2,1,0:T(8,128)(2,1)S(1)} %constant_dynamic-update-slice_fusion.8.near_ref), channel_id=1, source_target_pairs={{0,8},{8,0},{1,9},{9,1},{2,10},{10,2},{3,11},{11,3},{4,12},{12,4},... | collective-permute-start | bytes 3145736 | tf_op jit(solution)/shard_map/ppermute | solution.py:30
  128.0 2.3 %collective-permute-done.11.far_ref = bf16[8,512,128]{2,1,0:T(8,128)(2,1)S(1)} collective-permute-done((bf16[8,512,128]{2,1,0:T(8,128)(2,1)S(1)}, bf16[8,512,128]{2,1,0:T(8,128)(2,1)S(1)}, u32[]{:S(2)}, u32[]{:S(2)}) %collective-permute-start.11) | collective-permute-done | bytes 1048608 | tf_op jit(solution)/shard_map/ppermute | solution.py:30
  130.3 1.3 all-to-all-done.1.pair_ref
  131.5 1.8 %shard_map.57 = bf16[16,128,256]{2,1,0:T(8,128)(2,1)S(1)} custom-call(s32[5]{0:T(128)S(1)} %stack.32.where, bf16[4,2,128,512]{3,2,1,0:T(8,128)(2,1)S(1)} %all-to-all-done.1.pair_ref, bf16[8,512,128]{2,1,0:T(8,128)(2,1)S(1)} %constant_dynamic-update-slice_fusion.8.near_ref, bf16[8,512,128]{2,1,0:T(8,128)(2,1)S(1)} %collective-permute-done.11.far_ref), custom_call_target="tpu_custom_call" | custom-call | tf_op jit(solution)/shard_map/pallas_call | solution.py:180
  133.4 20.7 %all_to_all.15.in_ref = bf16[16,128,256]{2,1,0:T(8,128)(2,1)S(1)} all-to-all(bf16[16,128,256]{2,1,0:T(8,128)(2,1)S(1)} %shard_map.57), channel_id=1, replica_groups=mesh['za'=2,'zc'=2,'zd'=2,'ya'=2,'yb'=2,'c'=2,'h'=2,'x'=4] {'zd','yb','x'}, dimensions={0} | all-to-all | bytes 2097152 | tf_op jit(solution)/shard_map/all_to_all | solution.py:243
  154.1 0.8 shard_map.58
  (11 shorter events, 0.2 us)
Async XLA Ops:
  0.0 2.4 %copy-start.1 = (bf16[128,512]{1,0:T(8,128)(2,1)S(1)}, bf16[128,512]{1,0:T(8,128)(2,1)}, u32[]{:S(2)}) copy-start(bf16[128,512]{1,0:T(8,128)(2,1)} %param.5) | copy-start | bytes 393220
  0.8 23.3 %collective-permute-start.2 = (bf16[512,128]{1,0:T(8,128)(2,1)}, bf16[512,128]{1,0:T(8,128)(2,1)S(1)}, u32[]{:S(2)}, u32[]{:S(2)}) collective-permute-start(bf16[512,128]{1,0:T(8,128)(2,1)} %param.8), channel_id=1, source_target_pairs={{0,0},{4,256},{32,64},{36,320},{64,32},{68,288},{96,96},{100,352},... | collective-permute-start | bytes 393224 | tf_op jit(solution)/shard_map/ppermute | solution.py:206
  2.4 21.8 %collective-permute-start.1 = (bf16[128,512]{1,0:T(8,128)(2,1)S(1)}, bf16[128,512]{1,0:T(8,128)(2,1)S(1)}, u32[]{:S(2)}, u32[]{:S(2)}) collective-permute-start(bf16[128,512]{1,0:T(8,128)(2,1)S(1)} %copy-done.1), channel_id=1, source_target_pairs={{0,16},{16,0},{1,17},{17,1},{2,18},{18,2},{3,19},{19,3},{4,20},{20... | collective-permute-start | bytes 393224 | tf_op jit(solution)/shard_map/ppermute | solution.py:30
  6.4 17.7 %collective-permute-start = (bf16[1,256,128]{2,1,0:T(8,128)(2,1)S(1)}, bf16[1,256,128]{2,1,0:T(8,128)(2,1)S(1)}, u32[]{:S(2)}, u32[]{:S(2)}) collective-permute-start(bf16[1,256,128]{2,1,0:T(8,128)(2,1)S(1)} %maximum_bitcast_fusion), channel_id=1, source_target_pairs={{0,256},{256,0},{1,257},{257,1},{2,258},{258,2},{3,259},{259,3},{4... | collective-permute-start | bytes 196616 | tf_op jit(solution)/shard_map/ppermute | solution.py:30
  24.2 20.1 %collective-permute-start.4 = (bf16[2,128,512]{2,1,0:T(8,128)(2,1)S(1)}, bf16[2,128,512]{2,1,0:T(8,128)(2,1)S(1)}, u32[]{:S(2)}, u32[]{:S(2)}) collective-permute-start(bf16[2,128,512]{2,1,0:T(8,128)(2,1)S(1)} %pad_maximum_fusion.1.refs_0_), channel_id=1, source_target_pairs={{0,32},{32,0},{1,33},{33,1},{2,34},{34,2},{3,35},{35,3},{4,36},{36... | collective-permute-start | bytes 786440 | tf_op jit(solution)/shard_map/ppermute | solution.py:30
  32.6 11.7 %collective-permute-start.3 = (bf16[2,256,128]{2,1,0:T(8,128)(2,1)S(1)}, bf16[2,256,128]{2,1,0:T(8,128)(2,1)S(1)}, u32[]{:S(2)}, u32[]{:S(2)}) collective-permute-start(bf16[2,256,128]{2,1,0:T(8,128)(2,1)S(1)} %constant_dynamic-update-slice_fusion), channel_id=1, source_target_pairs={{0,128},{128,0},{1,129},{129,1},{2,130},{130,2},{3,131},{131,3},{4... | collective-permute-start | bytes 393224 | tf_op jit(solution)/shard_map/ppermute | solution.py:30
  44.3 9.1 %collective-permute-start.5 = (bf16[4,256,128]{2,1,0:T(8,128)(2,1)S(1)}, bf16[4,256,128]{2,1,0:T(8,128)(2,1)S(1)}, u32[]{:S(2)}, u32[]{:S(2)}) collective-permute-start(bf16[4,256,128]{2,1,0:T(8,128)(2,1)S(1)} %constant_dynamic-update-slice_fusion.2.refs_2_), channel_id=1, source_target_pairs={{0,64},{64,0},{1,65},{65,1},{2,66},{66,2},{3,67},{67,3},{4,68},{68... | collective-permute-start | bytes 786440 | tf_op jit(solution)/shard_map/ppermute | solution.py:30
  46.3 0.7 copy-start
  53.5 8.6 %collective-permute-start.6 = (bf16[8,256,128]{2,1,0:T(8,128)(2,1)S(1)}, bf16[8,256,128]{2,1,0:T(8,128)(2,1)S(1)}, u32[]{:S(2)}, u32[]{:S(2)}) collective-permute-start(bf16[8,256,128]{2,1,0:T(8,128)(2,1)S(1)} %pad_maximum_fusion), channel_id=1, source_target_pairs={{0,8},{8,0},{1,9},{9,1},{2,10},{10,2},{3,11},{11,3},{4,12},{12,4},... | collective-permute-start | bytes 1572872 | tf_op jit(solution)/shard_map/ppermute | solution.py:30
  56.9 18.7 %collective-permute-start.7 = (bf16[1,512,128]{2,1,0:T(8,128)(2,1)S(1)}, bf16[1,512,128]{2,1,0:T(8,128)(2,1)S(1)}, u32[]{:S(2)}, u32[]{:S(2)}) collective-permute-start(bf16[1,512,128]{2,1,0:T(8,128)(2,1)S(1)} %bitcast.10), channel_id=1, source_target_pairs={{0,256},{256,0},{1,257},{257,1},{2,258},{258,2},{3,259},{259,3},{4... | collective-permute-start | bytes 393224 | tf_op jit(solution)/shard_map/ppermute | solution.py:30
  75.6 17.4 %all-to-all-start = ((bf16[4,528,128]{2,1,0:T(8,128)(2,1)}), bf16[4,528,128]{2,1,0:T(8,128)(2,1)S(1)}, u32[]{:S(2)}, u32[]{:S(2)}) async-start(bf16[4,528,128]{2,1,0:T(8,128)(2,1)} %attend.5), calls=%async_computation | async-start | bytes 1081344 | tf_op jit(solution)/shard_map/all_to_all | solution.py:227
  79.1 13.9 %collective-permute-start.8 = (bf16[2,512,128]{2,1,0:T(8,128)(2,1)S(1)}, bf16[2,512,128]{2,1,0:T(8,128)(2,1)S(1)}, u32[]{:S(2)}, u32[]{:S(2)}) collective-permute-start(bf16[2,512,128]{2,1,0:T(8,128)(2,1)S(1)} %constant_dynamic-update-slice_fusion.4), channel_id=1, source_target_pairs={{0,128},{128,0},{1,129},{129,1},{2,130},{130,2},{3,131},{131,3},{4... | collective-permute-start | bytes 786440 | tf_op jit(solution)/shard_map/ppermute | solution.py:30
  93.1 24.0 %collective-permute-start.10 = (bf16[4,512,128]{2,1,0:T(8,128)(2,1)S(1)}, bf16[4,512,128]{2,1,0:T(8,128)(2,1)S(1)}, u32[]{:S(2)}, u32[]{:S(2)}) collective-permute-start(bf16[4,512,128]{2,1,0:T(8,128)(2,1)S(1)} %constant_dynamic-update-slice_fusion.6), channel_id=1, source_target_pairs={{0,32},{32,0},{1,33},{33,1},{2,34},{34,2},{3,35},{35,3},{4,36},{36... | collective-permute-start | bytes 1572872 | tf_op jit(solution)/shard_map/ppermute | solution.py:30
  98.1 18.9 %collective-permute-start.9 = (bf16[128,512]{1,0:T(8,128)(2,1)S(1)}, bf16[128,512]{1,0:T(8,128)(2,1)S(1)}, u32[]{:S(2)}, u32[]{:S(2)}) collective-permute-start(bf16[128,512]{1,0:T(8,128)(2,1)S(1)} %shard_map.55.own_ref), channel_id=1, source_target_pairs={{0,4},{4,0},{1,5},{5,1},{2,6},{6,2},{3,7},{7,3},{8,12},{12,8},{9,1... | collective-permute-start | bytes 393224 | tf_op jit(solution)/shard_map/ppermute | solution.py:30
  118.1 13.4 %all-to-all-start.1 = ((bf16[4,2,128,512]{3,2,1,0:T(8,128)(2,1)}), bf16[4,2,128,512]{3,2,1,0:T(8,128)(2,1)S(1)}, u32[]{:S(2)}, u32[]{:S(2)}) async-start(bf16[4,2,128,512]{3,2,1,0:T(8,128)(2,1)} %shard_map.56), calls=%async_computation.1 | async-start | bytes 2097152 | tf_op jit(solution)/shard_map/all_to_all | solution.py:241
  121.8 8.5 %collective-permute-start.11 = (bf16[8,512,128]{2,1,0:T(8,128)(2,1)S(1)}, bf16[8,512,128]{2,1,0:T(8,128)(2,1)S(1)}, u32[]{:S(2)}, u32[]{:S(2)}) collective-permute-start(bf16[8,512,128]{2,1,0:T(8,128)(2,1)S(1)} %constant_dynamic-update-slice_fusion.8.near_ref), channel_id=1, source_target_pairs={{0,8},{8,0},{1,9},{9,1},{2,10},{10,2},{3,11},{11,3},{4,12},{12,4},... | collective-permute-start | bytes 3145736 | tf_op jit(solution)/shard_map/ppermute | solution.py:30

commit v4 on v3

--- a/solution.py
+++ b/solution.py
@@ -104,6 +104,14 @@
         for j in range(4):
             o = o + in_ref[j, h * DH : (h + 1) * DH, :].astype(F32) * (parts[j] / total)
         out_ref[:, h * DH : (h + 1) * DH] = o.T.astype(BF16)
+
+
+def stack_kernel(_, *refs):
+    out_ref = refs[-1]
+    start = 0
+    for ref in refs[:-1]:
+        out_ref[start : start + ref.shape[0]] = ref[...]
+        start += ref.shape[0]
 
 
 def copies_kernel(own_ref, other_ref, out_ref):
@@ -186,6 +194,21 @@
     )(*arrays)
 
 
+COST = pl.CostEstimate(flops=4 << 30, transcendentals=0, bytes_accessed=8 << 20)
+
+
+def stack(first, *arrays):
+    rows = sum(a.shape[0] for a in arrays)
+    return pl.pallas_call(
+        stack_kernel,
+        out_shape=jax.ShapeDtypeStruct((rows,) + arrays[0].shape[1:], BF16),
+        in_specs=[pl.BlockSpec(memory_space=pl.ANY)] + [VM] * len(arrays),
+        out_specs=VM,
+        compiler_params=PARAMS,
+        cost_estimate=COST,
+    )(first, *arrays)
+
+
 def weight_moves():
     moves = []
     for za, zd, ya, h in itertools.product(range(2), repeat=4):
@@ -204,15 +227,17 @@
     kv_in = swap(kv, "za")
     q = swap(queries, "yb")
     w = lax.ppermute(out_weight, ("za", "zd", "ya", "h"), weight_moves())[None]
-    kv_in, q, kv, queries, w = together((kv_in, q, kv, queries, w))
-
-    kv = jnp.concatenate([kv, kv_in], axis=0)
+    kv, kv_in, queries, out_weight = together((kv, kv_in, queries, out_weight))
+
+    kv = stack(kv_in, kv, kv_in)
     kv_in = swap(kv, "zc")
+    kv, q, queries, w = together((kv, q, queries, w))
     q = jnp.stack([queries, q])
     q_in = swap(q, "ya")
-    kv_in, q_in, kv, q, w = together((kv_in, q_in, kv, q, w))
-
-    kv = jnp.concatenate([kv, kv_in], axis=0)
+    kv, kv_in = together((kv, kv_in))
+
+    kv = stack(kv_in, kv, kv_in)
+    kv, q_in, q = together((kv, q_in, q))
     kv_in = swap(kv, "zd")
     w_in = swap(w, "za")
     q = (q, q_in)

time: 157 us -> 163 us (1.038)
  starting transfers between devices: 70.6 us -> 74.4 us
  waiting for transfers between devices: 46.8 us -> 49.8 us
    all_to_all x1, waiting for transfers between devices: 1.27 us -> 7.56 us  [local(): pair = lax.all_to_all(pair, TEAM, 0, 0, tiled=True)]
    ppermute x11, starting transfers between devices: 62.1 us -> 65.8 us  [swap(): return lax.ppermute(value, axis, [(0, 1), (1, 0)])]
    ppermute x11, waiting for transfers between devices: 45.5 us -> 42.2 us  [swap(): return lax.ppermute(value, axis, [(0, 1), (1, 0)])]
  transfers between devices with their start and end apart: 14 -> 14, of which waited for: 8 -> 7; matrix products, arithmetic and copies ran while one was open for 0% -> 0% of each run, Pallas kernels for 7% -> 7%
where the time goes in v4:
time: 163 us; the launch traced here: 162 us
  starting transfers between devices  74.4 us (46%)
  waiting for transfers between devices  49.8 us (31%)
  blocking collectives  21.5 us (13%)
  Pallas kernels  14.8 us (9%)
    ppermute x11, starting transfers between devices, swap(): return lax.ppermute(value, axis, [(0, 1), (1, 0)])  65.8 us
    ppermute x11, waiting for transfers between devices, swap(): return lax.ppermute(value, axis, [(0, 1), (1, 0)])  42.2 us
    all_to_all x1, blocking collectives, local(): tiles = lax.all_to_all(tiles, TEAM + ('x',), 0, 0, tiled=True)  21.5 us
    pallas_call x3, Pallas kernels, attend(): pl.pallas_call(functools.partial(attend_kernel, count, near, side, first,...  10.8 us
    all_to_all x1, waiting for transfers between devices, local(): pair = lax.all_to_all(pair, TEAM, 0, 0, tiled=True)  7.56 us
    pallas_call x4, Pallas kernels, call(): pl.pallas_call(kernel, out_shape=jax.ShapeDtypeStruct(shape, BF16), in_sp...  3.91 us
    all_to_all x1, starting transfers between devices, local(): pair = lax.all_to_all(pair, TEAM, 0, 0, tiled=True)  3.51 us
    all_to_all x1, starting transfers between devices, local(): part = lax.all_to_all(part, Y, 0, 0, tiled=True)  3.47 us
  transfers between devices with their start and end apart: 14, of which 7 were waited for; matrix products, arithmetic and copies ran while one was open for 0% of the time, Pallas kernels for 7%

profile of v4, /device:TPU:1, one launch (start us, length us, event | category | flops | bytes accessed | tf_op | source)
XLA Modules:
  0.0 162.5 jit_solution(14618495702147425566)
XLA Ops:
  0.0 0.0 copy-start.1
  0.0 0.8 maximum_bitcast_fusion.refs_0_
  0.8 9.6 %collective-permute-start = (bf16[1,256,128]{2,1,0:T(8,128)(2,1)S(1)}, bf16[1,256,128]{2,1,0:T(8,128)(2,1)S(1)}, u32[]{:S(2)}, u32[]{:S(2)}) collective-permute-start(bf16[1,256,128]{2,1,0:T(8,128)(2,1)S(1)} %maximum_bitcast_fusion.refs_0_), channel_id=1, source_target_pairs={{0,256},{256,0},{1,257},{257,1},{2,258},{258,2},{3,259},{259,3},{4... | collective-permute-start | bytes 196616 | tf_op jit(solution)/shard_map/ppermute | solution.py:30
  10.5 0.0 copy-done.1
  10.5 3.2 %collective-permute-start.1 = (bf16[128,512]{1,0:T(8,128)(2,1)S(1)}, bf16[128,512]{1,0:T(8,128)(2,1)S(1)}, u32[]{:S(2)}, u32[]{:S(2)}) collective-permute-start(bf16[128,512]{1,0:T(8,128)(2,1)S(1)} %copy-done.1), channel_id=1, source_target_pairs={{0,16},{16,0},{1,17},{17,1},{2,18},{18,2},{3,19},{19,3},{4,20},{20... | collective-permute-start | bytes 393224 | tf_op jit(solution)/shard_map/ppermute | solution.py:30
  13.7 1.6 collective-permute-start.2
  15.2 0.0 collective-permute-done._.refs_1_
  15.3 4.9 %collective-permute-start.3 = (bf16[2,256,128]{2,1,0:T(8,128)(2,1)S(1)}, bf16[2,256,128]{2,1,0:T(8,128)(2,1)S(1)}, u32[]{:S(2)}, u32[]{:S(2)}) collective-permute-start(bf16[2,256,128]{2,1,0:T(8,128)(2,1)S(1)} %shard_map.55.refs_0_), channel_id=1, source_target_pairs={{0,128},{128,0},{1,129},{129,1},{2,130},{130,2},{3,131},{131,3},{4... | collective-permute-start | bytes 393224 | tf_op jit(solution)/shard_map/ppermute | solution.py:30
  20.2 0.0 collective-permute-done.1
  20.2 0.0 collective-permute-done.2
  20.2 8.7 %collective-permute-start.4 = (bf16[2,128,512]{2,1,0:T(8,128)(2,1)S(1)}, bf16[2,128,512]{2,1,0:T(8,128)(2,1)S(1)}, u32[]{:S(2)}, u32[]{:S(2)}) collective-permute-start(bf16[2,128,512]{2,1,0:T(8,128)(2,1)S(1)} %pad_maximum_fusion.1.refs_0_), channel_id=1, source_target_pairs={{0,32},{32,0},{1,33},{33,1},{2,34},{34,2},{3,35},{35,3},{4,36},{36... | collective-permute-start | bytes 786440 | tf_op jit(solution)/shard_map/ppermute | solution.py:30
  28.9 0.0 collective-permute-done.3._.refs_1_
  29.0 4.1 %collective-permute-done.4.refs_1_ = bf16[2,128,512]{2,1,0:T(8,128)(2,1)S(1)} collective-permute-done((bf16[2,128,512]{2,1,0:T(8,128)(2,1)S(1)}, bf16[2,128,512]{2,1,0:T(8,128)(2,1)S(1)}, u32[]{:S(2)}, u32[]{:S(2)}) %collective-permute-start.4) | collective-permute-done | bytes 262176 | tf_op jit(solution)/shard_map/ppermute | solution.py:30
  33.1 2.6 %collective-permute-start.5 = (bf16[4,256,128]{2,1,0:T(8,128)(2,1)S(1)}, bf16[4,256,128]{2,1,0:T(8,128)(2,1)S(1)}, u32[]{:S(2)}, u32[]{:S(2)}) collective-permute-start(bf16[4,256,128]{2,1,0:T(8,128)(2,1)S(1)} %shard_map.56.refs_2_), channel_id=1, source_target_pairs={{0,64},{64,0},{1,65},{65,1},{2,66},{66,2},{3,67},{67,3},{4,68},{68... | collective-permute-start | bytes 786440 | tf_op jit(solution)/shard_map/ppermute | solution.py:30
  35.7 0.0 copy-start
  35.7 0.1 stack.32.where
  35.8 0.6 copy-done
  36.4 2.7 %attend.3 = (f32[4,128,512]{2,1,0:T(8,128)S(1)}, f32[8,512]{1,0:T(8,128)S(1)}) custom-call(s32[5]{0:T(128)S(1)} %stack.32.where, s32[128]{0:T(128)S(1)} %copy-done, bf16[2,128,512]{2,1,0:T(8,128)(2,1)S(1)} %pad_maximum_fusion.1.refs_0_, bf16[2,128,512]{2,1,0:T(8,128)(2,1)S(1)} %collective-permute-done.4.refs_1_, bf16[4,256,128]{2,1,0:T(8,128)(2,1)S(1)} %shard_map.56.refs_2_), custom_call_target="tpu_custom_call" | custom-call | flops 536870912 | bytes 12582912 | tf_op jit(solution)/shard_map/attend/pallas_call | solution.py:166
  39.1 1.1 collective-permute-done.5.refs_2_
  40.2 6.2 %collective-permute-start.6 = (bf16[8,256,128]{2,1,0:T(8,128)(2,1)S(1)}, bf16[8,256,128]{2,1,0:T(8,128)(2,1)S(1)}, u32[]{:S(2)}, u32[]{:S(2)}) collective-permute-start(bf16[8,256,128]{2,1,0:T(8,128)(2,1)S(1)} %pad_maximum_fusion), channel_id=1, source_target_pairs={{0,8},{8,0},{1,9},{9,1},{2,10},{10,2},{3,11},{11,3},{4,12},{12,4},... | collective-permute-start | bytes 1572872 | tf_op jit(solution)/shard_map/ppermute | solution.py:30
  46.4 15.5 %collective-permute-start.7 = (bf16[1,512,128]{2,1,0:T(8,128)(2,1)S(1)}, bf16[1,512,128]{2,1,0:T(8,128)(2,1)S(1)}, u32[]{:S(2)}, u32[]{:S(2)}) collective-permute-start(bf16[1,512,128]{2,1,0:T(8,128)(2,1)S(1)} %bitcast.10), channel_id=1, source_target_pairs={{0,256},{256,0},{1,257},{257,1},{2,258},{258,2},{3,259},{259,3},{4... | collective-permute-start | bytes 393224 | tf_op jit(solution)/shard_map/ppermute | solution.py:30
  61.9 2.8 %attend.4 = (f32[4,128,512]{2,1,0:T(8,128)S(1)}, f32[8,512]{1,0:T(8,128)S(1)}) custom-call(s32[5]{0:T(128)S(1)} %stack.32.where, s32[128]{0:T(128)S(1)} %copy-done, bf16[2,128,512]{2,1,0:T(8,128)(2,1)S(1)} %pad_maximum_fusion.1.refs_0_, bf16[2,128,512]{2,1,0:T(8,128)(2,1)S(1)} %collective-permute-done.4.refs_1_, ...), custom_call_target="tpu_custom_call" | custom-call | flops 536870912 | bytes 12582912 | tf_op jit(solution)/shard_map/attend/pallas_call | solution.py:166
  64.7 0.0 collective-permute-done.6.refs_2_
  64.7 5.3 %attend.5 = bf16[4,528,128]{2,1,0:T(8,128)(2,1)} custom-call(s32[5]{0:T(128)S(1)} %stack.32.where, s32[128]{0:T(128)S(1)} %copy-done, bf16[2,128,512]{2,1,0:T(8,128)(2,1)S(1)} %pad_maximum_fusion.1.refs_0_, bf16[2,128,512]{2,1,0:T(8,128)(2,1)S(1)} %collective-permute-done.4.refs_1_, bf16[8,256,128]{2,1,0:T(8,128)(2,1)S(1)} %collective-permute-done.6.refs_2_, ...), custom_call_target="tpu_custom_call" | custom-call | flops 1073741824 | bytes 12582912 | tf_op jit(solution)/shard_map/attend/pallas_call | solution.py:166
  70.1 3.4 %collective-permute-done.7 = bf16[1,512,128]{2,1,0:T(8,128)(2,1)S(1)} collective-permute-done((bf16[1,512,128]{2,1,0:T(8,128)(2,1)S(1)}, bf16[1,512,128]{2,1,0:T(8,128)(2,1)S(1)}, u32[]{:S(2)}, u32[]{:S(2)}) %collective-permute-start.7) | collective-permute-done | bytes 131104 | tf_op jit(solution)/shard_map/ppermute | solution.py:30
  73.5 3.5 %all-to-all-start = ((bf16[4,528,128]{2,1,0:T(8,128)(2,1)}), bf16[4,528,128]{2,1,0:T(8,128)(2,1)S(1)}, u32[]{:S(2)}, u32[]{:S(2)}) async-start(bf16[4,528,128]{2,1,0:T(8,128)(2,1)} %attend.5), calls=%async_computation | async-start | bytes 1081344 | tf_op jit(solution)/shard_map/all_to_all | solution.py:252
  77.0 1.9 %collective-permute-start.8 = (bf16[2,512,128]{2,1,0:T(8,128)(2,1)S(1)}, bf16[2,512,128]{2,1,0:T(8,128)(2,1)S(1)}, u32[]{:S(2)}, u32[]{:S(2)}) collective-permute-start(bf16[2,512,128]{2,1,0:T(8,128)(2,1)S(1)} %constant_dynamic-update-slice_fusion), channel_id=1, source_target_pairs={{0,128},{128,0},{1,129},{129,1},{2,130},{130,2},{3,131},{131,3},{4... | collective-permute-start | bytes 786440 | tf_op jit(solution)/shard_map/ppermute | solution.py:30
  79.0 12.8 %collective-permute-done.8 = bf16[2,512,128]{2,1,0:T(8,128)(2,1)S(1)} collective-permute-done((bf16[2,512,128]{2,1,0:T(8,128)(2,1)S(1)}, bf16[2,512,128]{2,1,0:T(8,128)(2,1)S(1)}, u32[]{:S(2)}, u32[]{:S(2)}) %collective-permute-start.8) | collective-permute-done | bytes 262176 | tf_op jit(solution)/shard_map/ppermute | solution.py:30
  91.7 0.0 all-to-all-done.in_ref
  91.8 4.8 %collective-permute-start.10 = (bf16[4,512,128]{2,1,0:T(8,128)(2,1)S(1)}, bf16[4,512,128]{2,1,0:T(8,128)(2,1)S(1)}, u32[]{:S(2)}, u32[]{:S(2)}) collective-permute-start(bf16[4,512,128]{2,1,0:T(8,128)(2,1)S(1)} %constant_dynamic-update-slice_fusion.2), channel_id=1, source_target_pairs={{0,32},{32,0},{1,33},{33,1},{2,34},{34,2},{3,35},{35,3},{4,36},{36... | collective-permute-start | bytes 1572872 | tf_op jit(solution)/shard_map/ppermute | solution.py:30
  96.6 0.2 shard_map.57.own_ref
  96.8 5.2 %collective-permute-start.9 = (bf16[128,512]{1,0:T(8,128)(2,1)S(1)}, bf16[128,512]{1,0:T(8,128)(2,1)S(1)}, u32[]{:S(2)}, u32[]{:S(2)}) collective-permute-start(bf16[128,512]{1,0:T(8,128)(2,1)S(1)} %shard_map.57.own_ref), channel_id=1, source_target_pairs={{0,4},{4,0},{1,5},{5,1},{2,6},{6,2},{3,7},{7,3},{8,12},{12,8},{9,1... | collective-permute-start | bytes 393224 | tf_op jit(solution)/shard_map/ppermute | solution.py:30
  102.0 18.6 %collective-permute-done.9.other_ref = bf16[128,512]{1,0:T(8,128)(2,1)S(1)} collective-permute-done((bf16[128,512]{1,0:T(8,128)(2,1)S(1)}, bf16[128,512]{1,0:T(8,128)(2,1)S(1)}, u32[]{:S(2)}, u32[]{:S(2)}) %collective-permute-start.9) | collective-permute-done | bytes 131104 | tf_op jit(solution)/shard_map/ppermute | solution.py:30
  120.6 0.0 collective-permute-done.10
  120.6 1.0 shard_map.58
  121.7 3.5 %all-to-all-start.1 = ((bf16[4,2,128,512]{3,2,1,0:T(8,128)(2,1)}), bf16[4,2,128,512]{3,2,1,0:T(8,128)(2,1)S(1)}, u32[]{:S(2)}, u32[]{:S(2)}) async-start(bf16[4,2,128,512]{3,2,1,0:T(8,128)(2,1)} %shard_map.58), calls=%async_computation.1 | async-start | bytes 2097152 | tf_op jit(solution)/shard_map/all_to_all | solution.py:266
  125.2 0.1 constant_dynamic-update-slice_fusion.4.near_ref
  125.3 3.1 %collective-permute-start.11 = (bf16[8,512,128]{2,1,0:T(8,128)(2,1)S(1)}, bf16[8,512,128]{2,1,0:T(8,128)(2,1)S(1)}, u32[]{:S(2)}, u32[]{:S(2)}) collective-permute-start(bf16[8,512,128]{2,1,0:T(8,128)(2,1)S(1)} %constant_dynamic-update-slice_fusion.4.near_ref), channel_id=1, source_target_pairs={{0,8},{8,0},{1,9},{9,1},{2,10},{10,2},{3,11},{11,3},{4,12},{12,4},... | collective-permute-start | bytes 3145736 | tf_op jit(solution)/shard_map/ppermute | solution.py:30
  128.4 2.3 %collective-permute-done.11.far_ref = bf16[8,512,128]{2,1,0:T(8,128)(2,1)S(1)} collective-permute-done((bf16[8,512,128]{2,1,0:T(8,128)(2,1)S(1)}, bf16[8,512,128]{2,1,0:T(8,128)(2,1)S(1)}, u32[]{:S(2)}, u32[]{:S(2)}) %collective-permute-start.11) | collective-permute-done | bytes 1048608 | tf_op jit(solution)/shard_map/ppermute | solution.py:30
  130.7 7.6 %all-to-all-done.1.pair_ref = bf16[4,2,128,512]{3,2,1,0:T(8,128)(2,1)S(1)} async-done(((bf16[4,2,128,512]{3,2,1,0:T(8,128)(2,1)}), bf16[4,2,128,512]{3,2,1,0:T(8,128)(2,1)S(1)}, u32[]{:S(2)}, u32[]{:S(2)}) %all-to-all-start.1) | async-done | bytes 1048608 | tf_op jit(solution)/shard_map/all_to_all | solution.py:266
  138.2 1.8 %shard_map.59 = bf16[16,128,256]{2,1,0:T(8,128)(2,1)S(1)} custom-call(s32[5]{0:T(128)S(1)} %stack.32.where, bf16[4,2,128,512]{3,2,1,0:T(8,128)(2,1)S(1)} %all-to-all-done.1.pair_ref, bf16[8,512,128]{2,1,0:T(8,128)(2,1)S(1)} %constant_dynamic-update-slice_fusion.4.near_ref, bf16[8,512,128]{2,1,0:T(8,128)(2,1)S(1)} %collective-permute-done.11.far_ref), custom_call_target="tpu_custom_call" | custom-call | tf_op jit(solution)/shard_map/pallas_call | solution.py:188
  140.1 21.5 %all_to_all.15.in_ref = bf16[16,128,256]{2,1,0:T(8,128)(2,1)S(1)} all-to-all(bf16[16,128,256]{2,1,0:T(8,128)(2,1)S(1)} %shard_map.59), channel_id=1, replica_groups=mesh['za'=2,'zc'=2,'zd'=2,'ya'=2,'yb'=2,'c'=2,'h'=2,'x'=4] {'zd','yb','x'}, dimensions={0} | all-to-all | bytes 2097152 | tf_op jit(solution)/shard_map/all_to_all | solution.py:268
  161.6 0.8 shard_map.60
  (9 shorter events, 0.2 us)
Async XLA Ops:
  0.0 10.5 %copy-start.1 = (bf16[128,512]{1,0:T(8,128)(2,1)S(1)}, bf16[128,512]{1,0:T(8,128)(2,1)}, u32[]{:S(2)}) copy-start(bf16[128,512]{1,0:T(8,128)(2,1)} %param.5) | copy-start | bytes 393220
  0.8 14.4 %collective-permute-start = (bf16[1,256,128]{2,1,0:T(8,128)(2,1)S(1)}, bf16[1,256,128]{2,1,0:T(8,128)(2,1)S(1)}, u32[]{:S(2)}, u32[]{:S(2)}) collective-permute-start(bf16[1,256,128]{2,1,0:T(8,128)(2,1)S(1)} %maximum_bitcast_fusion.refs_0_), channel_id=1, source_target_pairs={{0,256},{256,0},{1,257},{257,1},{2,258},{258,2},{3,259},{259,3},{4... | collective-permute-start | bytes 196616 | tf_op jit(solution)/shard_map/ppermute | solution.py:30
  10.5 9.7 %collective-permute-start.1 = (bf16[128,512]{1,0:T(8,128)(2,1)S(1)}, bf16[128,512]{1,0:T(8,128)(2,1)S(1)}, u32[]{:S(2)}, u32[]{:S(2)}) collective-permute-start(bf16[128,512]{1,0:T(8,128)(2,1)S(1)} %copy-done.1), channel_id=1, source_target_pairs={{0,16},{16,0},{1,17},{17,1},{2,18},{18,2},{3,19},{19,3},{4,20},{20... | collective-permute-start | bytes 393224 | tf_op jit(solution)/shard_map/ppermute | solution.py:30
  13.7 6.5 %collective-permute-start.2 = (bf16[512,128]{1,0:T(8,128)(2,1)}, bf16[512,128]{1,0:T(8,128)(2,1)S(1)}, u32[]{:S(2)}, u32[]{:S(2)}) collective-permute-start(bf16[512,128]{1,0:T(8,128)(2,1)} %param.8), channel_id=1, source_target_pairs={{0,0},{4,256},{32,64},{36,320},{64,32},{68,288},{96,96},{100,352},... | collective-permute-start | bytes 393224 | tf_op jit(solution)/shard_map/ppermute | solution.py:229
  15.3 13.7 %collective-permute-start.3 = (bf16[2,256,128]{2,1,0:T(8,128)(2,1)S(1)}, bf16[2,256,128]{2,1,0:T(8,128)(2,1)S(1)}, u32[]{:S(2)}, u32[]{:S(2)}) collective-permute-start(bf16[2,256,128]{2,1,0:T(8,128)(2,1)S(1)} %shard_map.55.refs_0_), channel_id=1, source_target_pairs={{0,128},{128,0},{1,129},{129,1},{2,130},{130,2},{3,131},{131,3},{4... | collective-permute-start | bytes 393224 | tf_op jit(solution)/shard_map/ppermute | solution.py:30
  20.2 12.8 %collective-permute-start.4 = (bf16[2,128,512]{2,1,0:T(8,128)(2,1)S(1)}, bf16[2,128,512]{2,1,0:T(8,128)(2,1)S(1)}, u32[]{:S(2)}, u32[]{:S(2)}) collective-permute-start(bf16[2,128,512]{2,1,0:T(8,128)(2,1)S(1)} %pad_maximum_fusion.1.refs_0_), channel_id=1, source_target_pairs={{0,32},{32,0},{1,33},{33,1},{2,34},{34,2},{3,35},{35,3},{4,36},{36... | collective-permute-start | bytes 786440 | tf_op jit(solution)/shard_map/ppermute | solution.py:30
  33.1 7.1 %collective-permute-start.5 = (bf16[4,256,128]{2,1,0:T(8,128)(2,1)S(1)}, bf16[4,256,128]{2,1,0:T(8,128)(2,1)S(1)}, u32[]{:S(2)}, u32[]{:S(2)}) collective-permute-start(bf16[4,256,128]{2,1,0:T(8,128)(2,1)S(1)} %shard_map.56.refs_2_), channel_id=1, source_target_pairs={{0,64},{64,0},{1,65},{65,1},{2,66},{66,2},{3,67},{67,3},{4,68},{68... | collective-permute-start | bytes 786440 | tf_op jit(solution)/shard_map/ppermute | solution.py:30
  35.7 0.7 copy-start
  40.2 24.5 %collective-permute-start.6 = (bf16[8,256,128]{2,1,0:T(8,128)(2,1)S(1)}, bf16[8,256,128]{2,1,0:T(8,128)(2,1)S(1)}, u32[]{:S(2)}, u32[]{:S(2)}) collective-permute-start(bf16[8,256,128]{2,1,0:T(8,128)(2,1)S(1)} %pad_maximum_fusion), channel_id=1, source_target_pairs={{0,8},{8,0},{1,9},{9,1},{2,10},{10,2},{3,11},{11,3},{4,12},{12,4},... | collective-permute-start | bytes 1572872 | tf_op jit(solution)/shard_map/ppermute | solution.py:30
  46.4 27.1 %collective-permute-start.7 = (bf16[1,512,128]{2,1,0:T(8,128)(2,1)S(1)}, bf16[1,512,128]{2,1,0:T(8,128)(2,1)S(1)}, u32[]{:S(2)}, u32[]{:S(2)}) collective-permute-start(bf16[1,512,128]{2,1,0:T(8,128)(2,1)S(1)} %bitcast.10), channel_id=1, source_target_pairs={{0,256},{256,0},{1,257},{257,1},{2,258},{258,2},{3,259},{259,3},{4... | collective-permute-start | bytes 393224 | tf_op jit(solution)/shard_map/ppermute | solution.py:30
  73.5 18.2 %all-to-all-start = ((bf16[4,528,128]{2,1,0:T(8,128)(2,1)}), bf16[4,528,128]{2,1,0:T(8,128)(2,1)S(1)}, u32[]{:S(2)}, u32[]{:S(2)}) async-start(bf16[4,528,128]{2,1,0:T(8,128)(2,1)} %attend.5), calls=%async_computation | async-start | bytes 1081344 | tf_op jit(solution)/shard_map/all_to_all | solution.py:252
  77.0 14.7 %collective-permute-start.8 = (bf16[2,512,128]{2,1,0:T(8,128)(2,1)S(1)}, bf16[2,512,128]{2,1,0:T(8,128)(2,1)S(1)}, u32[]{:S(2)}, u32[]{:S(2)}) collective-permute-start(bf16[2,512,128]{2,1,0:T(8,128)(2,1)S(1)} %constant_dynamic-update-slice_fusion), channel_id=1, source_target_pairs={{0,128},{128,0},{1,129},{129,1},{2,130},{130,2},{3,131},{131,3},{4... | collective-permute-start | bytes 786440 | tf_op jit(solution)/shard_map/ppermute | solution.py:30
  91.8 28.8 %collective-permute-start.10 = (bf16[4,512,128]{2,1,0:T(8,128)(2,1)S(1)}, bf16[4,512,128]{2,1,0:T(8,128)(2,1)S(1)}, u32[]{:S(2)}, u32[]{:S(2)}) collective-permute-start(bf16[4,512,128]{2,1,0:T(8,128)(2,1)S(1)} %constant_dynamic-update-slice_fusion.2), channel_id=1, source_target_pairs={{0,32},{32,0},{1,33},{33,1},{2,34},{34,2},{3,35},{35,3},{4,36},{36... | collective-permute-start | bytes 1572872 | tf_op jit(solution)/shard_map/ppermute | solution.py:30
  96.8 23.8 %collective-permute-start.9 = (bf16[128,512]{1,0:T(8,128)(2,1)S(1)}, bf16[128,512]{1,0:T(8,128)(2,1)S(1)}, u32[]{:S(2)}, u32[]{:S(2)}) collective-permute-start(bf16[128,512]{1,0:T(8,128)(2,1)S(1)} %shard_map.57.own_ref), channel_id=1, source_target_pairs={{0,4},{4,0},{1,5},{5,1},{2,6},{6,2},{3,7},{7,3},{8,12},{12,8},{9,1... | collective-permute-start | bytes 393224 | tf_op jit(solution)/shard_map/ppermute | solution.py:30
  121.7 16.6 %all-to-all-start.1 = ((bf16[4,2,128,512]{3,2,1,0:T(8,128)(2,1)}), bf16[4,2,128,512]{3,2,1,0:T(8,128)(2,1)S(1)}, u32[]{:S(2)}, u32[]{:S(2)}) async-start(bf16[4,2,128,512]{3,2,1,0:T(8,128)(2,1)} %shard_map.58), calls=%async_computation.1 | async-start | bytes 2097152 | tf_op jit(solution)/shard_map/all_to_all | solution.py:266
  125.3 5.4 %collective-permute-start.11 = (bf16[8,512,128]{2,1,0:T(8,128)(2,1)S(1)}, bf16[8,512,128]{2,1,0:T(8,128)(2,1)S(1)}, u32[]{:S(2)}, u32[]{:S(2)}) collective-permute-start(bf16[8,512,128]{2,1,0:T(8,128)(2,1)S(1)} %constant_dynamic-update-slice_fusion.4.near_ref), channel_id=1, source_target_pairs={{0,8},{8,0},{1,9},{9,1},{2,10},{10,2},{3,11},{11,3},{4,12},{12,4},... | collective-permute-start | bytes 3145736 | tf_op jit(solution)/shard_map/ppermute | solution.py:30

commit v5 on v4

--- a/solution.py
+++ b/solution.py
@@ -252,17 +252,23 @@
     part = lax.all_to_all(part, Y, 0, 0, tiled=True)
     w = jnp.concatenate([w, w_in], axis=0)
     w_in = swap(w, "zc")
-    part, w, w_in = together((part, w, w_in))
-
     attended = call(merge_kernel, (TOK, FEAT), [VM], part)
+    _, w, w_in = together((attended, w, w_in))
     other = swap(attended, "h")
     w = jnp.concatenate([w, w_in], axis=0)
     w_in = swap(w, "ya")
-    attended, other, w, w_in = together((attended, other, w, w_in))
+    pair = pl.pallas_call(
+        copies_kernel,
+        out_shape=jax.ShapeDtypeStruct((4, 2, TOK, FEAT), BF16),
+        in_specs=[VM, VM],
+        out_specs=VM,
+        compiler_params=PARAMS,
+        cost_estimate=COST,
+    )(attended, other)
+    pair, w, w_in = together((pair, w, w_in))
 
     w = jnp.concatenate([w, w_in], axis=0)
     w_far = swap(w, "c")
-    pair = call(copies_kernel, (4, 2, TOK, FEAT), [VM, VM], attended, other)
     pair = lax.all_to_all(pair, TEAM, 0, 0, tiled=True)
     tiles = call(project_kernel, (16, TOK, 256), [SM, VM, VM, VM], where, pair, w, w_far)
     tiles = lax.all_to_all(tiles, TEAM + ("x",), 0, 0, tiled=True)

time: 163 us -> 157 us (0.963)
  waiting for transfers between devices: 49.8 us -> 36.6 us
  starting transfers between devices: 74.4 us -> 81.3 us
    ppermute x11, waiting for transfers between devices: 42.2 us -> 21.6 us  [swap(): return lax.ppermute(value, axis, [(0, 1), (1, 0)])]
    all_to_all x1, waiting for transfers between devices: 0.01 us -> 7.35 us  [local(): part = lax.all_to_all(part, Y, 0, 0, tiled=True)]
    ppermute x11, starting transfers between devices: 65.8 us -> 72.7 us  [swap(): return lax.ppermute(value, axis, [(0, 1), (1, 0)])]
    pallas_call x4 -> x3, Pallas kernels: 3.91 us -> 2.87 us  [call(): pl.pallas_call(kernel, out_shape=jax.ShapeDtypeStruct(shape, BF16), in_sp...]
  transfers between devices with their start and end apart: 14 -> 14, of which waited for: 7 -> 7; matrix products, arithmetic and copies ran while one was open for 0% -> 0% of each run, Pallas kernels for 7% -> 8%
where the time goes in v5:
time: 157 us; the launch traced here: 156 us
  starting transfers between devices  81.3 us (52%)
  waiting for transfers between devices  36.6 us (23%)
  blocking collectives  21.5 us (14%)
  Pallas kernels  14.8 us (9%)
    ppermute x11, starting transfers between devices, swap(): return lax.ppermute(value, axis, [(0, 1), (1, 0)])  72.7 us
    ppermute x11, waiting for transfers between devices, swap(): return lax.ppermute(value, axis, [(0, 1), (1, 0)])  21.6 us
    all_to_all x1, blocking collectives, local(): tiles = lax.all_to_all(tiles, TEAM + ('x',), 0, 0, tiled=True)  21.5 us
    pallas_call x3, Pallas kernels, attend(): pl.pallas_call(functools.partial(attend_kernel, count, near, side, first,...  10.8 us
    all_to_all x1, waiting for transfers between devices, local(): pair = lax.all_to_all(pair, TEAM, 0, 0, tiled=True)  7.65 us
    all_to_all x1, waiting for transfers between devices, local(): part = lax.all_to_all(part, Y, 0, 0, tiled=True)  7.35 us
    all_to_all x1, starting transfers between devices, local(): pair = lax.all_to_all(pair, TEAM, 0, 0, tiled=True)  3.52 us
    all_to_all x1, starting transfers between devices, local(): part = lax.all_to_all(part, Y, 0, 0, tiled=True)  3.47 us
  transfers between devices with their start and end apart: 14, of which 7 were waited for; matrix products, arithmetic and copies ran while one was open for 0% of the time, Pallas kernels for 8%

profile of v5, /device:TPU:1, one launch (start us, length us, event | category | flops | bytes accessed | tf_op | source)
XLA Modules:
  0.0 156.2 jit_solution(3580240610054008893)
XLA Ops:
  0.0 0.0 copy-start.1
  0.0 0.8 maximum_bitcast_fusion.refs_0_
  0.8 9.6 %collective-permute-start = (bf16[1,256,128]{2,1,0:T(8,128)(2,1)S(1)}, bf16[1,256,128]{2,1,0:T(8,128)(2,1)S(1)}, u32[]{:S(2)}, u32[]{:S(2)}) collective-permute-start(bf16[1,256,128]{2,1,0:T(8,128)(2,1)S(1)} %maximum_bitcast_fusion.refs_0_), channel_id=1, source_target_pairs={{0,256},{256,0},{1,257},{257,1},{2,258},{258,2},{3,259},{259,3},{4... | collective-permute-start | bytes 196616 | tf_op jit(solution)/shard_map/ppermute | solution.py:30
  10.5 0.0 copy-done.1
  10.5 3.2 %collective-permute-start.1 = (bf16[128,512]{1,0:T(8,128)(2,1)S(1)}, bf16[128,512]{1,0:T(8,128)(2,1)S(1)}, u32[]{:S(2)}, u32[]{:S(2)}) collective-permute-start(bf16[128,512]{1,0:T(8,128)(2,1)S(1)} %copy-done.1), channel_id=1, source_target_pairs={{0,16},{16,0},{1,17},{17,1},{2,18},{18,2},{3,19},{19,3},{4,20},{20... | collective-permute-start | bytes 393224 | tf_op jit(solution)/shard_map/ppermute | solution.py:30
  13.7 1.6 %collective-permute-start.2 = (bf16[512,128]{1,0:T(8,128)(2,1)}, bf16[512,128]{1,0:T(8,128)(2,1)S(1)}, u32[]{:S(2)}, u32[]{:S(2)}) collective-permute-start(bf16[512,128]{1,0:T(8,128)(2,1)} %param.8), channel_id=1, source_target_pairs={{0,0},{4,256},{32,64},{36,320},{64,32},{68,288},{96,96},{100,352},... | collective-permute-start | bytes 393224 | tf_op jit(solution)/shard_map/ppermute | solution.py:229
  15.2 0.0 collective-permute-done._.refs_1_
  15.3 4.9 %collective-permute-start.3 = (bf16[2,256,128]{2,1,0:T(8,128)(2,1)S(1)}, bf16[2,256,128]{2,1,0:T(8,128)(2,1)S(1)}, u32[]{:S(2)}, u32[]{:S(2)}) collective-permute-start(bf16[2,256,128]{2,1,0:T(8,128)(2,1)S(1)} %shard_map.55.refs_0_), channel_id=1, source_target_pairs={{0,128},{128,0},{1,129},{129,1},{2,130},{130,2},{3,131},{131,3},{4... | collective-permute-start | bytes 393224 | tf_op jit(solution)/shard_map/ppermute | solution.py:30
  20.2 0.0 collective-permute-done.1
  20.2 0.0 collective-permute-done.2
  20.2 8.7 %collective-permute-start.4 = (bf16[2,128,512]{2,1,0:T(8,128)(2,1)S(1)}, bf16[2,128,512]{2,1,0:T(8,128)(2,1)S(1)}, u32[]{:S(2)}, u32[]{:S(2)}) collective-permute-start(bf16[2,128,512]{2,1,0:T(8,128)(2,1)S(1)} %pad_maximum_fusion.1.refs_0_), channel_id=1, source_target_pairs={{0,32},{32,0},{1,33},{33,1},{2,34},{34,2},{3,35},{35,3},{4,36},{36... | collective-permute-start | bytes 786440 | tf_op jit(solution)/shard_map/ppermute | solution.py:30
  28.9 0.0 collective-permute-done.3._.refs_1_
  29.0 4.1 %collective-permute-done.4.refs_1_ = bf16[2,128,512]{2,1,0:T(8,128)(2,1)S(1)} collective-permute-done((bf16[2,128,512]{2,1,0:T(8,128)(2,1)S(1)}, bf16[2,128,512]{2,1,0:T(8,128)(2,1)S(1)}, u32[]{:S(2)}, u32[]{:S(2)}) %collective-permute-start.4) | collective-permute-done | bytes 262176 | tf_op jit(solution)/shard_map/ppermute | solution.py:30
  33.1 2.6 %collective-permute-start.5 = (bf16[4,256,128]{2,1,0:T(8,128)(2,1)S(1)}, bf16[4,256,128]{2,1,0:T(8,128)(2,1)S(1)}, u32[]{:S(2)}, u32[]{:S(2)}) collective-permute-start(bf16[4,256,128]{2,1,0:T(8,128)(2,1)S(1)} %shard_map.56.refs_2_), channel_id=1, source_target_pairs={{0,64},{64,0},{1,65},{65,1},{2,66},{66,2},{3,67},{67,3},{4,68},{68... | collective-permute-start | bytes 786440 | tf_op jit(solution)/shard_map/ppermute | solution.py:30
  35.7 0.0 copy-start
  35.7 0.1 stack.32.where
  35.8 0.6 copy-done
  36.4 2.7 %attend.3 = (f32[4,128,512]{2,1,0:T(8,128)S(1)}, f32[8,512]{1,0:T(8,128)S(1)}) custom-call(s32[5]{0:T(128)S(1)} %stack.32.where, s32[128]{0:T(128)S(1)} %copy-done, bf16[2,128,512]{2,1,0:T(8,128)(2,1)S(1)} %pad_maximum_fusion.1.refs_0_, bf16[2,128,512]{2,1,0:T(8,128)(2,1)S(1)} %collective-permute-done.4.refs_1_, bf16[4,256,128]{2,1,0:T(8,128)(2,1)S(1)} %shard_map.56.refs_2_), custom_call_target="tpu_custom_call" | custom-call | flops 536870912 | bytes 12582912 | tf_op jit(solution)/shard_map/attend/pallas_call | solution.py:166
  39.1 1.1 collective-permute-done.5.refs_2_
  40.2 6.2 %collective-permute-start.6 = (bf16[8,256,128]{2,1,0:T(8,128)(2,1)S(1)}, bf16[8,256,128]{2,1,0:T(8,128)(2,1)S(1)}, u32[]{:S(2)}, u32[]{:S(2)}) collective-permute-start(bf16[8,256,128]{2,1,0:T(8,128)(2,1)S(1)} %pad_maximum_fusion), channel_id=1, source_target_pairs={{0,8},{8,0},{1,9},{9,1},{2,10},{10,2},{3,11},{11,3},{4,12},{12,4},... | collective-permute-start | bytes 1572872 | tf_op jit(solution)/shard_map/ppermute | solution.py:30
  46.4 15.5 %collective-permute-start.7 = (bf16[1,512,128]{2,1,0:T(8,128)(2,1)S(1)}, bf16[1,512,128]{2,1,0:T(8,128)(2,1)S(1)}, u32[]{:S(2)}, u32[]{:S(2)}) collective-permute-start(bf16[1,512,128]{2,1,0:T(8,128)(2,1)S(1)} %bitcast.10), channel_id=1, source_target_pairs={{0,256},{256,0},{1,257},{257,1},{2,258},{258,2},{3,259},{259,3},{4... | collective-permute-start | bytes 393224 | tf_op jit(solution)/shard_map/ppermute | solution.py:30
  61.9 2.8 %attend.4 = (f32[4,128,512]{2,1,0:T(8,128)S(1)}, f32[8,512]{1,0:T(8,128)S(1)}) custom-call(s32[5]{0:T(128)S(1)} %stack.32.where, s32[128]{0:T(128)S(1)} %copy-done, bf16[2,128,512]{2,1,0:T(8,128)(2,1)S(1)} %pad_maximum_fusion.1.refs_0_, bf16[2,128,512]{2,1,0:T(8,128)(2,1)S(1)} %collective-permute-done.4.refs_1_, ...), custom_call_target="tpu_custom_call" | custom-call | flops 536870912 | bytes 12582912 | tf_op jit(solution)/shard_map/attend/pallas_call | solution.py:166
  64.7 0.0 collective-permute-done.6.refs_2_
  64.7 5.3 %attend.5 = bf16[4,528,128]{2,1,0:T(8,128)(2,1)} custom-call(s32[5]{0:T(128)S(1)} %stack.32.where, s32[128]{0:T(128)S(1)} %copy-done, bf16[2,128,512]{2,1,0:T(8,128)(2,1)S(1)} %pad_maximum_fusion.1.refs_0_, bf16[2,128,512]{2,1,0:T(8,128)(2,1)S(1)} %collective-permute-done.4.refs_1_, bf16[8,256,128]{2,1,0:T(8,128)(2,1)S(1)} %collective-permute-done.6.refs_2_, ...), custom_call_target="tpu_custom_call" | custom-call | flops 1073741824 | bytes 12582912 | tf_op jit(solution)/shard_map/attend/pallas_call | solution.py:166
  70.1 3.4 %collective-permute-done.7 = bf16[1,512,128]{2,1,0:T(8,128)(2,1)S(1)} collective-permute-done((bf16[1,512,128]{2,1,0:T(8,128)(2,1)S(1)}, bf16[1,512,128]{2,1,0:T(8,128)(2,1)S(1)}, u32[]{:S(2)}, u32[]{:S(2)}) %collective-permute-start.7) | collective-permute-done | bytes 131104 | tf_op jit(solution)/shard_map/ppermute | solution.py:30
  73.5 3.5 %all-to-all-start = ((bf16[4,528,128]{2,1,0:T(8,128)(2,1)}), bf16[4,528,128]{2,1,0:T(8,128)(2,1)S(1)}, u32[]{:S(2)}, u32[]{:S(2)}) async-start(bf16[4,528,128]{2,1,0:T(8,128)(2,1)} %attend.5), calls=%async_computation | async-start | bytes 1081344 | tf_op jit(solution)/shard_map/all_to_all | solution.py:252
  77.0 1.9 %collective-permute-start.9 = (bf16[2,512,128]{2,1,0:T(8,128)(2,1)S(1)}, bf16[2,512,128]{2,1,0:T(8,128)(2,1)S(1)}, u32[]{:S(2)}, u32[]{:S(2)}) collective-permute-start(bf16[2,512,128]{2,1,0:T(8,128)(2,1)S(1)} %constant_dynamic-update-slice_fusion), channel_id=1, source_target_pairs={{0,128},{128,0},{1,129},{129,1},{2,130},{130,2},{3,131},{131,3},{4... | collective-permute-start | bytes 786440 | tf_op jit(solution)/shard_map/ppermute | solution.py:30
  79.0 7.4 %all-to-all-done.in_ref = bf16[4,528,128]{2,1,0:T(8,128)(2,1)S(1)} async-done(((bf16[4,528,128]{2,1,0:T(8,128)(2,1)}), bf16[4,528,128]{2,1,0:T(8,128)(2,1)S(1)}, u32[]{:S(2)}, u32[]{:S(2)}) %all-to-all-start) | async-done | bytes 540704 | tf_op jit(solution)/shard_map/all_to_all | solution.py:252
  86.3 0.2 shard_map.57.own_ref
  86.5 9.9 %collective-permute-start.8 = (bf16[128,512]{1,0:T(8,128)(2,1)S(1)}, bf16[128,512]{1,0:T(8,128)(2,1)S(1)}, u32[]{:S(2)}, u32[]{:S(2)}) collective-permute-start(bf16[128,512]{1,0:T(8,128)(2,1)S(1)} %shard_map.57.own_ref), channel_id=1, source_target_pairs={{0,4},{4,0},{1,5},{5,1},{2,6},{6,2},{3,7},{7,3},{8,12},{12,8},{9,1... | collective-permute-start | bytes 393224 | tf_op jit(solution)/shard_map/ppermute | solution.py:30
  96.5 0.0 collective-permute-done.9
  96.5 7.1 %collective-permute-start.10 = (bf16[4,512,128]{2,1,0:T(8,128)(2,1)S(1)}, bf16[4,512,128]{2,1,0:T(8,128)(2,1)S(1)}, u32[]{:S(2)}, u32[]{:S(2)}) collective-permute-start(bf16[4,512,128]{2,1,0:T(8,128)(2,1)S(1)} %constant_dynamic-update-slice_fusion.2), channel_id=1, source_target_pairs={{0,32},{32,0},{1,33},{33,1},{2,34},{34,2},{3,35},{35,3},{4,36},{36... | collective-permute-start | bytes 1572872 | tf_op jit(solution)/shard_map/ppermute | solution.py:30
  103.6 0.0 collective-permute-done.8.other_ref
  103.6 1.0 shard_map.58
  104.7 10.7 %collective-permute-done.10 = bf16[4,512,128]{2,1,0:T(8,128)(2,1)S(1)} collective-permute-done((bf16[4,512,128]{2,1,0:T(8,128)(2,1)S(1)}, bf16[4,512,128]{2,1,0:T(8,128)(2,1)S(1)}, u32[]{:S(2)}, u32[]{:S(2)}) %collective-permute-start.10) | collective-permute-done | bytes 524320 | tf_op jit(solution)/shard_map/ppermute | solution.py:30
  115.4 3.5 %all-to-all-start.1 = ((bf16[4,2,128,512]{3,2,1,0:T(8,128)(2,1)}), bf16[4,2,128,512]{3,2,1,0:T(8,128)(2,1)S(1)}, u32[]{:S(2)}, u32[]{:S(2)}) async-start(bf16[4,2,128,512]{3,2,1,0:T(8,128)(2,1)} %shard_map.58), calls=%async_computation.1 | async-start | bytes 2097152 | tf_op jit(solution)/shard_map/all_to_all | solution.py:272
  119.0 0.1 constant_dynamic-update-slice_fusion.4.near_ref
  119.1 3.0 %collective-permute-start.11 = (bf16[8,512,128]{2,1,0:T(8,128)(2,1)S(1)}, bf16[8,512,128]{2,1,0:T(8,128)(2,1)S(1)}, u32[]{:S(2)}, u32[]{:S(2)}) collective-permute-start(bf16[8,512,128]{2,1,0:T(8,128)(2,1)S(1)} %constant_dynamic-update-slice_fusion.4.near_ref), channel_id=1, source_target_pairs={{0,8},{8,0},{1,9},{9,1},{2,10},{10,2},{3,11},{11,3},{4,12},{12,4},... | collective-permute-start | bytes 3145736 | tf_op jit(solution)/shard_map/ppermute | solution.py:30
  122.1 2.3 %collective-permute-done.11.far_ref = bf16[8,512,128]{2,1,0:T(8,128)(2,1)S(1)} collective-permute-done((bf16[8,512,128]{2,1,0:T(8,128)(2,1)S(1)}, bf16[8,512,128]{2,1,0:T(8,128)(2,1)S(1)}, u32[]{:S(2)}, u32[]{:S(2)}) %collective-permute-start.11) | collective-permute-done | bytes 1048608 | tf_op jit(solution)/shard_map/ppermute | solution.py:30
  124.3 7.7 %all-to-all-done.1.pair_ref = bf16[4,2,128,512]{3,2,1,0:T(8,128)(2,1)S(1)} async-done(((bf16[4,2,128,512]{3,2,1,0:T(8,128)(2,1)}), bf16[4,2,128,512]{3,2,1,0:T(8,128)(2,1)S(1)}, u32[]{:S(2)}, u32[]{:S(2)}) %all-to-all-start.1) | async-done | bytes 1048608 | tf_op jit(solution)/shard_map/all_to_all | solution.py:272
  132.0 1.8 %shard_map.59 = bf16[16,128,256]{2,1,0:T(8,128)(2,1)S(1)} custom-call(s32[5]{0:T(128)S(1)} %stack.32.where, bf16[4,2,128,512]{3,2,1,0:T(8,128)(2,1)S(1)} %all-to-all-done.1.pair_ref, bf16[8,512,128]{2,1,0:T(8,128)(2,1)S(1)} %constant_dynamic-update-slice_fusion.4.near_ref, bf16[8,512,128]{2,1,0:T(8,128)(2,1)S(1)} %collective-permute-done.11.far_ref), custom_call_target="tpu_custom_call" | custom-call | tf_op jit(solution)/shard_map/pallas_call | solution.py:188
  133.8 21.5 %all_to_all.15.in_ref = bf16[16,128,256]{2,1,0:T(8,128)(2,1)S(1)} all-to-all(bf16[16,128,256]{2,1,0:T(8,128)(2,1)S(1)} %shard_map.59), channel_id=1, replica_groups=mesh['za'=2,'zc'=2,'zd'=2,'ya'=2,'yb'=2,'c'=2,'h'=2,'x'=4] {'zd','yb','x'}, dimensions={0} | all-to-all | bytes 2097152 | tf_op jit(solution)/shard_map/all_to_all | solution.py:274
  155.4 0.8 shard_map.60
  (9 shorter events, 0.2 us)
Async XLA Ops:
  0.0 10.5 %copy-start.1 = (bf16[128,512]{1,0:T(8,128)(2,1)S(1)}, bf16[128,512]{1,0:T(8,128)(2,1)}, u32[]{:S(2)}) copy-start(bf16[128,512]{1,0:T(8,128)(2,1)} %param.5) | copy-start | bytes 393220
  0.8 14.4 %collective-permute-start = (bf16[1,256,128]{2,1,0:T(8,128)(2,1)S(1)}, bf16[1,256,128]{2,1,0:T(8,128)(2,1)S(1)}, u32[]{:S(2)}, u32[]{:S(2)}) collective-permute-start(bf16[1,256,128]{2,1,0:T(8,128)(2,1)S(1)} %maximum_bitcast_fusion.refs_0_), channel_id=1, source_target_pairs={{0,256},{256,0},{1,257},{257,1},{2,258},{258,2},{3,259},{259,3},{4... | collective-permute-start | bytes 196616 | tf_op jit(solution)/shard_map/ppermute | solution.py:30
  10.5 9.7 %collective-permute-start.1 = (bf16[128,512]{1,0:T(8,128)(2,1)S(1)}, bf16[128,512]{1,0:T(8,128)(2,1)S(1)}, u32[]{:S(2)}, u32[]{:S(2)}) collective-permute-start(bf16[128,512]{1,0:T(8,128)(2,1)S(1)} %copy-done.1), channel_id=1, source_target_pairs={{0,16},{16,0},{1,17},{17,1},{2,18},{18,2},{3,19},{19,3},{4,20},{20... | collective-permute-start | bytes 393224 | tf_op jit(solution)/shard_map/ppermute | solution.py:30
  13.7 6.5 %collective-permute-start.2 = (bf16[512,128]{1,0:T(8,128)(2,1)}, bf16[512,128]{1,0:T(8,128)(2,1)S(1)}, u32[]{:S(2)}, u32[]{:S(2)}) collective-permute-start(bf16[512,128]{1,0:T(8,128)(2,1)} %param.8), channel_id=1, source_target_pairs={{0,0},{4,256},{32,64},{36,320},{64,32},{68,288},{96,96},{100,352},... | collective-permute-start | bytes 393224 | tf_op jit(solution)/shard_map/ppermute | solution.py:229
  15.3 13.7 %collective-permute-start.3 = (bf16[2,256,128]{2,1,0:T(8,128)(2,1)S(1)}, bf16[2,256,128]{2,1,0:T(8,128)(2,1)S(1)}, u32[]{:S(2)}, u32[]{:S(2)}) collective-permute-start(bf16[2,256,128]{2,1,0:T(8,128)(2,1)S(1)} %shard_map.55.refs_0_), channel_id=1, source_target_pairs={{0,128},{128,0},{1,129},{129,1},{2,130},{130,2},{3,131},{131,3},{4... | collective-permute-start | bytes 393224 | tf_op jit(solution)/shard_map/ppermute | solution.py:30
  20.2 12.8 %collective-permute-start.4 = (bf16[2,128,512]{2,1,0:T(8,128)(2,1)S(1)}, bf16[2,128,512]{2,1,0:T(8,128)(2,1)S(1)}, u32[]{:S(2)}, u32[]{:S(2)}) collective-permute-start(bf16[2,128,512]{2,1,0:T(8,128)(2,1)S(1)} %pad_maximum_fusion.1.refs_0_), channel_id=1, source_target_pairs={{0,32},{32,0},{1,33},{33,1},{2,34},{34,2},{3,35},{35,3},{4,36},{36... | collective-permute-start | bytes 786440 | tf_op jit(solution)/shard_map/ppermute | solution.py:30
  33.1 7.1 %collective-permute-start.5 = (bf16[4,256,128]{2,1,0:T(8,128)(2,1)S(1)}, bf16[4,256,128]{2,1,0:T(8,128)(2,1)S(1)}, u32[]{:S(2)}, u32[]{:S(2)}) collective-permute-start(bf16[4,256,128]{2,1,0:T(8,128)(2,1)S(1)} %shard_map.56.refs_2_), channel_id=1, source_target_pairs={{0,64},{64,0},{1,65},{65,1},{2,66},{66,2},{3,67},{67,3},{4,68},{68... | collective-permute-start | bytes 786440 | tf_op jit(solution)/shard_map/ppermute | solution.py:30
  35.7 0.7 copy-start
  40.2 24.5 %collective-permute-start.6 = (bf16[8,256,128]{2,1,0:T(8,128)(2,1)S(1)}, bf16[8,256,128]{2,1,0:T(8,128)(2,1)S(1)}, u32[]{:S(2)}, u32[]{:S(2)}) collective-permute-start(bf16[8,256,128]{2,1,0:T(8,128)(2,1)S(1)} %pad_maximum_fusion), channel_id=1, source_target_pairs={{0,8},{8,0},{1,9},{9,1},{2,10},{10,2},{3,11},{11,3},{4,12},{12,4},... | collective-permute-start | bytes 1572872 | tf_op jit(solution)/shard_map/ppermute | solution.py:30
  46.4 27.1 %collective-permute-start.7 = (bf16[1,512,128]{2,1,0:T(8,128)(2,1)S(1)}, bf16[1,512,128]{2,1,0:T(8,128)(2,1)S(1)}, u32[]{:S(2)}, u32[]{:S(2)}) collective-permute-start(bf16[1,512,128]{2,1,0:T(8,128)(2,1)S(1)} %bitcast.10), channel_id=1, source_target_pairs={{0,256},{256,0},{1,257},{257,1},{2,258},{258,2},{3,259},{259,3},{4... | collective-permute-start | bytes 393224 | tf_op jit(solution)/shard_map/ppermute | solution.py:30
  73.5 12.8 %all-to-all-start = ((bf16[4,528,128]{2,1,0:T(8,128)(2,1)}), bf16[4,528,128]{2,1,0:T(8,128)(2,1)S(1)}, u32[]{:S(2)}, u32[]{:S(2)}) async-start(bf16[4,528,128]{2,1,0:T(8,128)(2,1)} %attend.5), calls=%async_computation | async-start | bytes 1081344 | tf_op jit(solution)/shard_map/all_to_all | solution.py:252
  77.0 19.4 %collective-permute-start.9 = (bf16[2,512,128]{2,1,0:T(8,128)(2,1)S(1)}, bf16[2,512,128]{2,1,0:T(8,128)(2,1)S(1)}, u32[]{:S(2)}, u32[]{:S(2)}) collective-permute-start(bf16[2,512,128]{2,1,0:T(8,128)(2,1)S(1)} %constant_dynamic-update-slice_fusion), channel_id=1, source_target_pairs={{0,128},{128,0},{1,129},{129,1},{2,130},{130,2},{3,131},{131,3},{4... | collective-permute-start | bytes 786440 | tf_op jit(solution)/shard_map/ppermute | solution.py:30
  86.5 17.1 %collective-permute-start.8 = (bf16[128,512]{1,0:T(8,128)(2,1)S(1)}, bf16[128,512]{1,0:T(8,128)(2,1)S(1)}, u32[]{:S(2)}, u32[]{:S(2)}) collective-permute-start(bf16[128,512]{1,0:T(8,128)(2,1)S(1)} %shard_map.57.own_ref), channel_id=1, source_target_pairs={{0,4},{4,0},{1,5},{5,1},{2,6},{6,2},{3,7},{7,3},{8,12},{12,8},{9,1... | collective-permute-start | bytes 393224 | tf_op jit(solution)/shard_map/ppermute | solution.py:30
  96.5 18.9 %collective-permute-start.10 = (bf16[4,512,128]{2,1,0:T(8,128)(2,1)S(1)}, bf16[4,512,128]{2,1,0:T(8,128)(2,1)S(1)}, u32[]{:S(2)}, u32[]{:S(2)}) collective-permute-start(bf16[4,512,128]{2,1,0:T(8,128)(2,1)S(1)} %constant_dynamic-update-slice_fusion.2), channel_id=1, source_target_pairs={{0,32},{32,0},{1,33},{33,1},{2,34},{34,2},{3,35},{35,3},{4,36},{36... | collective-permute-start | bytes 1572872 | tf_op jit(solution)/shard_map/ppermute | solution.py:30
  115.4 16.6 %all-to-all-start.1 = ((bf16[4,2,128,512]{3,2,1,0:T(8,128)(2,1)}), bf16[4,2,128,512]{3,2,1,0:T(8,128)(2,1)S(1)}, u32[]{:S(2)}, u32[]{:S(2)}) async-start(bf16[4,2,128,512]{3,2,1,0:T(8,128)(2,1)} %shard_map.58), calls=%async_computation.1 | async-start | bytes 2097152 | tf_op jit(solution)/shard_map/all_to_all | solution.py:272
  119.1 5.3 %collective-permute-start.11 = (bf16[8,512,128]{2,1,0:T(8,128)(2,1)S(1)}, bf16[8,512,128]{2,1,0:T(8,128)(2,1)S(1)}, u32[]{:S(2)}, u32[]{:S(2)}) collective-permute-start(bf16[8,512,128]{2,1,0:T(8,128)(2,1)S(1)} %constant_dynamic-update-slice_fusion.4.near_ref), channel_id=1, source_target_pairs={{0,8},{8,0},{1,9},{9,1},{2,10},{10,2},{3,11},{11,3},{4,12},{12,4},... | collective-permute-start | bytes 3145736 | tf_op jit(solution)/shard_map/ppermute | solution.py:30

commit v6 on v5

--- a/solution.py
+++ b/solution.py
@@ -247,7 +247,7 @@
     far = swap(jnp.concatenate([kv, kv_in], axis=0), "c")
     acc, stat = attend(4, 0, False, False, where, block_order, q, kv_in, acc, stat)
     part = attend(0, 1, False, True, where, block_order, q, far, acc, stat)
-    part, w, w_in = together((part, w, w_in))
+    _, w, w_in = together((part, w, w_in))
 
     part = lax.all_to_all(part, Y, 0, 0, tiled=True)
     w = jnp.concatenate([w, w_in], axis=0)

time: 157 us -> 155 us (0.987)
  the two profiles are of different devices: /device:TPU:1 before, /device:TPU:384 now
where the time goes in v6:
time: 155 us; the launch traced here: 154 us
  starting transfers between devices  66 us (43%)
  waiting for transfers between devices  48.6 us (31%)
  blocking collectives  22.6 us (15%)
  Pallas kernels  14.7 us (9%)
    ppermute x11, starting transfers between devices, swap(): return lax.ppermute(value, axis, [(0, 1), (1, 0)])  56.6 us
    ppermute x11, waiting for transfers between devices, swap(): return lax.ppermute(value, axis, [(0, 1), (1, 0)])  37.3 us
    all_to_all x1, blocking collectives, local(): tiles = lax.all_to_all(tiles, TEAM + ('x',), 0, 0, tiled=True)  22.6 us
    pallas_call x3, Pallas kernels, attend(): pl.pallas_call(functools.partial(attend_kernel, count, near, side, first,...  10.8 us
    all_to_all x1, waiting for transfers between devices, local(): pair = lax.all_to_all(pair, TEAM, 0, 0, tiled=True)  8.54 us
    all_to_all x1, starting transfers between devices, local(): part = lax.all_to_all(part, Y, 0, 0, tiled=True)  4.35 us
    all_to_all x1, starting transfers between devices, local(): pair = lax.all_to_all(pair, TEAM, 0, 0, tiled=True)  3.52 us
  transfers between devices with their start and end apart: 14, of which 8 were waited for; matrix products, arithmetic and copies ran while one was open for 0% of the time, Pallas kernels for 8%

profile of v6, /device:TPU:384, one launch (start us, length us, event | category | flops | bytes accessed | tf_op | source)
XLA Modules:
  0.0 154.0 jit_solution(13509897146502454022)
XLA Ops:
  0.0 0.0 copy-start.1
  0.0 0.8 maximum_bitcast_fusion.refs_0_
  0.8 5.4 %collective-permute-start = (bf16[1,256,128]{2,1,0:T(8,128)(2,1)S(1)}, bf16[1,256,128]{2,1,0:T(8,128)(2,1)S(1)}, u32[]{:S(2)}, u32[]{:S(2)}) collective-permute-start(bf16[1,256,128]{2,1,0:T(8,128)(2,1)S(1)} %maximum_bitcast_fusion.refs_0_), channel_id=1, source_target_pairs={{0,256},{256,0},{1,257},{257,1},{2,258},{258,2},{3,259},{259,3},{4... | collective-permute-start | bytes 196616 | tf_op jit(solution)/shard_map/ppermute | solution.py:30
  6.3 0.0 copy-done.1
  6.3 3.5 %collective-permute-start.1 = (bf16[128,512]{1,0:T(8,128)(2,1)S(1)}, bf16[128,512]{1,0:T(8,128)(2,1)S(1)}, u32[]{:S(2)}, u32[]{:S(2)}) collective-permute-start(bf16[128,512]{1,0:T(8,128)(2,1)S(1)} %copy-done.1), channel_id=1, source_target_pairs={{0,16},{16,0},{1,17},{17,1},{2,18},{18,2},{3,19},{19,3},{4,20},{20... | collective-permute-start | bytes 393224 | tf_op jit(solution)/shard_map/ppermute | solution.py:30
  9.8 1.6 %collective-permute-start.2 = (bf16[512,128]{1,0:T(8,128)(2,1)}, bf16[512,128]{1,0:T(8,128)(2,1)S(1)}, u32[]{:S(2)}, u32[]{:S(2)}) collective-permute-start(bf16[512,128]{1,0:T(8,128)(2,1)} %param.8), channel_id=1, source_target_pairs={{0,0},{4,256},{32,64},{36,320},{64,32},{68,288},{96,96},{100,352},... | collective-permute-start | bytes 393224 | tf_op jit(solution)/shard_map/ppermute | solution.py:229
  11.3 0.5 collective-permute-done._.refs_1_
  11.9 4.9 %collective-permute-start.3 = (bf16[2,256,128]{2,1,0:T(8,128)(2,1)S(1)}, bf16[2,256,128]{2,1,0:T(8,128)(2,1)S(1)}, u32[]{:S(2)}, u32[]{:S(2)}) collective-permute-start(bf16[2,256,128]{2,1,0:T(8,128)(2,1)S(1)} %shard_map.55.refs_0_), channel_id=1, source_target_pairs={{0,128},{128,0},{1,129},{129,1},{2,130},{130,2},{3,131},{131,3},{4... | collective-permute-start | bytes 393224 | tf_op jit(solution)/shard_map/ppermute | solution.py:30
  16.8 0.0 collective-permute-done.1
  16.8 0.0 collective-permute-done.2
  16.8 9.8 %collective-permute-start.4 = (bf16[2,128,512]{2,1,0:T(8,128)(2,1)S(1)}, bf16[2,128,512]{2,1,0:T(8,128)(2,1)S(1)}, u32[]{:S(2)}, u32[]{:S(2)}) collective-permute-start(bf16[2,128,512]{2,1,0:T(8,128)(2,1)S(1)} %pad_maximum_fusion.1.refs_0_), channel_id=1, source_target_pairs={{0,32},{32,0},{1,33},{33,1},{2,34},{34,2},{3,35},{35,3},{4,36},{36... | collective-permute-start | bytes 786440 | tf_op jit(solution)/shard_map/ppermute | solution.py:30
  26.6 0.0 collective-permute-done.3._.refs_1_
  26.7 5.4 %collective-permute-done.4.refs_1_ = bf16[2,128,512]{2,1,0:T(8,128)(2,1)S(1)} collective-permute-done((bf16[2,128,512]{2,1,0:T(8,128)(2,1)S(1)}, bf16[2,128,512]{2,1,0:T(8,128)(2,1)S(1)}, u32[]{:S(2)}, u32[]{:S(2)}) %collective-permute-start.4) | collective-permute-done | bytes 262176 | tf_op jit(solution)/shard_map/ppermute | solution.py:30
  32.0 1.9 %collective-permute-start.5 = (bf16[4,256,128]{2,1,0:T(8,128)(2,1)S(1)}, bf16[4,256,128]{2,1,0:T(8,128)(2,1)S(1)}, u32[]{:S(2)}, u32[]{:S(2)}) collective-permute-start(bf16[4,256,128]{2,1,0:T(8,128)(2,1)S(1)} %shard_map.56.refs_2_), channel_id=1, source_target_pairs={{0,64},{64,0},{1,65},{65,1},{2,66},{66,2},{3,67},{67,3},{4,68},{68... | collective-permute-start | bytes 786440 | tf_op jit(solution)/shard_map/ppermute | solution.py:30
  33.9 0.0 copy-start
  34.0 0.1 stack.32.where
  34.0 0.6 copy-done
  34.6 2.7 %attend.3 = (f32[4,128,512]{2,1,0:T(8,128)S(1)}, f32[8,512]{1,0:T(8,128)S(1)}) custom-call(s32[5]{0:T(128)S(1)} %stack.32.where, s32[128]{0:T(128)S(1)} %copy-done, bf16[2,128,512]{2,1,0:T(8,128)(2,1)S(1)} %pad_maximum_fusion.1.refs_0_, bf16[2,128,512]{2,1,0:T(8,128)(2,1)S(1)} %collective-permute-done.4.refs_1_, bf16[4,256,128]{2,1,0:T(8,128)(2,1)S(1)} %shard_map.56.refs_2_), custom_call_target="tpu_custom_call" | custom-call | flops 536870912 | bytes 12582912 | tf_op jit(solution)/shard_map/attend/pallas_call | solution.py:166
  37.3 3.1 %collective-permute-done.5.refs_2_ = bf16[4,256,128]{2,1,0:T(8,128)(2,1)S(1)} collective-permute-done((bf16[4,256,128]{2,1,0:T(8,128)(2,1)S(1)}, bf16[4,256,128]{2,1,0:T(8,128)(2,1)S(1)}, u32[]{:S(2)}, u32[]{:S(2)}) %collective-permute-start.5) | collective-permute-done | bytes 262176 | tf_op jit(solution)/shard_map/ppermute | solution.py:30
  40.5 1.9 %collective-permute-start.6 = (bf16[8,256,128]{2,1,0:T(8,128)(2,1)S(1)}, bf16[8,256,128]{2,1,0:T(8,128)(2,1)S(1)}, u32[]{:S(2)}, u32[]{:S(2)}) collective-permute-start(bf16[8,256,128]{2,1,0:T(8,128)(2,1)S(1)} %pad_maximum_fusion), channel_id=1, source_target_pairs={{0,8},{8,0},{1,9},{9,1},{2,10},{10,2},{3,11},{11,3},{4,12},{12,4},... | collective-permute-start | bytes 1572872 | tf_op jit(solution)/shard_map/ppermute | solution.py:30
  42.4 9.8 %collective-permute-start.8 = (bf16[1,512,128]{2,1,0:T(8,128)(2,1)S(1)}, bf16[1,512,128]{2,1,0:T(8,128)(2,1)S(1)}, u32[]{:S(2)}, u32[]{:S(2)}) collective-permute-start(bf16[1,512,128]{2,1,0:T(8,128)(2,1)S(1)} %bitcast.10), channel_id=1, source_target_pairs={{0,256},{256,0},{1,257},{257,1},{2,258},{258,2},{3,259},{259,3},{4... | collective-permute-start | bytes 393224 | tf_op jit(solution)/shard_map/ppermute | solution.py:30
  52.2 2.8 %attend.4 = (f32[4,128,512]{2,1,0:T(8,128)S(1)}, f32[8,512]{1,0:T(8,128)S(1)}) custom-call(s32[5]{0:T(128)S(1)} %stack.32.where, s32[128]{0:T(128)S(1)} %copy-done, bf16[2,128,512]{2,1,0:T(8,128)(2,1)S(1)} %pad_maximum_fusion.1.refs_0_, bf16[2,128,512]{2,1,0:T(8,128)(2,1)S(1)} %collective-permute-done.4.refs_1_, ...), custom_call_target="tpu_custom_call" | custom-call | flops 536870912 | bytes 12582912 | tf_op jit(solution)/shard_map/attend/pallas_call | solution.py:166
  55.0 0.0 collective-permute-done.6.refs_2_
  55.0 5.3 %attend.5 = bf16[4,528,128]{2,1,0:T(8,128)(2,1)} custom-call(s32[5]{0:T(128)S(1)} %stack.32.where, s32[128]{0:T(128)S(1)} %copy-done, bf16[2,128,512]{2,1,0:T(8,128)(2,1)S(1)} %pad_maximum_fusion.1.refs_0_, bf16[2,128,512]{2,1,0:T(8,128)(2,1)S(1)} %collective-permute-done.4.refs_1_, bf16[8,256,128]{2,1,0:T(8,128)(2,1)S(1)} %collective-permute-done.6.refs_2_, ...), custom_call_target="tpu_custom_call" | custom-call | flops 1073741824 | bytes 12582912 | tf_op jit(solution)/shard_map/attend/pallas_call | solution.py:166
  60.4 4.3 %all-to-all-start = ((bf16[4,528,128]{2,1,0:T(8,128)(2,1)}), bf16[4,528,128]{2,1,0:T(8,128)(2,1)S(1)}, u32[]{:S(2)}, u32[]{:S(2)}) async-start(bf16[4,528,128]{2,1,0:T(8,128)(2,1)} %attend.5), calls=%async_computation | async-start | bytes 1081344 | tf_op jit(solution)/shard_map/all_to_all | solution.py:252
  64.7 0.0 collective-permute-done.8
  64.7 7.1 %collective-permute-start.9 = (bf16[2,512,128]{2,1,0:T(8,128)(2,1)S(1)}, bf16[2,512,128]{2,1,0:T(8,128)(2,1)S(1)}, u32[]{:S(2)}, u32[]{:S(2)}) collective-permute-start(bf16[2,512,128]{2,1,0:T(8,128)(2,1)S(1)} %constant_dynamic-update-slice_fusion), channel_id=1, source_target_pairs={{0,128},{128,0},{1,129},{129,1},{2,130},{130,2},{3,131},{131,3},{4... | collective-permute-start | bytes 786440 | tf_op jit(solution)/shard_map/ppermute | solution.py:30
  71.9 2.8 %all-to-all-done.in_ref = bf16[4,528,128]{2,1,0:T(8,128)(2,1)S(1)} async-done(((bf16[4,528,128]{2,1,0:T(8,128)(2,1)}), bf16[4,528,128]{2,1,0:T(8,128)(2,1)S(1)}, u32[]{:S(2)}, u32[]{:S(2)}) %all-to-all-start) | async-done | bytes 540704 | tf_op jit(solution)/shard_map/all_to_all | solution.py:252
  74.7 0.2 shard_map.57.own_ref
  74.9 4.6 %collective-permute-start.7 = (bf16[128,512]{1,0:T(8,128)(2,1)S(1)}, bf16[128,512]{1,0:T(8,128)(2,1)S(1)}, u32[]{:S(2)}, u32[]{:S(2)}) collective-permute-start(bf16[128,512]{1,0:T(8,128)(2,1)S(1)} %shard_map.57.own_ref), channel_id=1, source_target_pairs={{0,4},{4,0},{1,5},{5,1},{2,6},{6,2},{3,7},{7,3},{8,12},{12,8},{9,1... | collective-permute-start | bytes 393224 | tf_op jit(solution)/shard_map/ppermute | solution.py:30
  79.6 14.9 %collective-permute-done.9 = bf16[2,512,128]{2,1,0:T(8,128)(2,1)S(1)} collective-permute-done((bf16[2,512,128]{2,1,0:T(8,128)(2,1)S(1)}, bf16[2,512,128]{2,1,0:T(8,128)(2,1)S(1)}, u32[]{:S(2)}, u32[]{:S(2)}) %collective-permute-start.9) | collective-permute-done | bytes 262176 | tf_op jit(solution)/shard_map/ppermute | solution.py:30
  94.5 5.6 %collective-permute-start.10 = (bf16[4,512,128]{2,1,0:T(8,128)(2,1)S(1)}, bf16[4,512,128]{2,1,0:T(8,128)(2,1)S(1)}, u32[]{:S(2)}, u32[]{:S(2)}) collective-permute-start(bf16[4,512,128]{2,1,0:T(8,128)(2,1)S(1)} %constant_dynamic-update-slice_fusion.2), channel_id=1, source_target_pairs={{0,32},{32,0},{1,33},{33,1},{2,34},{34,2},{3,35},{35,3},{4,36},{36... | collective-permute-start | bytes 1572872 | tf_op jit(solution)/shard_map/ppermute | solution.py:30
  100.1 0.0 collective-permute-done.7.other_ref
  100.2 1.0 shard_map.58
  101.2 10.8 %collective-permute-done.10 = bf16[4,512,128]{2,1,0:T(8,128)(2,1)S(1)} collective-permute-done((bf16[4,512,128]{2,1,0:T(8,128)(2,1)S(1)}, bf16[4,512,128]{2,1,0:T(8,128)(2,1)S(1)}, u32[]{:S(2)}, u32[]{:S(2)}) %collective-permute-start.10) | collective-permute-done | bytes 524320 | tf_op jit(solution)/shard_map/ppermute | solution.py:30
  112.0 3.5 %all-to-all-start.1 = ((bf16[4,2,128,512]{3,2,1,0:T(8,128)(2,1)}), bf16[4,2,128,512]{3,2,1,0:T(8,128)(2,1)S(1)}, u32[]{:S(2)}, u32[]{:S(2)}) async-start(bf16[4,2,128,512]{3,2,1,0:T(8,128)(2,1)} %shard_map.58), calls=%async_computation.1 | async-start | bytes 2097152 | tf_op jit(solution)/shard_map/all_to_all | solution.py:272
  115.5 0.1 constant_dynamic-update-slice_fusion.4.near_ref
  115.6 1.9 %collective-permute-start.11 = (bf16[8,512,128]{2,1,0:T(8,128)(2,1)S(1)}, bf16[8,512,128]{2,1,0:T(8,128)(2,1)S(1)}, u32[]{:S(2)}, u32[]{:S(2)}) collective-permute-start(bf16[8,512,128]{2,1,0:T(8,128)(2,1)S(1)} %constant_dynamic-update-slice_fusion.4.near_ref), channel_id=1, source_target_pairs={{0,8},{8,0},{1,9},{9,1},{2,10},{10,2},{3,11},{11,3},{4,12},{12,4},... | collective-permute-start | bytes 3145736 | tf_op jit(solution)/shard_map/ppermute | solution.py:30
  117.5 2.6 %collective-permute-done.11.far_ref = bf16[8,512,128]{2,1,0:T(8,128)(2,1)S(1)} collective-permute-done((bf16[8,512,128]{2,1,0:T(8,128)(2,1)S(1)}, bf16[8,512,128]{2,1,0:T(8,128)(2,1)S(1)}, u32[]{:S(2)}, u32[]{:S(2)}) %collective-permute-start.11) | collective-permute-done | bytes 1048608 | tf_op jit(solution)/shard_map/ppermute | solution.py:30
  120.2 8.5 %all-to-all-done.1.pair_ref = bf16[4,2,128,512]{3,2,1,0:T(8,128)(2,1)S(1)} async-done(((bf16[4,2,128,512]{3,2,1,0:T(8,128)(2,1)}), bf16[4,2,128,512]{3,2,1,0:T(8,128)(2,1)S(1)}, u32[]{:S(2)}, u32[]{:S(2)}) %all-to-all-start.1) | async-done | bytes 1048608 | tf_op jit(solution)/shard_map/all_to_all | solution.py:272
  128.7 1.8 %shard_map.59 = bf16[16,128,256]{2,1,0:T(8,128)(2,1)S(1)} custom-call(s32[5]{0:T(128)S(1)} %stack.32.where, bf16[4,2,128,512]{3,2,1,0:T(8,128)(2,1)S(1)} %all-to-all-done.1.pair_ref, bf16[8,512,128]{2,1,0:T(8,128)(2,1)S(1)} %constant_dynamic-update-slice_fusion.4.near_ref, bf16[8,512,128]{2,1,0:T(8,128)(2,1)S(1)} %collective-permute-done.11.far_ref), custom_call_target="tpu_custom_call" | custom-call | tf_op jit(solution)/shard_map/pallas_call | solution.py:188
  130.5 22.6 %all_to_all.15.in_ref = bf16[16,128,256]{2,1,0:T(8,128)(2,1)S(1)} all-to-all(bf16[16,128,256]{2,1,0:T(8,128)(2,1)S(1)} %shard_map.59), channel_id=1, replica_groups=mesh['za'=2,'zc'=2,'zd'=2,'ya'=2,'yb'=2,'c'=2,'h'=2,'x'=4] {'zd','yb','x'}, dimensions={0} | all-to-all | bytes 2097152 | tf_op jit(solution)/shard_map/all_to_all | solution.py:274
  153.2 0.8 shard_map.60
  (9 shorter events, 0.2 us)
Async XLA Ops:
  0.0 6.3 %copy-start.1 = (bf16[128,512]{1,0:T(8,128)(2,1)S(1)}, bf16[128,512]{1,0:T(8,128)(2,1)}, u32[]{:S(2)}) copy-start(bf16[128,512]{1,0:T(8,128)(2,1)} %param.5) | copy-start | bytes 393220
  0.8 11.0 %collective-permute-start = (bf16[1,256,128]{2,1,0:T(8,128)(2,1)S(1)}, bf16[1,256,128]{2,1,0:T(8,128)(2,1)S(1)}, u32[]{:S(2)}, u32[]{:S(2)}) collective-permute-start(bf16[1,256,128]{2,1,0:T(8,128)(2,1)S(1)} %maximum_bitcast_fusion.refs_0_), channel_id=1, source_target_pairs={{0,256},{256,0},{1,257},{257,1},{2,258},{258,2},{3,259},{259,3},{4... | collective-permute-start | bytes 196616 | tf_op jit(solution)/shard_map/ppermute | solution.py:30
  6.3 10.5 %collective-permute-start.1 = (bf16[128,512]{1,0:T(8,128)(2,1)S(1)}, bf16[128,512]{1,0:T(8,128)(2,1)S(1)}, u32[]{:S(2)}, u32[]{:S(2)}) collective-permute-start(bf16[128,512]{1,0:T(8,128)(2,1)S(1)} %copy-done.1), channel_id=1, source_target_pairs={{0,16},{16,0},{1,17},{17,1},{2,18},{18,2},{3,19},{19,3},{4,20},{20... | collective-permute-start | bytes 393224 | tf_op jit(solution)/shard_map/ppermute | solution.py:30
  9.8 7.0 %collective-permute-start.2 = (bf16[512,128]{1,0:T(8,128)(2,1)}, bf16[512,128]{1,0:T(8,128)(2,1)S(1)}, u32[]{:S(2)}, u32[]{:S(2)}) collective-permute-start(bf16[512,128]{1,0:T(8,128)(2,1)} %param.8), channel_id=1, source_target_pairs={{0,0},{4,256},{32,64},{36,320},{64,32},{68,288},{96,96},{100,352},... | collective-permute-start | bytes 393224 | tf_op jit(solution)/shard_map/ppermute | solution.py:229
  11.9 14.8 %collective-permute-start.3 = (bf16[2,256,128]{2,1,0:T(8,128)(2,1)S(1)}, bf16[2,256,128]{2,1,0:T(8,128)(2,1)S(1)}, u32[]{:S(2)}, u32[]{:S(2)}) collective-permute-start(bf16[2,256,128]{2,1,0:T(8,128)(2,1)S(1)} %shard_map.55.refs_0_), channel_id=1, source_target_pairs={{0,128},{128,0},{1,129},{129,1},{2,130},{130,2},{3,131},{131,3},{4... | collective-permute-start | bytes 393224 | tf_op jit(solution)/shard_map/ppermute | solution.py:30
  16.8 15.2 %collective-permute-start.4 = (bf16[2,128,512]{2,1,0:T(8,128)(2,1)S(1)}, bf16[2,128,512]{2,1,0:T(8,128)(2,1)S(1)}, u32[]{:S(2)}, u32[]{:S(2)}) collective-permute-start(bf16[2,128,512]{2,1,0:T(8,128)(2,1)S(1)} %pad_maximum_fusion.1.refs_0_), channel_id=1, source_target_pairs={{0,32},{32,0},{1,33},{33,1},{2,34},{34,2},{3,35},{35,3},{4,36},{36... | collective-permute-start | bytes 786440 | tf_op jit(solution)/shard_map/ppermute | solution.py:30
  32.0 8.4 %collective-permute-start.5 = (bf16[4,256,128]{2,1,0:T(8,128)(2,1)S(1)}, bf16[4,256,128]{2,1,0:T(8,128)(2,1)S(1)}, u32[]{:S(2)}, u32[]{:S(2)}) collective-permute-start(bf16[4,256,128]{2,1,0:T(8,128)(2,1)S(1)} %shard_map.56.refs_2_), channel_id=1, source_target_pairs={{0,64},{64,0},{1,65},{65,1},{2,66},{66,2},{3,67},{67,3},{4,68},{68... | collective-permute-start | bytes 786440 | tf_op jit(solution)/shard_map/ppermute | solution.py:30
  33.9 0.7 copy-start
  40.5 14.5 %collective-permute-start.6 = (bf16[8,256,128]{2,1,0:T(8,128)(2,1)S(1)}, bf16[8,256,128]{2,1,0:T(8,128)(2,1)S(1)}, u32[]{:S(2)}, u32[]{:S(2)}) collective-permute-start(bf16[8,256,128]{2,1,0:T(8,128)(2,1)S(1)} %pad_maximum_fusion), channel_id=1, source_target_pairs={{0,8},{8,0},{1,9},{9,1},{2,10},{10,2},{3,11},{11,3},{4,12},{12,4},... | collective-permute-start | bytes 1572872 | tf_op jit(solution)/shard_map/ppermute | solution.py:30
  42.4 22.3 %collective-permute-start.8 = (bf16[1,512,128]{2,1,0:T(8,128)(2,1)S(1)}, bf16[1,512,128]{2,1,0:T(8,128)(2,1)S(1)}, u32[]{:S(2)}, u32[]{:S(2)}) collective-permute-start(bf16[1,512,128]{2,1,0:T(8,128)(2,1)S(1)} %bitcast.10), channel_id=1, source_target_pairs={{0,256},{256,0},{1,257},{257,1},{2,258},{258,2},{3,259},{259,3},{4... | collective-permute-start | bytes 393224 | tf_op jit(solution)/shard_map/ppermute | solution.py:30
  60.4 14.4 %all-to-all-start = ((bf16[4,528,128]{2,1,0:T(8,128)(2,1)}), bf16[4,528,128]{2,1,0:T(8,128)(2,1)S(1)}, u32[]{:S(2)}, u32[]{:S(2)}) async-start(bf16[4,528,128]{2,1,0:T(8,128)(2,1)} %attend.5), calls=%async_computation | async-start | bytes 1081344 | tf_op jit(solution)/shard_map/all_to_all | solution.py:252
  64.7 29.7 %collective-permute-start.9 = (bf16[2,512,128]{2,1,0:T(8,128)(2,1)S(1)}, bf16[2,512,128]{2,1,0:T(8,128)(2,1)S(1)}, u32[]{:S(2)}, u32[]{:S(2)}) collective-permute-start(bf16[2,512,128]{2,1,0:T(8,128)(2,1)S(1)} %constant_dynamic-update-slice_fusion), channel_id=1, source_target_pairs={{0,128},{128,0},{1,129},{129,1},{2,130},{130,2},{3,131},{131,3},{4... | collective-permute-start | bytes 786440 | tf_op jit(solution)/shard_map/ppermute | solution.py:30
  74.9 25.2 %collective-permute-start.7 = (bf16[128,512]{1,0:T(8,128)(2,1)S(1)}, bf16[128,512]{1,0:T(8,128)(2,1)S(1)}, u32[]{:S(2)}, u32[]{:S(2)}) collective-permute-start(bf16[128,512]{1,0:T(8,128)(2,1)S(1)} %shard_map.57.own_ref), channel_id=1, source_target_pairs={{0,4},{4,0},{1,5},{5,1},{2,6},{6,2},{3,7},{7,3},{8,12},{12,8},{9,1... | collective-permute-start | bytes 393224 | tf_op jit(solution)/shard_map/ppermute | solution.py:30
  94.5 17.4 %collective-permute-start.10 = (bf16[4,512,128]{2,1,0:T(8,128)(2,1)S(1)}, bf16[4,512,128]{2,1,0:T(8,128)(2,1)S(1)}, u32[]{:S(2)}, u32[]{:S(2)}) collective-permute-start(bf16[4,512,128]{2,1,0:T(8,128)(2,1)S(1)} %constant_dynamic-update-slice_fusion.2), channel_id=1, source_target_pairs={{0,32},{32,0},{1,33},{33,1},{2,34},{34,2},{3,35},{35,3},{4,36},{36... | collective-permute-start | bytes 1572872 | tf_op jit(solution)/shard_map/ppermute | solution.py:30
  112.0 16.7 %all-to-all-start.1 = ((bf16[4,2,128,512]{3,2,1,0:T(8,128)(2,1)}), bf16[4,2,128,512]{3,2,1,0:T(8,128)(2,1)S(1)}, u32[]{:S(2)}, u32[]{:S(2)}) async-start(bf16[4,2,128,512]{3,2,1,0:T(8,128)(2,1)} %shard_map.58), calls=%async_computation.1 | async-start | bytes 2097152 | tf_op jit(solution)/shard_map/all_to_all | solution.py:272
  115.6 4.6 %collective-permute-start.11 = (bf16[8,512,128]{2,1,0:T(8,128)(2,1)S(1)}, bf16[8,512,128]{2,1,0:T(8,128)(2,1)S(1)}, u32[]{:S(2)}, u32[]{:S(2)}) collective-permute-start(bf16[8,512,128]{2,1,0:T(8,128)(2,1)S(1)} %constant_dynamic-update-slice_fusion.4.near_ref), channel_id=1, source_target_pairs={{0,8},{8,0},{1,9},{9,1},{2,10},{10,2},{3,11},{11,3},{4,12},{12,4},... | collective-permute-start | bytes 3145736 | tf_op jit(solution)/shard_map/ppermute | solution.py:30

commit v7 on v6

--- a/solution.py
+++ b/solution.py
@@ -265,7 +265,7 @@
         compiler_params=PARAMS,
         cost_estimate=COST,
     )(attended, other)
-    pair, w, w_in = together((pair, w, w_in))
+    _, w, w_in = together((pair, w, w_in))
 
     w = jnp.concatenate([w, w_in], axis=0)
     w_far = swap(w, "c")

time: 155 us -> 183 us (1.18)
  the two profiles are of different devices: /device:TPU:384 before, /device:TPU:1 now
where the time goes in v7:
time: 183 us; the launch traced here: 182 us
  starting transfers between devices  83.7 us (46%)
  waiting for transfers between devices  44.8 us (24%)
  blocking collectives  38 us (21%)
  Pallas kernels  14 us (8%)
    ppermute x11, starting transfers between devices, swap(): return lax.ppermute(value, axis, [(0, 1), (1, 0)])  78.6 us
    ppermute x11, waiting for transfers between devices, swap(): return lax.ppermute(value, axis, [(0, 1), (1, 0)])  44.8 us
    all_to_all x1, blocking collectives, local(): tiles = lax.all_to_all(tiles, TEAM + ('x',), 0, 0, tiled=True)  24.5 us
    all_to_all x1, blocking collectives, local(): part = lax.all_to_all(part, Y, 0, 0, tiled=True)  13.5 us
    pallas_call x3, Pallas kernels, attend(): pl.pallas_call(functools.partial(attend_kernel, count, near, side, first,...  10 us
  transfers between devices with their start and end apart: 13, of which 7 were waited for; matrix products, arithmetic and copies ran while one was open for 0% of the time, Pallas kernels for 3%

profile of v7, /device:TPU:1, one launch (start us, length us, event | category | flops | bytes accessed | tf_op | source)
XLA Modules:
  0.0 182.4 jit_solution(7131499667596913735)
XLA Ops:
  0.0 0.0 copy-start.1
  0.0 0.8 maximum_bitcast_fusion.refs_0_
  0.8 9.6 %collective-permute-start = (bf16[1,256,128]{2,1,0:T(8,128)(2,1)S(1)}, bf16[1,256,128]{2,1,0:T(8,128)(2,1)S(1)}, u32[]{:S(2)}, u32[]{:S(2)}) collective-permute-start(bf16[1,256,128]{2,1,0:T(8,128)(2,1)S(1)} %maximum_bitcast_fusion.refs_0_), channel_id=1, source_target_pairs={{0,256},{256,0},{1,257},{257,1},{2,258},{258,2},{3,259},{259,3},{4... | collective-permute-start | bytes 196616 | tf_op jit(solution)/shard_map/ppermute | solution.py:30
  10.5 0.0 copy-done.1
  10.5 3.2 %collective-permute-start.1 = (bf16[128,512]{1,0:T(8,128)(2,1)S(1)}, bf16[128,512]{1,0:T(8,128)(2,1)S(1)}, u32[]{:S(2)}, u32[]{:S(2)}) collective-permute-start(bf16[128,512]{1,0:T(8,128)(2,1)S(1)} %copy-done.1), channel_id=1, source_target_pairs={{0,16},{16,0},{1,17},{17,1},{2,18},{18,2},{3,19},{19,3},{4,20},{20... | collective-permute-start | bytes 393224 | tf_op jit(solution)/shard_map/ppermute | solution.py:30
  13.7 1.6 collective-permute-start.2
  15.2 0.0 collective-permute-done._.refs_1_
  15.3 4.9 %collective-permute-start.3 = (bf16[2,256,128]{2,1,0:T(8,128)(2,1)S(1)}, bf16[2,256,128]{2,1,0:T(8,128)(2,1)S(1)}, u32[]{:S(2)}, u32[]{:S(2)}) collective-permute-start(bf16[2,256,128]{2,1,0:T(8,128)(2,1)S(1)} %shard_map.55.refs_0_), channel_id=1, source_target_pairs={{0,128},{128,0},{1,129},{129,1},{2,130},{130,2},{3,131},{131,3},{4... | collective-permute-start | bytes 393224 | tf_op jit(solution)/shard_map/ppermute | solution.py:30
  20.2 0.0 collective-permute-done.1
  20.2 0.0 collective-permute-done.2
  20.2 8.7 %collective-permute-start.4 = (bf16[2,128,512]{2,1,0:T(8,128)(2,1)S(1)}, bf16[2,128,512]{2,1,0:T(8,128)(2,1)S(1)}, u32[]{:S(2)}, u32[]{:S(2)}) collective-permute-start(bf16[2,128,512]{2,1,0:T(8,128)(2,1)S(1)} %pad_maximum_fusion.1.refs_0_), channel_id=1, source_target_pairs={{0,32},{32,0},{1,33},{33,1},{2,34},{34,2},{3,35},{35,3},{4,36},{36... | collective-permute-start | bytes 786440 | tf_op jit(solution)/shard_map/ppermute | solution.py:30
  28.9 0.0 collective-permute-done.3._.refs_1_
  29.0 4.1 %collective-permute-done.4.refs_1_ = bf16[2,128,512]{2,1,0:T(8,128)(2,1)S(1)} collective-permute-done((bf16[2,128,512]{2,1,0:T(8,128)(2,1)S(1)}, bf16[2,128,512]{2,1,0:T(8,128)(2,1)S(1)}, u32[]{:S(2)}, u32[]{:S(2)}) %collective-permute-start.4) | collective-permute-done | bytes 262176 | tf_op jit(solution)/shard_map/ppermute | solution.py:30
  33.1 2.6 %collective-permute-start.5 = (bf16[4,256,128]{2,1,0:T(8,128)(2,1)S(1)}, bf16[4,256,128]{2,1,0:T(8,128)(2,1)S(1)}, u32[]{:S(2)}, u32[]{:S(2)}) collective-permute-start(bf16[4,256,128]{2,1,0:T(8,128)(2,1)S(1)} %shard_map.56.refs_2_), channel_id=1, source_target_pairs={{0,64},{64,0},{1,65},{65,1},{2,66},{66,2},{3,67},{67,3},{4,68},{68... | collective-permute-start | bytes 786440 | tf_op jit(solution)/shard_map/ppermute | solution.py:30
  35.7 0.0 copy-start
  35.7 0.1 stack.32.where
  35.8 0.6 copy-done
  36.4 2.7 %attend.3 = (f32[4,128,512]{2,1,0:T(8,128)S(1)}, f32[8,512]{1,0:T(8,128)S(1)}) custom-call(s32[5]{0:T(128)S(1)} %stack.32.where, s32[128]{0:T(128)S(1)} %copy-done, bf16[2,128,512]{2,1,0:T(8,128)(2,1)S(1)} %pad_maximum_fusion.1.refs_0_, bf16[2,128,512]{2,1,0:T(8,128)(2,1)S(1)} %collective-permute-done.4.refs_1_, bf16[4,256,128]{2,1,0:T(8,128)(2,1)S(1)} %shard_map.56.refs_2_), custom_call_target="tpu_custom_call" | custom-call | flops 536870912 | bytes 12582912 | tf_op jit(solution)/shard_map/attend/pallas_call | solution.py:166
  39.1 1.1 collective-permute-done.5.refs_2_
  40.2 6.2 %collective-permute-start.6 = (bf16[8,256,128]{2,1,0:T(8,128)(2,1)S(1)}, bf16[8,256,128]{2,1,0:T(8,128)(2,1)S(1)}, u32[]{:S(2)}, u32[]{:S(2)}) collective-permute-start(bf16[8,256,128]{2,1,0:T(8,128)(2,1)S(1)} %pad_maximum_fusion), channel_id=1, source_target_pairs={{0,8},{8,0},{1,9},{9,1},{2,10},{10,2},{3,11},{11,3},{4,12},{12,4},... | collective-permute-start | bytes 1572872 | tf_op jit(solution)/shard_map/ppermute | solution.py:30
  46.4 2.8 %attend.4 = (f32[4,128,512]{2,1,0:T(8,128)S(1)}, f32[8,512]{1,0:T(8,128)S(1)}) custom-call(s32[5]{0:T(128)S(1)} %stack.32.where, s32[128]{0:T(128)S(1)} %copy-done, bf16[2,128,512]{2,1,0:T(8,128)(2,1)S(1)} %pad_maximum_fusion.1.refs_0_, bf16[2,128,512]{2,1,0:T(8,128)(2,1)S(1)} %collective-permute-done.4.refs_1_, ...), custom_call_target="tpu_custom_call" | custom-call | flops 536870912 | bytes 12582912 | tf_op jit(solution)/shard_map/attend/pallas_call | solution.py:166
  49.2 0.0 collective-permute-done.6.refs_2_
  49.2 4.5 %attend.5 = bf16[4,528,128]{2,1,0:T(8,128)(2,1)S(1)} custom-call(s32[5]{0:T(128)S(1)} %stack.32.where, s32[128]{0:T(128)S(1)} %copy-done, bf16[2,128,512]{2,1,0:T(8,128)(2,1)S(1)} %pad_maximum_fusion.1.refs_0_, bf16[2,128,512]{2,1,0:T(8,128)(2,1)S(1)} %collective-permute-done.4.refs_1_, bf16[8,256,128]{2,1,0:T(8,128)(2,1)S(1)} %collective-permute-done.6.refs_2_, ...), custom_call_target="tpu_custom_call" | custom-call | flops 1073741824 | bytes 12582912 | tf_op jit(solution)/shard_map/attend/pallas_call | solution.py:166
  53.8 13.5 %all_to_all.15.in_ref = bf16[4,528,128]{2,1,0:T(8,128)(2,1)S(1)} all-to-all(bf16[4,528,128]{2,1,0:T(8,128)(2,1)S(1)} %attend.5), channel_id=1, replica_groups=mesh['za'=2,'zc'=2,'zd'=2,'ya'=2,'yb'=2,'c'=2,'h'=2,'x'=4] {'ya','yb'}, dimensions={0} | all-to-all | bytes 1081344 | tf_op jit(solution)/shard_map/all_to_all | solution.py:252
  67.3 0.2 shard_map.57.own_ref
  67.5 17.0 %collective-permute-start.7 = (bf16[128,512]{1,0:T(8,128)(2,1)S(1)}, bf16[128,512]{1,0:T(8,128)(2,1)S(1)}, u32[]{:S(2)}, u32[]{:S(2)}) collective-permute-start(bf16[128,512]{1,0:T(8,128)(2,1)S(1)} %shard_map.57.own_ref), channel_id=1, source_target_pairs={{0,4},{4,0},{1,5},{5,1},{2,6},{6,2},{3,7},{7,3},{8,12},{12,8},{9,1... | collective-permute-start | bytes 393224 | tf_op jit(solution)/shard_map/ppermute | solution.py:30
  84.5 8.7 %collective-permute-done.7.other_ref = bf16[128,512]{1,0:T(8,128)(2,1)S(1)} collective-permute-done((bf16[128,512]{1,0:T(8,128)(2,1)S(1)}, bf16[128,512]{1,0:T(8,128)(2,1)S(1)}, u32[]{:S(2)}, u32[]{:S(2)}) %collective-permute-start.7) | collective-permute-done | bytes 131104 | tf_op jit(solution)/shard_map/ppermute | solution.py:30
  93.2 1.1 shard_map.58
  94.2 3.5 %all-to-all-start.1 = ((bf16[4,2,128,512]{3,2,1,0:T(8,128)(2,1)}), bf16[4,2,128,512]{3,2,1,0:T(8,128)(2,1)S(1)}, u32[]{:S(2)}, u32[]{:S(2)}) async-start(bf16[4,2,128,512]{3,2,1,0:T(8,128)(2,1)} %shard_map.58), calls=%async_computation.1 | async-start | bytes 2097152 | tf_op jit(solution)/shard_map/all_to_all | solution.py:272
  97.8 10.5 %collective-permute-start.8 = (bf16[1,512,128]{2,1,0:T(8,128)(2,1)S(1)}, bf16[1,512,128]{2,1,0:T(8,128)(2,1)S(1)}, u32[]{:S(2)}, u32[]{:S(2)}) collective-permute-start(bf16[1,512,128]{2,1,0:T(8,128)(2,1)S(1)} %bitcast.10), channel_id=1, source_target_pairs={{0,256},{256,0},{1,257},{257,1},{2,258},{258,2},{3,259},{259,3},{4... | collective-permute-start | bytes 393224 | tf_op jit(solution)/shard_map/ppermute | solution.py:30
  108.3 7.0 %collective-permute-done.8 = bf16[1,512,128]{2,1,0:T(8,128)(2,1)S(1)} collective-permute-done((bf16[1,512,128]{2,1,0:T(8,128)(2,1)S(1)}, bf16[1,512,128]{2,1,0:T(8,128)(2,1)S(1)}, u32[]{:S(2)}, u32[]{:S(2)}) %collective-permute-start.8) | collective-permute-done | bytes 131104 | tf_op jit(solution)/shard_map/ppermute | solution.py:30
  115.3 8.9 %collective-permute-start.9 = (bf16[2,512,128]{2,1,0:T(8,128)(2,1)S(1)}, bf16[2,512,128]{2,1,0:T(8,128)(2,1)S(1)}, u32[]{:S(2)}, u32[]{:S(2)}) collective-permute-start(bf16[2,512,128]{2,1,0:T(8,128)(2,1)S(1)} %constant_dynamic-update-slice_fusion), channel_id=1, source_target_pairs={{0,128},{128,0},{1,129},{129,1},{2,130},{130,2},{3,131},{131,3},{4... | collective-permute-start | bytes 786440 | tf_op jit(solution)/shard_map/ppermute | solution.py:30
  124.3 8.9 %collective-permute-done.9 = bf16[2,512,128]{2,1,0:T(8,128)(2,1)S(1)} collective-permute-done((bf16[2,512,128]{2,1,0:T(8,128)(2,1)S(1)}, bf16[2,512,128]{2,1,0:T(8,128)(2,1)S(1)}, u32[]{:S(2)}, u32[]{:S(2)}) %collective-permute-start.9) | collective-permute-done | bytes 262176 | tf_op jit(solution)/shard_map/ppermute | solution.py:30
  133.2 2.8 %collective-permute-start.10 = (bf16[4,512,128]{2,1,0:T(8,128)(2,1)S(1)}, bf16[4,512,128]{2,1,0:T(8,128)(2,1)S(1)}, u32[]{:S(2)}, u32[]{:S(2)}) collective-permute-start(bf16[4,512,128]{2,1,0:T(8,128)(2,1)S(1)} %constant_dynamic-update-slice_fusion.2), channel_id=1, source_target_pairs={{0,32},{32,0},{1,33},{33,1},{2,34},{34,2},{3,35},{35,3},{4,36},{36... | collective-permute-start | bytes 1572872 | tf_op jit(solution)/shard_map/ppermute | solution.py:30
  136.0 12.8 %collective-permute-done.10 = bf16[4,512,128]{2,1,0:T(8,128)(2,1)S(1)} collective-permute-done((bf16[4,512,128]{2,1,0:T(8,128)(2,1)S(1)}, bf16[4,512,128]{2,1,0:T(8,128)(2,1)S(1)}, u32[]{:S(2)}, u32[]{:S(2)}) %collective-permute-start.10) | collective-permute-done | bytes 524320 | tf_op jit(solution)/shard_map/ppermute | solution.py:30
  148.8 0.1 constant_dynamic-update-slice_fusion.4.near_ref
  148.9 4.0 %collective-permute-start.11 = (bf16[8,512,128]{2,1,0:T(8,128)(2,1)S(1)}, bf16[8,512,128]{2,1,0:T(8,128)(2,1)S(1)}, u32[]{:S(2)}, u32[]{:S(2)}) collective-permute-start(bf16[8,512,128]{2,1,0:T(8,128)(2,1)S(1)} %constant_dynamic-update-slice_fusion.4.near_ref), channel_id=1, source_target_pairs={{0,8},{8,0},{1,9},{9,1},{2,10},{10,2},{3,11},{11,3},{4,12},{12,4},... | collective-permute-start | bytes 3145736 | tf_op jit(solution)/shard_map/ppermute | solution.py:30
  153.0 2.3 %collective-permute-done.11.far_ref = bf16[8,512,128]{2,1,0:T(8,128)(2,1)S(1)} collective-permute-done((bf16[8,512,128]{2,1,0:T(8,128)(2,1)S(1)}, bf16[8,512,128]{2,1,0:T(8,128)(2,1)S(1)}, u32[]{:S(2)}, u32[]{:S(2)}) %collective-permute-start.11) | collective-permute-done | bytes 1048608 | tf_op jit(solution)/shard_map/ppermute | solution.py:30
  155.2 0.0 all-to-all-done.1.pair_ref
  155.2 1.8 %shard_map.59 = bf16[16,128,256]{2,1,0:T(8,128)(2,1)S(1)} custom-call(s32[5]{0:T(128)S(1)} %stack.32.where, bf16[4,2,128,512]{3,2,1,0:T(8,128)(2,1)S(1)} %all-to-all-done.1.pair_ref, bf16[8,512,128]{2,1,0:T(8,128)(2,1)S(1)} %constant_dynamic-update-slice_fusion.4.near_ref, bf16[8,512,128]{2,1,0:T(8,128)(2,1)S(1)} %collective-permute-done.11.far_ref), custom_call_target="tpu_custom_call" | custom-call | tf_op jit(solution)/shard_map/pallas_call | solution.py:188
  157.1 24.5 %all_to_all.16.in_ref = bf16[16,128,256]{2,1,0:T(8,128)(2,1)S(1)} all-to-all(bf16[16,128,256]{2,1,0:T(8,128)(2,1)S(1)} %shard_map.59), channel_id=1, replica_groups=mesh['za'=2,'zc'=2,'zd'=2,'ya'=2,'yb'=2,'c'=2,'h'=2,'x'=4] {'zd','yb','x'}, dimensions={0} | all-to-all | bytes 2097152 | tf_op jit(solution)/shard_map/all_to_all | solution.py:274
  181.6 0.8 shard_map.60
  (9 shorter events, 0.2 us)
Async XLA Ops:
  0.0 10.5 %copy-start.1 = (bf16[128,512]{1,0:T(8,128)(2,1)S(1)}, bf16[128,512]{1,0:T(8,128)(2,1)}, u32[]{:S(2)}) copy-start(bf16[128,512]{1,0:T(8,128)(2,1)} %param.5) | copy-start | bytes 393220
  0.8 14.4 %collective-permute-start = (bf16[1,256,128]{2,1,0:T(8,128)(2,1)S(1)}, bf16[1,256,128]{2,1,0:T(8,128)(2,1)S(1)}, u32[]{:S(2)}, u32[]{:S(2)}) collective-permute-start(bf16[1,256,128]{2,1,0:T(8,128)(2,1)S(1)} %maximum_bitcast_fusion.refs_0_), channel_id=1, source_target_pairs={{0,256},{256,0},{1,257},{257,1},{2,258},{258,2},{3,259},{259,3},{4... | collective-permute-start | bytes 196616 | tf_op jit(solution)/shard_map/ppermute | solution.py:30
  10.5 9.7 %collective-permute-start.1 = (bf16[128,512]{1,0:T(8,128)(2,1)S(1)}, bf16[128,512]{1,0:T(8,128)(2,1)S(1)}, u32[]{:S(2)}, u32[]{:S(2)}) collective-permute-start(bf16[128,512]{1,0:T(8,128)(2,1)S(1)} %copy-done.1), channel_id=1, source_target_pairs={{0,16},{16,0},{1,17},{17,1},{2,18},{18,2},{3,19},{19,3},{4,20},{20... | collective-permute-start | bytes 393224 | tf_op jit(solution)/shard_map/ppermute | solution.py:30
  13.7 6.5 %collective-permute-start.2 = (bf16[512,128]{1,0:T(8,128)(2,1)}, bf16[512,128]{1,0:T(8,128)(2,1)S(1)}, u32[]{:S(2)}, u32[]{:S(2)}) collective-permute-start(bf16[512,128]{1,0:T(8,128)(2,1)} %param.8), channel_id=1, source_target_pairs={{0,0},{4,256},{32,64},{36,320},{64,32},{68,288},{96,96},{100,352},... | collective-permute-start | bytes 393224 | tf_op jit(solution)/shard_map/ppermute | solution.py:229
  15.3 13.7 %collective-permute-start.3 = (bf16[2,256,128]{2,1,0:T(8,128)(2,1)S(1)}, bf16[2,256,128]{2,1,0:T(8,128)(2,1)S(1)}, u32[]{:S(2)}, u32[]{:S(2)}) collective-permute-start(bf16[2,256,128]{2,1,0:T(8,128)(2,1)S(1)} %shard_map.55.refs_0_), channel_id=1, source_target_pairs={{0,128},{128,0},{1,129},{129,1},{2,130},{130,2},{3,131},{131,3},{4... | collective-permute-start | bytes 393224 | tf_op jit(solution)/shard_map/ppermute | solution.py:30
  20.2 12.8 %collective-permute-start.4 = (bf16[2,128,512]{2,1,0:T(8,128)(2,1)S(1)}, bf16[2,128,512]{2,1,0:T(8,128)(2,1)S(1)}, u32[]{:S(2)}, u32[]{:S(2)}) collective-permute-start(bf16[2,128,512]{2,1,0:T(8,128)(2,1)S(1)} %pad_maximum_fusion.1.refs_0_), channel_id=1, source_target_pairs={{0,32},{32,0},{1,33},{33,1},{2,34},{34,2},{3,35},{35,3},{4,36},{36... | collective-permute-start | bytes 786440 | tf_op jit(solution)/shard_map/ppermute | solution.py:30
  33.1 7.1 %collective-permute-start.5 = (bf16[4,256,128]{2,1,0:T(8,128)(2,1)S(1)}, bf16[4,256,128]{2,1,0:T(8,128)(2,1)S(1)}, u32[]{:S(2)}, u32[]{:S(2)}) collective-permute-start(bf16[4,256,128]{2,1,0:T(8,128)(2,1)S(1)} %shard_map.56.refs_2_), channel_id=1, source_target_pairs={{0,64},{64,0},{1,65},{65,1},{2,66},{66,2},{3,67},{67,3},{4,68},{68... | collective-permute-start | bytes 786440 | tf_op jit(solution)/shard_map/ppermute | solution.py:30
  35.7 0.7 copy-start
  40.2 9.0 %collective-permute-start.6 = (bf16[8,256,128]{2,1,0:T(8,128)(2,1)S(1)}, bf16[8,256,128]{2,1,0:T(8,128)(2,1)S(1)}, u32[]{:S(2)}, u32[]{:S(2)}) collective-permute-start(bf16[8,256,128]{2,1,0:T(8,128)(2,1)S(1)} %pad_maximum_fusion), channel_id=1, source_target_pairs={{0,8},{8,0},{1,9},{9,1},{2,10},{10,2},{3,11},{11,3},{4,12},{12,4},... | collective-permute-start | bytes 1572872 | tf_op jit(solution)/shard_map/ppermute | solution.py:30
  67.5 25.7 %collective-permute-start.7 = (bf16[128,512]{1,0:T(8,128)(2,1)S(1)}, bf16[128,512]{1,0:T(8,128)(2,1)S(1)}, u32[]{:S(2)}, u32[]{:S(2)}) collective-permute-start(bf16[128,512]{1,0:T(8,128)(2,1)S(1)} %shard_map.57.own_ref), channel_id=1, source_target_pairs={{0,4},{4,0},{1,5},{5,1},{2,6},{6,2},{3,7},{7,3},{8,12},{12,8},{9,1... | collective-permute-start | bytes 393224 | tf_op jit(solution)/shard_map/ppermute | solution.py:30
  94.2 61.0 %all-to-all-start.1 = ((bf16[4,2,128,512]{3,2,1,0:T(8,128)(2,1)}), bf16[4,2,128,512]{3,2,1,0:T(8,128)(2,1)S(1)}, u32[]{:S(2)}, u32[]{:S(2)}) async-start(bf16[4,2,128,512]{3,2,1,0:T(8,128)(2,1)} %shard_map.58), calls=%async_computation.1 | async-start | bytes 2097152 | tf_op jit(solution)/shard_map/all_to_all | solution.py:272
  97.8 17.5 %collective-permute-start.8 = (bf16[1,512,128]{2,1,0:T(8,128)(2,1)S(1)}, bf16[1,512,128]{2,1,0:T(8,128)(2,1)S(1)}, u32[]{:S(2)}, u32[]{:S(2)}) collective-permute-start(bf16[1,512,128]{2,1,0:T(8,128)(2,1)S(1)} %bitcast.10), channel_id=1, source_target_pairs={{0,256},{256,0},{1,257},{257,1},{2,258},{258,2},{3,259},{259,3},{4... | collective-permute-start | bytes 393224 | tf_op jit(solution)/shard_map/ppermute | solution.py:30
  115.3 17.8 %collective-permute-start.9 = (bf16[2,512,128]{2,1,0:T(8,128)(2,1)S(1)}, bf16[2,512,128]{2,1,0:T(8,128)(2,1)S(1)}, u32[]{:S(2)}, u32[]{:S(2)}) collective-permute-start(bf16[2,512,128]{2,1,0:T(8,128)(2,1)S(1)} %constant_dynamic-update-slice_fusion), channel_id=1, source_target_pairs={{0,128},{128,0},{1,129},{129,1},{2,130},{130,2},{3,131},{131,3},{4... | collective-permute-start | bytes 786440 | tf_op jit(solution)/shard_map/ppermute | solution.py:30
  133.2 15.6 %collective-permute-start.10 = (bf16[4,512,128]{2,1,0:T(8,128)(2,1)S(1)}, bf16[4,512,128]{2,1,0:T(8,128)(2,1)S(1)}, u32[]{:S(2)}, u32[]{:S(2)}) collective-permute-start(bf16[4,512,128]{2,1,0:T(8,128)(2,1)S(1)} %constant_dynamic-update-slice_fusion.2), channel_id=1, source_target_pairs={{0,32},{32,0},{1,33},{33,1},{2,34},{34,2},{3,35},{35,3},{4,36},{36... | collective-permute-start | bytes 1572872 | tf_op jit(solution)/shard_map/ppermute | solution.py:30
  148.9 6.3 %collective-permute-start.11 = (bf16[8,512,128]{2,1,0:T(8,128)(2,1)S(1)}, bf16[8,512,128]{2,1,0:T(8,128)(2,1)S(1)}, u32[]{:S(2)}, u32[]{:S(2)}) collective-permute-start(bf16[8,512,128]{2,1,0:T(8,128)(2,1)S(1)} %constant_dynamic-update-slice_fusion.4.near_ref), channel_id=1, source_target_pairs={{0,8},{8,0},{1,9},{9,1},{2,10},{10,2},{3,11},{11,3},{4,12},{12,4},... | collective-permute-start | bytes 3145736 | tf_op jit(solution)/shard_map/ppermute | solution.py:30
